TPU v7x, 256 devices: a whole 4x4x8 slice. The times are simulated.
256 devices in a mesh: grp: 8 (over z), tp: 32 (over y, x, core).
Axes of the slice: x: 4, y: 4, z: 8, core: 2. Of those that a mesh axis runs over, the one named last changes fastest.
Arguments:
- hidden_in: bfloat16 [512, 4096], P('grp'), may hold values from -6 to 6
- norm_gain: float32 [4096], replicated, may hold values from 0.25 to 1.75
- head_weight: bfloat16 [4096, 128256], P('grp', 'tp'), may hold values from -1 to 1
- ffn_act: bfloat16 [512, 14336], P('grp', 'tp'), may hold values from -6 to 6
- labels: int32 [512], P('grp'), may hold values from 0 to 128255
- lengths: int32 [64], P('grp'), may hold values from 1 to 8
- proj_hidden: bfloat16 [4096, 64], replicated, may hold values from -0.09375 to 0.09375
- proj_vocab: bfloat16 [128256, 64], P('tp'), may hold values from -6 to 6
- proj_ffn: bfloat16 [14336, 64], P('tp'), may hold values from -0.046875 to 0.046875
- proj_down: bfloat16 [4096, 64], replicated, may hold values from -6 to 6
- store: bfloat16 [65536, 8192], P('grp', 'tp'), may hold values from -0.0625 to 0.0625
Outputs:
- scores: float32 [64, 65536], P('tp', 'grp')
All inputs are finite; a program needn't handle non-finite values.
Results may differ from a plain program's by a relative error of at most 0.012.
Values may be sent and summed in bfloat16 or wider, within the bound.
No kernel may reach another device: no remote copies, remote signals or barrier semaphores. Data moves between devices by JAX's collectives and lax.ppermute only.
A program may use at most 64 MiB of HBM per device.

v0:
```python
import jax
import jax.numpy as jnp
from jax import lax
from jax.experimental import pallas as pl
from jax.experimental.pallas import tpu as pltpu
from jax.sharding import PartitionSpec as P


epsilon = 1e-05
f32 = jnp.float32
bf16 = jnp.bfloat16
by_last = (((1,), (1,)), ((), ()))

early_shifts = (1, 7)
late_shifts = (4, 3, 5, 2, 6)


small = pltpu.CompilerParams(vmem_limit_bytes=16 * 1024 * 1024)


def vmem(count):
    return [pl.BlockSpec(memory_space=pltpu.VMEM)] * count


def traded(value, axis, groups=None):
    return lax.all_to_all(
        value, axis, split_axis=0, concat_axis=0, tiled=True, axis_index_groups=groups
    )


def norm_kernel(info, gain_ref, down_ref, hidden_proj_ref, *refs, width):
    pieces, (lhs_ref, side_ref, own_ref) = refs[:-3], refs[-3:]
    xs, tokens, lane = pieces[0].shape
    rank = down_ref.shape[0]
    mine = side_ref.shape[0]
    rows = 64
    half = len(pieces) // 2
    places = []
    for n in range(len(pieces)):
        y = lax.rem(info[0] + half - n % half, half)
        core = info[1] if n < half else 1 - info[1]
        for x in range(xs):
            places.append((n, x, pl.multiple_of(((y * xs + x) * 2 + core) * lane, lane)))

    @pl.loop(0, tokens // rows)
    def _(i):
        at = pl.ds(pl.multiple_of(i * rows, rows), rows)
        squares = jnp.zeros((rows, lane), f32)
        for n, x, _ in places:
            value = pieces[n][x, at, :].astype(f32)
            squares += value * value
        mean = jnp.sum(squares, axis=1, keepdims=True) / width
        inverse = jnp.broadcast_to(lax.rsqrt(mean + epsilon), (rows, lane))
        for n, x, place in places:
            value = pieces[n][x, at, :].astype(f32)
            lhs_ref[at, pl.ds(place, lane)] = (gain_ref[:, pl.ds(place, lane)] * (value * inverse)).astype(bf16)

    gained = gain_ref[...] * down_ref[...].astype(f32)
    high = gained.astype(bf16)
    lhs_ref[tokens : tokens + rank] = high
    lhs_ref[tokens + rank :] = (gained - high.astype(f32)).astype(bf16)
    own = pl.ds(pl.multiple_of(info[2], mine), mine)
    squares = jnp.zeros((mine, lane), f32)
    for n, x, place in places:
        value = pieces[n][x, own, :]
        own_ref[:, pl.ds(place, lane)] = value
        squares += value.astype(f32) * value.astype(f32)
    inverse = lax.rsqrt(jnp.sum(squares, axis=1, keepdims=True) / width + epsilon)
    unit_down = inverse * lax.dot_general(own_ref[...], down_ref[...], by_last, preferred_element_type=f32)
    hidden_side = lax.dot_general(
        lhs_ref[own, :], hidden_proj_ref[...], by_last, preferred_element_type=f32
    )
    side_ref[:, :rank] = unit_down
    side_ref[:, rank : 2 * rank] = hidden_side
    side_ref[:, 2 * rank :] = jnp.broadcast_to(inverse, (mine, side_ref.shape[1] - 2 * rank))


def soft_kernel(
    info, sums_ref, lhs_ref, first_ref, last_ref, vocab_ref, label_ref, ffn_ref, keep_ref, send_ref, out_ref
):
    tokens, rank = label_ref.shape[0], vocab_ref.shape[0]
    columns, depth = last_ref.shape

    def finished(first, count):
        total = sums_ref[first : first + count]
        for n, ref in enumerate((first_ref, last_ref)):
            at = pl.ds(pl.multiple_of(info[4 + n], depth), depth)
            total += lax.dot_general(
                lhs_ref[first : first + count, at], ref[...], by_last, preferred_element_type=f32
            )
        return total

    fold = finished(tokens, 2 * rank)
    fold = fold[:rank] + fold[rank:]
    fold_high = fold.astype(bf16)
    fold_low = (fold - fold_high.astype(f32)).astype(bf16)
    right = jnp.concatenate([vocab_ref[...], fold_high, fold_low, fold_low], axis=0)
    keep = lax.broadcasted_iota(jnp.int32, (1, 2 * rank), 1) >= rank
    spot = lax.broadcasted_iota(jnp.int32, (1, columns), 1)
    counted = spot >= info[1]
    count = 128
    lane = lax.broadcasted_iota(jnp.int32, (count, 2 * rank), 1)
    for first in range(0, tokens, count):
        rows = slice(first, first + count)
        logits = finished(first, count)
        peak = jnp.max(jnp.where(counted, logits, -jnp.inf), axis=1, keepdims=True)
        grown = jnp.where(counted, jnp.exp(jnp.minimum(logits - peak, 0.0)), 0.0)
        total = jnp.sum(grown, axis=1, keepdims=True)
        rounded = grown.astype(bf16)
        hit = counted & (label_ref[rows] == spot + info[0])
        dot_all = jnp.sum(rounded.astype(f32) * logits, axis=1, keepdims=True)
        dot_hit = jnp.sum(jnp.where(hit, logits, 0.0), axis=1, keepdims=True)
        soft = lax.dot_general(rounded, right, by_last, preferred_element_type=f32)
        mark = lax.dot_general(hit.astype(f32).astype(bf16), right, by_last, preferred_element_type=f32)
        out_ref[rows, : 2 * rank] = soft[:, : 2 * rank] + jnp.where(keep, soft[:, 2 * rank :], 0.0)
        out_ref[rows, 2 * rank : 4 * rank] = mark[:, : 2 * rank] + jnp.where(keep, mark[:, 2 * rank :], 0.0)
        stats = jnp.where(lane == 0, peak, jnp.where(lane == 1, total, jnp.where(lane == 2, dot_all, dot_hit)))
        out_ref[rows, 4 * rank :] = jnp.where(lane < 4, stats, 0.0)
    here = ffn_ref.shape[0]
    own = pl.ds(pl.multiple_of(info[2], here), here)
    lane = lax.broadcasted_iota(jnp.int32, (here, 2 * rank), 1)
    out_ref[own, 4 * rank :] = jnp.where(lane < rank, out_ref[own, 4 * rank :], ffn_ref[...])
    mine = keep_ref.shape[1]
    for core in range(2):

        @pl.when(info[3] == core)
        def _():
            for pair in range(keep_ref.shape[0]):
                first, second = 2 * pair + core, 2 * pair + 1 - core
                keep_ref[pair] = out_ref[mine * first : mine * (first + 1)]
                send_ref[pair] = out_ref[mine * second : mine * (second + 1)]


def merged(x):
    stats = x[:, :, 256:]
    peaks = stats[:, :, 0:1]
    peak = jnp.max(peaks, axis=0)
    weight = jnp.exp(peaks - peak)
    soft = jnp.sum(x[:, :, :128] * weight, axis=0)
    mark = jnp.sum(x[:, :, 128:256], axis=0)
    lane = lax.broadcasted_iota(jnp.int32, stats.shape[1:], 1)
    scaled = jnp.sum(stats * weight, axis=0)
    plain = jnp.sum(stats, axis=0)
    kept = jnp.where(lane == 0, peak, jnp.where(lane < 3, scaled, plain))
    return soft, mark, kept


def pair_merge_kernel(keep_ref, came_ref, out_ref):
    for n in range(out_ref.shape[0]):
        soft, mark, kept = merged(jnp.stack([keep_ref[n], came_ref[n]]))
        out_ref[n, :, :128] = soft
        out_ref[n, :, 128:256] = mark
        out_ref[n, :, 256:] = kept


def first_merge_kernel(x_ref, out_ref):
    soft, mark, kept = merged(x_ref[...])
    for copy in range(out_ref.shape[0]):
        out_ref[copy, :, :128] = soft
        out_ref[copy, :, 128:256] = mark
        out_ref[copy, :, 256:] = kept


def last_merge_kernel(x_ref, side_ref, valid_ref, out_ref, *, width):
    soft, mark, kept = merged(x_ref[...])
    total, dot_all, dot_hit = kept[:, 1:2], kept[:, 2:3], kept[:, 3:4]
    both = soft / total - mark
    label_dot = dot_all / total - dot_hit
    rank = both.shape[1] // 2
    inverse, valid = side_ref[:, 2 * rank : 2 * rank + 1], valid_ref[...] > 0
    down_side = inverse * (both[:, rank:] - (label_dot / width) * side_ref[:, :rank])
    head_side = jnp.where(valid, both[:, :rank], 0.0)
    down_side = jnp.where(valid, down_side, 0.0)
    first = jnp.concatenate([head_side, side_ref[:, rank : 2 * rank]], axis=1).astype(bf16)
    second = jnp.concatenate([down_side, kept[:, rank:]], axis=1).astype(bf16)
    half = out_ref.shape[0] // 2
    for copy in range(half):
        out_ref[copy] = first
        out_ref[half + copy] = second


def query_kernel(info, sides_ref, out_ref, *, span):
    rank = sides_ref.shape[1] // 2
    sides = sides_ref[...]
    features = out_ref.shape[1]
    column = lax.broadcasted_iota(jnp.int32, (2 * rank, features), 0)
    wanted = rank + info[0] + lax.broadcasted_iota(jnp.int32, (2 * rank, features), 1) // rank
    chosen = (column == wanted).astype(f32).astype(bf16)
    left = jnp.dot(sides, chosen, preferred_element_type=f32)
    right = sides[:, :rank].astype(f32)
    product = left * jnp.concatenate([right] * (features // rank), axis=1)
    query = jnp.sum(product.reshape(-1, span, features), axis=1).astype(bf16)
    count = query.shape[0]
    spot = lax.broadcasted_iota(jnp.int32, (count, count), 0)
    source = lax.broadcasted_iota(jnp.int32, (count, count), 1)
    half, each = count // 2, info[1]
    far = spot // half
    near = spot - far * half
    core = info[2] + far - 2 * info[2] * far
    wanted = (2 * (near // each) + core) * each + lax.rem(near, each)
    order = (source == wanted).astype(f32).astype(bf16)
    out_ref[...] = jnp.dot(order, query, preferred_element_type=f32).astype(bf16)


def per_device(
    hidden_in,
    norm_gain,
    head_weight,
    ffn_act,
    labels,
    lengths,
    proj_hidden,
    proj_vocab,
    proj_ffn,
    proj_down,
    store,
):
    here, width = hidden_in.shape
    rows_owned, vocab_owned = head_weight.shape
    rank = proj_hidden.shape[1]
    groups, lanes = lax.axis_size("grp"), lax.axis_size("tp")
    tokens = here * groups
    seq_span = here // lengths.shape[0]
    z, j = lax.axis_index("grp"), lax.axis_index("tp")

    block = -(-vocab_owned // (8 * groups)) * 8
    turned = head_weight.T

    def first_of(group):
        return jnp.minimum(block * group, vocab_owned - block)

    start = first_of(z)
    skipped = block * z - start

    part = width // lanes
    digits = [labels % 128, labels // 128 % 128, labels // 16384, lengths]
    digits = jnp.concatenate(digits).astype(bf16)
    digits = jnp.pad(digits, (0, 16 * part - digits.shape[0])).reshape(16, part)
    share = lax.dynamic_slice_in_dim(hidden_in, j * part, part, 1)
    share = jnp.concatenate([share, digits], axis=0)

    came = {}

    def head_moves(source, shifts):
        for s in shifts:
            cut = lax.dynamic_slice_in_dim(source, first_of((z + s) % groups), block, 0)
            came[s] = lax.ppermute(cut, "grp", [(i, (i + s) % groups) for i in range(groups)])

    head_moves(turned, early_shifts)
    later, share = lax.optimization_barrier((turned, share))
    head_moves(later, late_shifts)
    came[0] = lax.dynamic_slice_in_dim(later, start, block, 0)
    column = jnp.zeros((groups, here, part), bf16)
    ints = jnp.zeros((groups, 2, part), bf16)
    for s in range(groups):
        got = lax.ppermute(share, "grp", [(i, (i + s) % groups) for i in range(groups)]) if s else share
        column = lax.dynamic_update_index_in_dim(column, got[:here], (z - s) % groups, 0)
        ints = lax.dynamic_update_index_in_dim(ints, got[here : here + 2], (z - s) % groups, 0)
    column = column.reshape(tokens, part)
    y_at, x_at, core_at = j // 8, (j // 2) % 4, j % 2

    def moved(value, move):
        return lax.ppermute(value, "tp", [(i, move(i)) for i in range(lanes)])

    row = jnp.zeros((4, tokens, part), bf16)
    for s in range(4):
        came_x = moved(column, lambda i: i // 8 * 8 + (i % 8 + 2 * s) % 8) if s else column
        row = lax.dynamic_update_index_in_dim(row, came_x, (x_at - s) % 4, 0)
    pieces = [moved(row, lambda i: (i + 8 * s) % 32) if s else row for s in range(4)]
    pieces += [moved(piece, lambda i: i ^ 1) for piece in pieces]

    mine = tokens // lanes
    of_one_core = [[2 * i + core for i in range(lanes // 2)] for core in range(2)]
    in_smem = pl.BlockSpec(memory_space=pltpu.SMEM)
    in_vmem = pl.BlockSpec(memory_space=pltpu.VMEM)
    lhs, side = pl.pallas_call(
        lambda *refs: norm_kernel(*refs, width=width),
        out_shape=(
            jax.ShapeDtypeStruct((tokens + 2 * rank, width), bf16),
            jax.ShapeDtypeStruct((mine, 4 * rank), f32),
        ),
        in_specs=[in_smem, *vmem(3 + len(pieces))],
        out_specs=(in_vmem, in_vmem),
        scratch_shapes=[pltpu.VMEM((mine, width), bf16)],
        compiler_params=small,
    )(
        jnp.stack([y_at, core_at, j * mine]).astype(jnp.int32),
        norm_gain[None, :],
        proj_down.T,
        proj_hidden.T,
        *pieces,
    )

    ints = ints.astype(jnp.int32).reshape(groups, 2 * part)
    all_labels = ints[:, :here] + 128 * ints[:, here : 2 * here] + 16384 * ints[:, 2 * here : 3 * here]
    all_labels = all_labels.reshape(tokens, 1)
    all_lengths = ints[:, 3 * here : 3 * here + lengths.shape[0]].reshape(-1)
    spot = j * mine + lax.broadcasted_iota(jnp.int32, (mine, 1), 0)
    own_length = lax.dynamic_slice_in_dim(all_lengths, j * (mine // seq_span), mine // seq_span, 0)
    valid = (spot % seq_span < jnp.repeat(own_length, seq_span)[:, None]).astype(jnp.int32)
    ffn = jnp.dot(ffn_act, proj_ffn, preferred_element_type=f32)
    ffn = jnp.concatenate([jnp.zeros_like(ffn), ffn], axis=1)
    vocab_turned = lax.dynamic_slice_in_dim(proj_vocab, start, block, 0).T

    sums = None
    shifts = (0, *early_shifts, *late_shifts)
    for s in shifts[:-2]:
        depth = lax.dynamic_slice_in_dim(lhs, ((z - s) % groups) * rows_owned, rows_owned, 1)
        term = lax.dot_general(depth, came[s], by_last, preferred_element_type=f32)
        sums = term if sums is None else sums + term
    last = shifts[-2:]
    info = [j * vocab_owned + start, skipped, z * here, core_at]
    info = jnp.stack([*info, *(((z - s) % groups) * rows_owned for s in last)]).astype(jnp.int32)
    by_core = (lanes // 2, mine, 6 * rank)
    keep, send = pl.pallas_call(
        soft_kernel,
        out_shape=(jax.ShapeDtypeStruct(by_core, f32), jax.ShapeDtypeStruct(by_core, f32)),
        in_specs=[in_smem, *vmem(7)],
        out_specs=(in_vmem, in_vmem),
        scratch_shapes=[pltpu.VMEM((tokens, 6 * rank), f32)],
        compiler_params=small,
    )(info, sums, lhs, came[last[0]], came[last[1]], vocab_turned, all_labels, ffn)
    packed = pl.pallas_call(
        pair_merge_kernel,
        out_shape=jax.ShapeDtypeStruct(by_core, f32),
        in_specs=vmem(2),
        out_specs=in_vmem,
        compiler_params=small,
    )(keep, moved(send, lambda i: i ^ 1))
    packed = traded(packed, "tp", of_one_core)
    packed = pl.pallas_call(
        first_merge_kernel,
        out_shape=jax.ShapeDtypeStruct((groups, mine, 6 * rank), f32),
        in_specs=vmem(1),
        out_specs=in_vmem,
        compiler_params=small,
    )(packed)
    packed = traded(packed, "grp")
    sides = pl.pallas_call(
        lambda *refs: last_merge_kernel(*refs, width=width),
        out_shape=jax.ShapeDtypeStruct((lanes, mine, 2 * rank), bf16),
        in_specs=vmem(3),
        out_specs=in_vmem,
        compiler_params=small,
    )(packed, side, valid)
    sides = traded(sides, "tp").reshape(tokens, 2 * rank)

    stored, features = store.shape
    queries = tokens // seq_span
    per = features // rank
    query = pl.pallas_call(
        lambda *refs: query_kernel(*refs, span=seq_span),
        out_shape=jax.ShapeDtypeStruct((queries, features), bf16),
        in_specs=[in_smem, *vmem(1)],
        out_specs=in_vmem,
        compiler_params=small,
    )(jnp.stack([j % (lanes // 2) * per, queries // lanes, core_at]).astype(jnp.int32), sides)
    partial = lax.dot_general(query, store, by_last, preferred_element_type=f32)
    half = queries // 2
    other = moved(partial[half:].astype(bf16), lambda i: i ^ 1)
    partial = (partial[:half] + other.astype(f32)).astype(bf16)
    partial = traded(partial.reshape(lanes // 2, queries // lanes, stored), "tp", of_one_core)
    return jnp.sum(partial.astype(f32), axis=0)


def solution(mesh):
    return jax.shard_map(
        per_device,
        mesh=mesh,
        in_specs=(
            P("grp", None),
            P(),
            P("grp", "tp"),
            P("grp", "tp"),
            P("grp"),
            P("grp"),
            P(),
            P("tp", None),
            P("tp", None),
            P(),
            P("grp", "tp"),
        ),
        out_specs=P("tp", "grp"),
        check_vma=False,
    )
```

profile of v0, /device:TPU:1, one launch (start us, length us, event | category | flops | bytes accessed | tf_op | source)
XLA Modules:
  0.0 230.7 jit_solution(5562358334275312315)
XLA Ops:
  2.2 2.5 %collective-permute-start = (bf16[80,128]{1,0:T(8,128)(2,1)S(1)}, bf16[80,128]{1,0:T(8,128)(2,1)S(1)}, u32[]{:S(2)}, u32[]{:S(2)}) collective-permute-start(bf16[80,128]{1,0:T(8,128)(2,1)S(1)} %pad_maximum_fusion), channel_id=1, source_target_pairs={{0,32},{32,64},{64,96},{96,128},{128,160},{160,192},{192,224},{224... | collective-permute-start | bytes 61448 | tf_op jit(solution)/shard_map/ppermute | solution.py:256
  4.7 3.0 %collective-permute-start.1 = (bf16[80,128]{1,0:T(8,128)(2,1)S(1)}, bf16[80,128]{1,0:T(8,128)(2,1)S(1)}, u32[]{:S(2)}, u32[]{:S(2)}) collective-permute-start(bf16[80,128]{1,0:T(8,128)(2,1)S(1)} %pad_maximum_fusion), channel_id=1, source_target_pairs={{0,64},{32,96},{64,128},{96,160},{128,192},{160,224},{192,0},{224,... | collective-permute-start | bytes 61448 | tf_op jit(solution)/shard_map/ppermute | solution.py:256
  7.7 3.8 %collective-permute-start.2 = (bf16[80,128]{1,0:T(8,128)(2,1)S(1)}, bf16[80,128]{1,0:T(8,128)(2,1)S(1)}, u32[]{:S(2)}, u32[]{:S(2)}) collective-permute-start(bf16[80,128]{1,0:T(8,128)(2,1)S(1)} %pad_maximum_fusion), channel_id=1, source_target_pairs={{0,96},{32,128},{64,160},{96,192},{128,224},{160,0},{192,32},{224,... | collective-permute-start | bytes 61448 | tf_op jit(solution)/shard_map/ppermute | solution.py:256
  11.9 4.5 %collective-permute-start.4 = (bf16[80,128]{1,0:T(8,128)(2,1)S(1)}, bf16[80,128]{1,0:T(8,128)(2,1)S(1)}, u32[]{:S(2)}, u32[]{:S(2)}) collective-permute-start(bf16[80,128]{1,0:T(8,128)(2,1)S(1)} %pad_maximum_fusion), channel_id=1, source_target_pairs={{0,160},{32,192},{64,224},{96,0},{128,32},{160,64},{192,96},{224,1... | collective-permute-start | bytes 61448 | tf_op jit(solution)/shard_map/ppermute | solution.py:256
  16.4 2.4 %dynamic-slice_bitcast_fusion = (bf16[504,512]{1,0:T(8,128)(2,1)}, bf16[504,512]{1,0:T(8,128)(2,1)}) fusion(bf16[512,4008]{0,1:T(8,128)(2,1)} %param.13, s32[]{:T(128)S(6)} %select_n.299, s32[]{:T(128)S(6)} %select_n.296), kind=kLoop, calls=%fused_computation.19 | loop fusion | bytes 2064392 | tf_op jit(solution)/shard_map/dynamic_slice | solution.py:246
  19.2 3.4 %constant_dynamic-slice_fusion = (bf16[504,512]{1,0:T(8,128)(2,1)}, bf16[504,512]{1,0:T(8,128)(2,1)}, bf16[504,512]{1,0:T(8,128)(2,1)}, bf16[504,512]{1,0:T(8,128)(2,1)}, bf16[504,512]{1,0:T(8,128)(2,1)}) fusion(bf16[4008,512]{1,0:T(8,128)(2,1)} %bitcast.96, s32[]{:T(128)S(6)} %select_n.312, s32[]{:T(128)S(6)} %select_n.310, s32[]{:T(128)S(6)} %select_n.308, ...), kind=kLoop, calls=%fused_computation.48 | loop fusion | bytes 5160980 | tf_op jit(solution)/shard_map/dynamic_slice | solution.py:246
  23.2 2.4 %collective-permute-start.5 = (bf16[80,128]{1,0:T(8,128)(2,1)S(1)}, bf16[80,128]{1,0:T(8,128)(2,1)S(1)}, u32[]{:S(2)}, u32[]{:S(2)}) collective-permute-start(bf16[80,128]{1,0:T(8,128)(2,1)S(1)} %pad_maximum_fusion), channel_id=1, source_target_pairs={{0,192},{32,224},{64,0},{96,32},{128,64},{160,96},{192,128},{224,1... | collective-permute-start | bytes 61448 | tf_op jit(solution)/shard_map/ppermute | solution.py:256
  29.5 2.5 %collective-permute-start.8 = (bf16[512,128]{1,0:T(8,128)(2,1)S(1)}, bf16[512,128]{1,0:T(8,128)(2,1)S(1)}, u32[]{:S(2)}, u32[]{:S(2)}) collective-permute-start(bf16[512,128]{1,0:T(8,128)(2,1)S(1)} %bitcast.99), channel_id=1, source_target_pairs={{0,4},{1,5},{2,6},{3,7},{4,0},{5,1},{6,2},{7,3},{8,12},{9,13},{10,... | collective-permute-start | bytes 393224 | tf_op jit(solution)/shard_map/ppermute | solution.py:263
  33.4 2.4 %collective-permute-done.8 = bf16[512,128]{1,0:T(8,128)(2,1)S(1)} collective-permute-done((bf16[512,128]{1,0:T(8,128)(2,1)S(1)}, bf16[512,128]{1,0:T(8,128)(2,1)S(1)}, u32[]{:S(2)}, u32[]{:S(2)}) %collective-permute-start.8) | collective-permute-done | bytes 131104 | tf_op jit(solution)/shard_map/ppermute | solution.py:263
  37.6 2.6 %collective-permute-start.11 = (bf16[4,512,128]{2,1,0:T(8,128)(2,1)S(1)}, bf16[4,512,128]{2,1,0:T(8,128)(2,1)S(1)}, u32[]{:S(2)}, u32[]{:S(2)}) collective-permute-start(bf16[4,512,128]{2,1,0:T(8,128)(2,1)S(1)} %bitcast_dynamic-update-slice_fusion.refs_4_), channel_id=1, source_target_pairs={{0,16},{1,17},{2,18},{3,19},{4,20},{5,21},{6,22},{7,23},{8,24},{9,... | collective-permute-start | bytes 1572872 | tf_op jit(solution)/shard_map/ppermute | solution.py:263
  42.7 5.7 %collective-permute-start.13 = (bf16[4,512,128]{2,1,0:T(8,128)(2,1)S(1)}, bf16[4,512,128]{2,1,0:T(8,128)(2,1)}, u32[]{:S(2)}, u32[]{:S(2)}) collective-permute-start(bf16[4,512,128]{2,1,0:T(8,128)(2,1)S(1)} %bitcast_dynamic-update-slice_fusion.refs_4_), channel_id=1, source_target_pairs={{0,1},{1,0},{2,3},{3,2},{4,5},{5,4},{6,7},{7,6},{8,9},{9,8},{10,11... | collective-permute-start | bytes 1572872 | tf_op jit(solution)/shard_map/ppermute | solution.py:263
  48.3 7.7 %collective-permute-start.14 = (bf16[4,512,128]{2,1,0:T(8,128)(2,1)S(1)}, bf16[4,512,128]{2,1,0:T(8,128)(2,1)}, u32[]{:S(2)}, u32[]{:S(2)}) collective-permute-start(bf16[4,512,128]{2,1,0:T(8,128)(2,1)S(1)} %collective-permute-done.10.refs_5_), channel_id=1, source_target_pairs={{0,1},{1,0},{2,3},{3,2},{4,5},{5,4},{6,7},{7,6},{8,9},{9,8},{10,11... | collective-permute-start | bytes 1572872 | tf_op jit(solution)/shard_map/ppermute | solution.py:263
  56.0 2.6 %collective-permute-done.11.refs_6_ = bf16[4,512,128]{2,1,0:T(8,128)(2,1)S(1)} collective-permute-done((bf16[4,512,128]{2,1,0:T(8,128)(2,1)S(1)}, bf16[4,512,128]{2,1,0:T(8,128)(2,1)S(1)}, u32[]{:S(2)}, u32[]{:S(2)}) %collective-permute-start.11) | collective-permute-done | bytes 524320 | tf_op jit(solution)/shard_map/ppermute | solution.py:263
  58.6 5.7 %collective-permute-start.15 = (bf16[4,512,128]{2,1,0:T(8,128)(2,1)S(1)}, bf16[4,512,128]{2,1,0:T(8,128)(2,1)}, u32[]{:S(2)}, u32[]{:S(2)}) collective-permute-start(bf16[4,512,128]{2,1,0:T(8,128)(2,1)S(1)} %collective-permute-done.11.refs_6_), channel_id=1, source_target_pairs={{0,1},{1,0},{2,3},{3,2},{4,5},{5,4},{6,7},{7,6},{8,9},{9,8},{10,11... | collective-permute-start | bytes 1572872 | tf_op jit(solution)/shard_map/ppermute | solution.py:263
  65.9 4.0 %collective-permute-start.20 = (bf16[504,512]{1,0:T(8,128)(2,1)}, bf16[504,512]{1,0:T(8,128)(2,1)S(1)}, u32[]{:S(2)}, u32[]{:S(2)}) collective-permute-start(bf16[504,512]{1,0:T(8,128)(2,1)} %get-tuple-element.20), channel_id=1, source_target_pairs={{0,96},{32,128},{64,160},{96,192},{128,224},{160,0},{192,32},{224,... | collective-permute-start | bytes 1548296 | tf_op jit(solution)/shard_map/ppermute | solution.py:247
  71.8 5.2 %shard_map.109 = (bf16[640,4096]{1,0:T(8,128)(2,1)S(1)}, f32[16,256]{1,0:T(8,128)S(1)}) custom-call(s32[3]{0:T(128)S(1)} %pad_add_fusion.1.refs_0_, f32[1,4096]{1,0:T(1,128)S(1)} %bitcast.95, bf16[64,4096]{1,0:T(8,128)(2,1)S(1)} %bitcast.93, bf16[64,4096]{1,0:T(8,128)(2,1)S(1)} %bitcast.94, ...), custom_call_target="tpu_custom_call" | custom-call | tf_op jit(solution)/shard_map/pallas_call | solution.py:276
  77.0 2.1 collective-permute-start.22
  80.8 2.8 %convolution_add_fusion.1 = f32[640,504]{0,1:T(8,128)} fusion(f32[640,504]{0,1:T(8,128)S(1)} %fusion.11, bf16[640,4096]{1,0:T(8,128)(2,1)S(1)} %get-tuple-element.12.lhs_ref, s32[]{:T(128)S(6)} %select_n.292, bf16[4008,512]{1,0:T(8,128)(2,1)} %bitcast.97, s32[]{:T(128)S(6)} %select_n.293), kind=kOutput, calls=%fused_computation.4 | convolution fusion | flops 330624000 | bytes 3751944 | tf_op jit(solution)/shard_map/dot_general | solution.py:309
  83.5 5.7 %collective-permute-done.19 = bf16[504,512]{1,0:T(8,128)(2,1)S(1)} collective-permute-done((bf16[504,512]{1,0:T(8,128)(2,1)}, bf16[504,512]{1,0:T(8,128)(2,1)S(1)}, u32[]{:S(2)}, u32[]{:S(2)}) %collective-permute-start.19) | collective-permute-done | bytes 516128 | tf_op jit(solution)/shard_map/ppermute | solution.py:247
  89.3 7.5 %collective-permute-start.23 = (bf16[504,512]{1,0:T(8,128)(2,1)S(1)}, bf16[504,512]{1,0:T(8,128)(2,1)S(1)}, u32[]{:S(2)}, u32[]{:S(2)}) collective-permute-start(bf16[504,512]{1,0:T(8,128)(2,1)S(1)} %copy-done.5), channel_id=1, source_target_pairs={{0,192},{32,224},{64,0},{96,32},{128,64},{160,96},{192,128},{224,1... | collective-permute-start | bytes 1548296 | tf_op jit(solution)/shard_map/ppermute | solution.py:247
  98.4 28.5 %collective-permute-done.20 = bf16[504,512]{1,0:T(8,128)(2,1)S(1)} collective-permute-done((bf16[504,512]{1,0:T(8,128)(2,1)}, bf16[504,512]{1,0:T(8,128)(2,1)S(1)}, u32[]{:S(2)}, u32[]{:S(2)}) %collective-permute-start.20) | collective-permute-done | bytes 516128 | tf_op jit(solution)/shard_map/ppermute | solution.py:247
  130.3 2.9 %copy.43 = f32[640,504]{1,0:T(8,128)} copy(f32[640,504]{0,1:T(8,128)} %convolution_add_fusion.1) | data formatting | bytes 2580480 | tf_op jit(solution)/shard_map/add | solution.py:310
  134.9 3.5 %fusion.2.sums_ref = f32[640,504]{1,0:T(8,128)S(1)} fusion(f32[640,504]{1,0:T(8,128)} %fusion.4, f32[640,504]{1,0:T(8,128)} %fusion.6, f32[640,504]{1,0:T(8,128)} %fusion.8, f32[640,504]{1,0:T(8,128)} %copy.43, bf16[504,512]{1,0:T(8,128)(2,1)} %collective-permute-done.18, bf16[640,4096]{1,0:T(8,128)(2,1)} %copy-done.1, s32[]{:T(128)S(6)} %select_n.297), kind=kOutput, calls=%fused_computation.3 | convolution fusion | flops 331591680 | bytes 7704580 | tf_op jit(solution)/shard_map/dot_general | solution.py:309
  138.3 21.4 %collective-permute-done.23.last_ref = bf16[504,512]{1,0:T(8,128)(2,1)S(1)} collective-permute-done((bf16[504,512]{1,0:T(8,128)(2,1)S(1)}, bf16[504,512]{1,0:T(8,128)(2,1)S(1)}, u32[]{:S(2)}, u32[]{:S(2)}) %collective-permute-start.23) | collective-permute-done | bytes 516128 | tf_op jit(solution)/shard_map/ppermute | solution.py:247
  159.8 3.7 %shard_map.110 = (f32[16,16,384]{2,1,0:T(8,128)S(1)}, f32[16,16,384]{2,1,0:T(8,128)S(1)}) custom-call(s32[6]{0:T(128)S(1)} %stack.46.info, f32[640,504]{1,0:T(8,128)S(1)} %fusion.2.sums_ref, bf16[640,4096]{1,0:T(8,128)(2,1)S(1)} %bitcast.91, bf16[504,512]{1,0:T(8,128)(2,1)S(1)} %collective-permute-done.22.first_ref, ...), custom_call_target="tpu_custom_call" | custom-call | tf_op jit(solution)/shard_map/pallas_call | solution.py:315
  165.6 15.2 %all_to_all.20.x_ref = f32[16,16,384]{2,1,0:T(8,128)S(1)} all-to-all(f32[16,16,384]{2,1,0:T(8,128)S(1)} %shard_map.111), channel_id=1, replica_groups={{0,2,4,6,8,10,12,14,16,18,20,22,24,26,28,30},{1,3,5,7,9,11,13,15,17,19,..., dimensions={0} | all-to-all | bytes 786432 | tf_op jit(solution)/shard_map/all_to_all | solution.py:26
  181.5 3.4 %all-to-all-start.1 = ((f32[8,16,384]{2,1,0:T(8,128)}), f32[8,16,384]{2,1,0:T(8,128)S(1)}, u32[]{:S(2)}, u32[]{:S(2)}) async-start(f32[8,16,384]{2,1,0:T(8,128)} %shard_map.112), calls=%async_computation.1 | async-start | bytes 393216 | tf_op jit(solution)/shard_map/all_to_all | solution.py:26
  185.5 7.9 %all-to-all-done.1.refs_0_ = f32[8,16,384]{2,1,0:T(8,128)S(1)} async-done(((f32[8,16,384]{2,1,0:T(8,128)}), f32[8,16,384]{2,1,0:T(8,128)S(1)}, u32[]{:S(2)}, u32[]{:S(2)}) %all-to-all-start.1) | async-done | bytes 196640 | tf_op jit(solution)/shard_map/all_to_all | solution.py:26
  194.4 6.5 %all-to-all-start.2 = ((bf16[32,16,128]{2,1,0:T(8,128)(2,1)}), bf16[32,16,128]{2,1,0:T(8,128)(2,1)S(1)}, u32[]{:S(2)}, u32[]{:S(2)}) async-start(bf16[32,16,128]{2,1,0:T(8,128)(2,1)} %shard_map.113), calls=%async_computation.2 | async-start | bytes 262144 | tf_op jit(solution)/shard_map/all_to_all | solution.py:26
  200.9 7.6 %all-to-all-done.2 = bf16[32,16,128]{2,1,0:T(8,128)(2,1)S(1)} async-done(((bf16[32,16,128]{2,1,0:T(8,128)(2,1)}), bf16[32,16,128]{2,1,0:T(8,128)(2,1)S(1)}, u32[]{:S(2)}, u32[]{:S(2)}) %all-to-all-start.2) | async-done | bytes 131104 | tf_op jit(solution)/shard_map/all_to_all | solution.py:26
  209.8 3.6 %fusion.45 = f32[64,8192]{1,0:T(8,128)S(1)} fusion(bf16[64,256]{1,0:T(8,128)(2,1)S(1)} %shard_map.114, bf16[8192,256]{1,0:T(8,128)(2,1)} %param.21), kind=kOutput, calls=%fused_computation.101 | convolution fusion | flops 268435456 | bytes 6324224 | tf_op jit(solution)/shard_map/dot_general | solution.py:358
  216.0 13.6 %all_to_all.21 = bf16[16,2,8192]{2,1,0:T(2,128)(2,1)S(1)} all-to-all(bf16[16,2,8192]{2,1,0:T(2,128)(2,1)S(1)} %reshape.95), channel_id=1, replica_groups={{0,2,4,6,8,10,12,14,16,18,20,22,24,26,28,30},{1,3,5,7,9,11,13,15,17,19,..., dimensions={0} | all-to-all | bytes 1048576 | tf_op jit(solution)/shard_map/all_to_all | solution.py:26
  (132 shorter events, 33.8 us)
Async XLA Ops:
  2.2 21.0 %collective-permute-start = (bf16[80,128]{1,0:T(8,128)(2,1)S(1)}, bf16[80,128]{1,0:T(8,128)(2,1)S(1)}, u32[]{:S(2)}, u32[]{:S(2)}) collective-permute-start(bf16[80,128]{1,0:T(8,128)(2,1)S(1)} %pad_maximum_fusion), channel_id=1, source_target_pairs={{0,32},{32,64},{64,96},{96,128},{128,160},{160,192},{192,224},{224... | collective-permute-start | bytes 61448 | tf_op jit(solution)/shard_map/ppermute | solution.py:256
  4.7 21.0 %collective-permute-start.1 = (bf16[80,128]{1,0:T(8,128)(2,1)S(1)}, bf16[80,128]{1,0:T(8,128)(2,1)S(1)}, u32[]{:S(2)}, u32[]{:S(2)}) collective-permute-start(bf16[80,128]{1,0:T(8,128)(2,1)S(1)} %pad_maximum_fusion), channel_id=1, source_target_pairs={{0,64},{32,96},{64,128},{96,160},{128,192},{160,224},{192,0},{224,... | collective-permute-start | bytes 61448 | tf_op jit(solution)/shard_map/ppermute | solution.py:256
  7.7 18.7 %collective-permute-start.2 = (bf16[80,128]{1,0:T(8,128)(2,1)S(1)}, bf16[80,128]{1,0:T(8,128)(2,1)S(1)}, u32[]{:S(2)}, u32[]{:S(2)}) collective-permute-start(bf16[80,128]{1,0:T(8,128)(2,1)S(1)} %pad_maximum_fusion), channel_id=1, source_target_pairs={{0,96},{32,128},{64,160},{96,192},{128,224},{160,0},{192,32},{224,... | collective-permute-start | bytes 61448 | tf_op jit(solution)/shard_map/ppermute | solution.py:256
  11.4 15.7 %collective-permute-start.3 = (bf16[80,128]{1,0:T(8,128)(2,1)S(1)}, bf16[80,128]{1,0:T(8,128)(2,1)S(1)}, u32[]{:S(2)}, u32[]{:S(2)}) collective-permute-start(bf16[80,128]{1,0:T(8,128)(2,1)S(1)} %pad_maximum_fusion), channel_id=1, source_target_pairs={{0,128},{32,160},{64,192},{96,224},{128,0},{160,32},{192,64},{224,... | collective-permute-start | bytes 61448 | tf_op jit(solution)/shard_map/ppermute | solution.py:256
  11.9 15.3 %collective-permute-start.4 = (bf16[80,128]{1,0:T(8,128)(2,1)S(1)}, bf16[80,128]{1,0:T(8,128)(2,1)S(1)}, u32[]{:S(2)}, u32[]{:S(2)}) collective-permute-start(bf16[80,128]{1,0:T(8,128)(2,1)S(1)} %pad_maximum_fusion), channel_id=1, source_target_pairs={{0,160},{32,192},{64,224},{96,0},{128,32},{160,64},{192,96},{224,1... | collective-permute-start | bytes 61448 | tf_op jit(solution)/shard_map/ppermute | solution.py:256
  22.6 49.2 %copy-start.2 = (bf16[4096,64]{0,1:T(8,128)(2,1)S(1)}, bf16[4096,64]{0,1:T(8,128)(2,1)}, u32[]{:S(2)}) copy-start(bf16[4096,64]{0,1:T(8,128)(2,1)} %param.20) | copy-start | bytes 1572868
  22.6 49.2 %copy-start.3 = (bf16[4096,64]{0,1:T(8,128)(2,1)S(1)}, bf16[4096,64]{0,1:T(8,128)(2,1)}, u32[]{:S(2)}) copy-start(bf16[4096,64]{0,1:T(8,128)(2,1)} %param.17) | copy-start | bytes 1572868
  22.6 49.2 %copy-start.4 = (f32[4096]{0:T(1024)S(1)}, f32[4096]{0:T(1024)}, u32[]{:S(2)}) copy-start(f32[4096]{0:T(1024)} %param.12) | copy-start | bytes 49156
  23.2 4.0 %collective-permute-start.5 = (bf16[80,128]{1,0:T(8,128)(2,1)S(1)}, bf16[80,128]{1,0:T(8,128)(2,1)S(1)}, u32[]{:S(2)}, u32[]{:S(2)}) collective-permute-start(bf16[80,128]{1,0:T(8,128)(2,1)S(1)} %pad_maximum_fusion), channel_id=1, source_target_pairs={{0,192},{32,224},{64,0},{96,32},{128,64},{160,96},{192,128},{224,1... | collective-permute-start | bytes 61448 | tf_op jit(solution)/shard_map/ppermute | solution.py:256
  25.7 2.6 %collective-permute-start.6 = (bf16[80,128]{1,0:T(8,128)(2,1)S(1)}, bf16[80,128]{1,0:T(8,128)(2,1)S(1)}, u32[]{:S(2)}, u32[]{:S(2)}) collective-permute-start(bf16[80,128]{1,0:T(8,128)(2,1)S(1)} %pad_maximum_fusion), channel_id=1, source_target_pairs={{0,224},{32,0},{64,32},{96,64},{128,96},{160,128},{192,160},{224,1... | collective-permute-start | bytes 61448 | tf_op jit(solution)/shard_map/ppermute | solution.py:256
  26.4 50.6 %collective-permute-start.17 = (bf16[504,512]{1,0:T(8,128)(2,1)}, bf16[504,512]{1,0:T(8,128)(2,1)}, u32[]{:S(2)}, u32[]{:S(2)}) collective-permute-start(bf16[504,512]{1,0:T(8,128)(2,1)} %get-tuple-element.23), channel_id=1, source_target_pairs={{0,32},{32,64},{64,96},{96,128},{128,160},{160,192},{192,224},{224... | collective-permute-start | bytes 1548296 | tf_op jit(solution)/shard_map/ppermute | solution.py:247
  28.3 5.0 %collective-permute-start.7 = (bf16[512,128]{1,0:T(8,128)(2,1)S(1)}, bf16[512,128]{1,0:T(8,128)(2,1)S(1)}, u32[]{:S(2)}, u32[]{:S(2)}) collective-permute-start(bf16[512,128]{1,0:T(8,128)(2,1)S(1)} %bitcast.98), channel_id=1, source_target_pairs={{0,2},{1,3},{2,4},{3,5},{4,6},{5,7},{6,0},{7,1},{8,10},{9,11},{10,... | collective-permute-start | bytes 393224 | tf_op jit(solution)/shard_map/ppermute | solution.py:263
  29.5 6.2 %collective-permute-start.8 = (bf16[512,128]{1,0:T(8,128)(2,1)S(1)}, bf16[512,128]{1,0:T(8,128)(2,1)S(1)}, u32[]{:S(2)}, u32[]{:S(2)}) collective-permute-start(bf16[512,128]{1,0:T(8,128)(2,1)S(1)} %bitcast.99), channel_id=1, source_target_pairs={{0,4},{1,5},{2,6},{3,7},{4,0},{5,1},{6,2},{7,3},{8,12},{9,13},{10,... | collective-permute-start | bytes 393224 | tf_op jit(solution)/shard_map/ppermute | solution.py:263
  32.0 4.2 %collective-permute-start.9 = (bf16[512,128]{1,0:T(8,128)(2,1)S(1)}, bf16[512,128]{1,0:T(8,128)(2,1)S(1)}, u32[]{:S(2)}, u32[]{:S(2)}) collective-permute-start(bf16[512,128]{1,0:T(8,128)(2,1)S(1)} %bitcast.100), channel_id=1, source_target_pairs={{0,6},{1,7},{2,0},{3,1},{4,2},{5,3},{6,4},{7,5},{8,14},{9,15},{10,... | collective-permute-start | bytes 393224 | tf_op jit(solution)/shard_map/ppermute | solution.py:263
  36.2 12.1 %collective-permute-start.10 = (bf16[4,512,128]{2,1,0:T(8,128)(2,1)S(1)}, bf16[4,512,128]{2,1,0:T(8,128)(2,1)S(1)}, u32[]{:S(2)}, u32[]{:S(2)}) collective-permute-start(bf16[4,512,128]{2,1,0:T(8,128)(2,1)S(1)} %bitcast_dynamic-update-slice_fusion.refs_4_), channel_id=1, source_target_pairs={{0,8},{1,9},{2,10},{3,11},{4,12},{5,13},{6,14},{7,15},{8,16},{9,17... | collective-permute-start | bytes 1572872 | tf_op jit(solution)/shard_map/ppermute | solution.py:263
  37.6 21.1 %collective-permute-start.11 = (bf16[4,512,128]{2,1,0:T(8,128)(2,1)S(1)}, bf16[4,512,128]{2,1,0:T(8,128)(2,1)S(1)}, u32[]{:S(2)}, u32[]{:S(2)}) collective-permute-start(bf16[4,512,128]{2,1,0:T(8,128)(2,1)S(1)} %bitcast_dynamic-update-slice_fusion.refs_4_), channel_id=1, source_target_pairs={{0,16},{1,17},{2,18},{3,19},{4,20},{5,21},{6,22},{7,23},{8,24},{9,... | collective-permute-start | bytes 1572872 | tf_op jit(solution)/shard_map/ppermute | solution.py:263
  40.2 24.1 %collective-permute-start.12 = (bf16[4,512,128]{2,1,0:T(8,128)(2,1)S(1)}, bf16[4,512,128]{2,1,0:T(8,128)(2,1)}, u32[]{:S(2)}, u32[]{:S(2)}) collective-permute-start(bf16[4,512,128]{2,1,0:T(8,128)(2,1)S(1)} %bitcast_dynamic-update-slice_fusion.refs_4_), channel_id=1, source_target_pairs={{0,24},{1,25},{2,26},{3,27},{4,28},{5,29},{6,30},{7,31},{8,0},{9,1... | collective-permute-start | bytes 1572872 | tf_op jit(solution)/shard_map/ppermute | solution.py:263
  42.7 22.3 %collective-permute-start.13 = (bf16[4,512,128]{2,1,0:T(8,128)(2,1)S(1)}, bf16[4,512,128]{2,1,0:T(8,128)(2,1)}, u32[]{:S(2)}, u32[]{:S(2)}) collective-permute-start(bf16[4,512,128]{2,1,0:T(8,128)(2,1)S(1)} %bitcast_dynamic-update-slice_fusion.refs_4_), channel_id=1, source_target_pairs={{0,1},{1,0},{2,3},{3,2},{4,5},{5,4},{6,7},{7,6},{8,9},{9,8},{10,11... | collective-permute-start | bytes 1572872 | tf_op jit(solution)/shard_map/ppermute | solution.py:263
  48.3 17.6 %collective-permute-start.14 = (bf16[4,512,128]{2,1,0:T(8,128)(2,1)S(1)}, bf16[4,512,128]{2,1,0:T(8,128)(2,1)}, u32[]{:S(2)}, u32[]{:S(2)}) collective-permute-start(bf16[4,512,128]{2,1,0:T(8,128)(2,1)S(1)} %collective-permute-done.10.refs_5_), channel_id=1, source_target_pairs={{0,1},{1,0},{2,3},{3,2},{4,5},{5,4},{6,7},{7,6},{8,9},{9,8},{10,11... | collective-permute-start | bytes 1572872 | tf_op jit(solution)/shard_map/ppermute | solution.py:263
  58.6 11.3 %collective-permute-start.15 = (bf16[4,512,128]{2,1,0:T(8,128)(2,1)S(1)}, bf16[4,512,128]{2,1,0:T(8,128)(2,1)}, u32[]{:S(2)}, u32[]{:S(2)}) collective-permute-start(bf16[4,512,128]{2,1,0:T(8,128)(2,1)S(1)} %collective-permute-done.11.refs_6_), channel_id=1, source_target_pairs={{0,1},{1,0},{2,3},{3,2},{4,5},{5,4},{6,7},{7,6},{8,9},{9,8},{10,11... | collective-permute-start | bytes 1572872 | tf_op jit(solution)/shard_map/ppermute | solution.py:263
  64.3 6.1 %collective-permute-start.16 = (bf16[4,512,128]{2,1,0:T(8,128)(2,1)}, bf16[4,512,128]{2,1,0:T(8,128)(2,1)}, u32[]{:S(2)}, u32[]{:S(2)}) collective-permute-start(bf16[4,512,128]{2,1,0:T(8,128)(2,1)} %collective-permute-done.12.refs_7_), channel_id=1, source_target_pairs={{0,1},{1,0},{2,3},{3,2},{4,5},{5,4},{6,7},{7,6},{8,9},{9,8},{10,11... | collective-permute-start | bytes 1572872 | tf_op jit(solution)/shard_map/ppermute | solution.py:263
  64.9 24.4 %collective-permute-start.19 = (bf16[504,512]{1,0:T(8,128)(2,1)}, bf16[504,512]{1,0:T(8,128)(2,1)S(1)}, u32[]{:S(2)}, u32[]{:S(2)}) collective-permute-start(bf16[504,512]{1,0:T(8,128)(2,1)} %get-tuple-element.21), channel_id=1, source_target_pairs={{0,128},{32,160},{64,192},{96,224},{128,0},{160,32},{192,64},{224,... | collective-permute-start | bytes 1548296 | tf_op jit(solution)/shard_map/ppermute | solution.py:247
  65.9 61.0 %collective-permute-start.20 = (bf16[504,512]{1,0:T(8,128)(2,1)}, bf16[504,512]{1,0:T(8,128)(2,1)S(1)}, u32[]{:S(2)}, u32[]{:S(2)}) collective-permute-start(bf16[504,512]{1,0:T(8,128)(2,1)} %get-tuple-element.20), channel_id=1, source_target_pairs={{0,96},{32,128},{64,160},{96,192},{128,224},{160,0},{192,32},{224,... | collective-permute-start | bytes 1548296 | tf_op jit(solution)/shard_map/ppermute | solution.py:247
  69.9 58.7 %collective-permute-start.21 = (bf16[504,512]{1,0:T(8,128)(2,1)}, bf16[504,512]{1,0:T(8,128)(2,1)S(1)}, u32[]{:S(2)}, u32[]{:S(2)}) collective-permute-start(bf16[504,512]{1,0:T(8,128)(2,1)} %get-tuple-element.19), channel_id=1, source_target_pairs={{0,160},{32,192},{64,224},{96,0},{128,32},{160,64},{192,96},{224,1... | collective-permute-start | bytes 1548296 | tf_op jit(solution)/shard_map/ppermute | solution.py:247
  70.4 64.4 %collective-permute-start.18 = (bf16[504,512]{1,0:T(8,128)(2,1)}, bf16[504,512]{1,0:T(8,128)(2,1)}, u32[]{:S(2)}, u32[]{:S(2)}) collective-permute-start(bf16[504,512]{1,0:T(8,128)(2,1)} %get-tuple-element.22), channel_id=1, source_target_pairs={{0,224},{32,0},{64,32},{96,64},{128,96},{160,128},{192,160},{224,1... | collective-permute-start | bytes 1548296 | tf_op jit(solution)/shard_map/ppermute | solution.py:247
  77.0 51.6 %copy-start.1 = (bf16[640,4096]{1,0:T(8,128)(2,1)}, bf16[640,4096]{1,0:T(8,128)(2,1)S(1)}, u32[]{:S(2)}) copy-start(bf16[640,4096]{1,0:T(8,128)(2,1)S(1)} %get-tuple-element.12.lhs_ref) | copy-start | bytes 15728644
  77.0 61.3 %collective-permute-start.22 = (bf16[504,512]{1,0:T(8,128)(2,1)}, bf16[504,512]{1,0:T(8,128)(2,1)S(1)}, u32[]{:S(2)}, u32[]{:S(2)}) collective-permute-start(bf16[504,512]{1,0:T(8,128)(2,1)} %get-tuple-element.18), channel_id=1, source_target_pairs={{0,64},{32,96},{64,128},{96,160},{128,192},{160,224},{192,0},{224,... | collective-permute-start | bytes 1548296 | tf_op jit(solution)/shard_map/ppermute | solution.py:247
  89.3 70.5 %collective-permute-start.23 = (bf16[504,512]{1,0:T(8,128)(2,1)S(1)}, bf16[504,512]{1,0:T(8,128)(2,1)S(1)}, u32[]{:S(2)}, u32[]{:S(2)}) collective-permute-start(bf16[504,512]{1,0:T(8,128)(2,1)S(1)} %copy-done.5), channel_id=1, source_target_pairs={{0,192},{32,224},{64,0},{96,32},{128,64},{160,96},{192,128},{224,1... | collective-permute-start | bytes 1548296 | tf_op jit(solution)/shard_map/ppermute | solution.py:247
  163.4 1.9 collective-permute-start.24
  181.5 11.8 %all-to-all-start.1 = ((f32[8,16,384]{2,1,0:T(8,128)}), f32[8,16,384]{2,1,0:T(8,128)S(1)}, u32[]{:S(2)}, u32[]{:S(2)}) async-start(f32[8,16,384]{2,1,0:T(8,128)} %shard_map.112), calls=%async_computation.1 | async-start | bytes 393216 | tf_op jit(solution)/shard_map/all_to_all | solution.py:26
  194.4 14.2 %all-to-all-start.2 = ((bf16[32,16,128]{2,1,0:T(8,128)(2,1)}), bf16[32,16,128]{2,1,0:T(8,128)(2,1)S(1)}, u32[]{:S(2)}, u32[]{:S(2)}) async-start(bf16[32,16,128]{2,1,0:T(8,128)(2,1)} %shard_map.113), calls=%async_computation.2 | async-start | bytes 262144 | tf_op jit(solution)/shard_map/all_to_all | solution.py:26
  213.5 2.0 collective-permute-start.25
  (8 other events, 126.2 us)
where the time goes:
time: 231 us
  waiting for transfers between devices  82.4 us (36%)
  starting transfers between devices  74.3 us (32%)
  blocking collectives  28.8 us (12%)
  matrix products  16.6 us (7%)
  local copies, waits for them, and re-layouts  12.7 us (5%)
  Pallas kernels  12.2 us (5%)
  other arithmetic  2.93 us (1%)
    ppermute x7, waiting for transfers between devices, head_moves(): lax.ppermute(cut, 'grp', [(i, (i + s) % groups) for i in range(groups)])  57.4 us
    ppermute x12, starting transfers between devices, moved(): return lax.ppermute(value, 'tp', [(i, move(i)) for i in range(lanes)])  30 us
    all_to_all x2, blocking collectives, traded(): lax.all_to_all(value, axis, split_axis=0, concat_axis=0, tiled=True, axis...  28.8 us
    ppermute x7, starting transfers between devices, per_device(): lax.ppermute(share, 'grp', [(i, (i + s) % groups) for i in range(groups)])  17.3 us
    ppermute x7, starting transfers between devices, head_moves(): lax.ppermute(cut, 'grp', [(i, (i + s) % groups) for i in range(groups)])  17.2 us
    all_to_all x2, waiting for transfers between devices, traded(): lax.all_to_all(value, axis, split_axis=0, concat_axis=0, tiled=True, axis...  15.5 us
    dot_general x6, matrix products, per_device(): term = lax.dot_general(depth, came[s], by_last, preferred_element_type=f32)  12.8 us
    all_to_all x2, starting transfers between devices, traded(): lax.all_to_all(value, axis, split_axis=0, concat_axis=0, tiled=True, axis...  9.87 us
  transfers between devices with their start and end apart: 28, of which 13 were waited for; matrix products, arithmetic and copies ran while one was open for 11% of the time, Pallas kernels for 2%

commit v1 on v0

--- a/solution.py
+++ b/solution.py
@@ -250,12 +250,8 @@
     later, share = lax.optimization_barrier((turned, share))
     head_moves(later, late_shifts)
     came[0] = lax.dynamic_slice_in_dim(later, start, block, 0)
-    column = jnp.zeros((groups, here, part), bf16)
-    ints = jnp.zeros((groups, 2, part), bf16)
-    for s in range(groups):
-        got = lax.ppermute(share, "grp", [(i, (i + s) % groups) for i in range(groups)]) if s else share
-        column = lax.dynamic_update_index_in_dim(column, got[:here], (z - s) % groups, 0)
-        ints = lax.dynamic_update_index_in_dim(ints, got[here : here + 2], (z - s) % groups, 0)
+    shares = traded(jnp.broadcast_to(share, (groups, *share.shape)), "grp")
+    column, ints = shares[:, :here], shares[:, here : here + 2]
     column = column.reshape(tokens, part)
     y_at, x_at, core_at = j // 8, (j // 2) % 4, j % 2
 

time: 231 us -> 226 us (0.978)
  starting transfers between devices: 74.3 us -> 65.1 us
  waiting for transfers between devices: 82.4 us -> 88.3 us
    ppermute x7 -> x0, starting transfers between devices: 17.3 us -> none  [per_device(): lax.ppermute(share, 'grp', [(i, (i + s) % groups) for i in range(groups)])]
    all_to_all x2 -> x3, starting transfers between devices: 9.87 us -> 18.8 us  [traded(): lax.all_to_all(value, axis, split_axis=0, concat_axis=0, tiled=True, axis...]
    all_to_all x2 -> x3, waiting for transfers between devices: 15.5 us -> 24 us  [traded(): lax.all_to_all(value, axis, split_axis=0, concat_axis=0, tiled=True, axis...]
    ppermute x12, starting transfers between devices: 30 us -> 26.2 us  [moved(): return lax.ppermute(value, 'tp', [(i, move(i)) for i in range(lanes)])]
    ppermute x7, starting transfers between devices: 17.2 us -> 20.1 us  [head_moves(): lax.ppermute(cut, 'grp', [(i, (i + s) % groups) for i in range(groups)])]
    ppermute x7, waiting for transfers between devices: 57.4 us -> 54.9 us  [head_moves(): lax.ppermute(cut, 'grp', [(i, (i + s) % groups) for i in range(groups)])]
  transfers between devices with their start and end apart: 28 -> 22, of which waited for: 13 -> 12; matrix products, arithmetic and copies ran while one was open for 11% -> 10% of each run, Pallas kernels for 2% -> 2%
where the time goes in v1:
time: 226 us
  waiting for transfers between devices  88.3 us (39%)
  starting transfers between devices  65.1 us (29%)
  blocking collectives  28.8 us (13%)
  matrix products  16.5 us (7%)
  Pallas kernels  12.2 us (5%)
  local copies, waits for them, and re-layouts  11.8 us (5%)
  other arithmetic  2.92 us (1%)
    ppermute x7, waiting for transfers between devices, head_moves(): lax.ppermute(cut, 'grp', [(i, (i + s) % groups) for i in range(groups)])  54.9 us
    all_to_all x2, blocking collectives, traded(): lax.all_to_all(value, axis, split_axis=0, concat_axis=0, tiled=True, axis...  28.8 us
    ppermute x12, starting transfers between devices, moved(): return lax.ppermute(value, 'tp', [(i, move(i)) for i in range(lanes)])  26.2 us
    all_to_all x3, waiting for transfers between devices, traded(): lax.all_to_all(value, axis, split_axis=0, concat_axis=0, tiled=True, axis...  24 us
    ppermute x7, starting transfers between devices, head_moves(): lax.ppermute(cut, 'grp', [(i, (i + s) % groups) for i in range(groups)])  20.1 us
    all_to_all x3, starting transfers between devices, traded(): lax.all_to_all(value, axis, split_axis=0, concat_axis=0, tiled=True, axis...  18.8 us
    dot_general x6, matrix products, per_device(): term = lax.dot_general(depth, came[s], by_last, preferred_element_type=f32)  12.8 us
    ppermute x12, waiting for transfers between devices, moved(): return lax.ppermute(value, 'tp', [(i, move(i)) for i in range(lanes)])  9.3 us
  transfers between devices with their start and end apart: 22, of which 12 were waited for; matrix products, arithmetic and copies ran while one was open for 10% of the time, Pallas kernels for 2%

profile of v1, /device:TPU:1, one launch (start us, length us, event | category | flops | bytes accessed | tf_op | source)
XLA Modules:
  0.0 225.8 jit_solution(5496108920343410810)
XLA Ops:
  2.9 9.0 %all-to-all-start = ((bf16[8,80,128]{2,1,0:T(8,128)(2,1)}), bf16[8,80,128]{2,1,0:T(8,128)(2,1)S(1)}, u32[]{:S(2)}, u32[]{:S(2)}) async-start(bf16[8,80,128]{2,1,0:T(8,128)(2,1)} %broadcast_in_dim.28), calls=%async_computation | async-start | bytes 327680 | tf_op jit(solution)/shard_map/all_to_all | solution.py:26
  11.9 8.2 %all-to-all-done = bf16[8,80,128]{2,1,0:T(8,128)(2,1)S(1)} async-done(((bf16[8,80,128]{2,1,0:T(8,128)(2,1)}), bf16[8,80,128]{2,1,0:T(8,128)(2,1)S(1)}, u32[]{:S(2)}, u32[]{:S(2)}) %all-to-all-start) | async-done | bytes 163872 | tf_op jit(solution)/shard_map/all_to_all | solution.py:26
  21.4 2.4 %dynamic-slice_bitcast_fusion = (bf16[504,512]{1,0:T(8,128)(2,1)}, bf16[504,512]{1,0:T(8,128)(2,1)}) fusion(bf16[512,4008]{0,1:T(8,128)(2,1)} %param.13, s32[]{:T(128)S(6)} %select_n.222, s32[]{:T(128)S(6)} %select_n.218), kind=kLoop, calls=%fused_computation.19 | loop fusion | bytes 2064392 | tf_op jit(solution)/shard_map/dynamic_slice | solution.py:246
  24.4 2.5 %collective-permute-start.1 = (bf16[512,128]{1,0:T(8,128)(2,1)S(1)}, bf16[512,128]{1,0:T(8,128)(2,1)S(1)}, u32[]{:S(2)}, u32[]{:S(2)}) collective-permute-start(bf16[512,128]{1,0:T(8,128)(2,1)S(1)} %bitcast.55), channel_id=1, source_target_pairs={{0,4},{1,5},{2,6},{3,7},{4,0},{5,1},{6,2},{7,3},{8,12},{9,13},{10,... | collective-permute-start | bytes 393224 | tf_op jit(solution)/shard_map/ppermute | solution.py:259
  28.2 2.4 %collective-permute-done.1 = bf16[512,128]{1,0:T(8,128)(2,1)S(1)} collective-permute-done((bf16[512,128]{1,0:T(8,128)(2,1)S(1)}, bf16[512,128]{1,0:T(8,128)(2,1)S(1)}, u32[]{:S(2)}, u32[]{:S(2)}) %collective-permute-start.1) | collective-permute-done | bytes 131104 | tf_op jit(solution)/shard_map/ppermute | solution.py:259
  32.1 2.6 %collective-permute-start.4 = (bf16[4,512,128]{2,1,0:T(8,128)(2,1)S(1)}, bf16[4,512,128]{2,1,0:T(8,128)(2,1)S(1)}, u32[]{:S(2)}, u32[]{:S(2)}) collective-permute-start(bf16[4,512,128]{2,1,0:T(8,128)(2,1)S(1)} %bitcast_dynamic-update-slice_fusion.refs_4_), channel_id=1, source_target_pairs={{0,16},{1,17},{2,18},{3,19},{4,20},{5,21},{6,22},{7,23},{8,24},{9,... | collective-permute-start | bytes 1572872 | tf_op jit(solution)/shard_map/ppermute | solution.py:259
  36.3 3.6 %constant_dynamic-slice_fusion = (bf16[504,512]{1,0:T(8,128)(2,1)}, bf16[504,512]{1,0:T(8,128)(2,1)}, bf16[504,512]{1,0:T(8,128)(2,1)}, bf16[504,512]{1,0:T(8,128)(2,1)}, bf16[504,512]{1,0:T(8,128)(2,1)}) fusion(bf16[4008,512]{1,0:T(8,128)(2,1)} %bitcast.52, s32[]{:T(128)S(6)} %select_n.238, s32[]{:T(128)S(6)} %select_n.236, s32[]{:T(128)S(6)} %select_n.234, ...), kind=kLoop, calls=%fused_computation.35 | loop fusion | bytes 5160980 | tf_op jit(solution)/shard_map/dynamic_slice | solution.py:246
  39.8 5.0 %collective-permute-start.6 = (bf16[4,512,128]{2,1,0:T(8,128)(2,1)S(1)}, bf16[4,512,128]{2,1,0:T(8,128)(2,1)}, u32[]{:S(2)}, u32[]{:S(2)}) collective-permute-start(bf16[4,512,128]{2,1,0:T(8,128)(2,1)S(1)} %bitcast_dynamic-update-slice_fusion.refs_4_), channel_id=1, source_target_pairs={{0,1},{1,0},{2,3},{3,2},{4,5},{5,4},{6,7},{7,6},{8,9},{9,8},{10,11... | collective-permute-start | bytes 1572872 | tf_op jit(solution)/shard_map/ppermute | solution.py:259
  44.9 5.0 %collective-permute-start.7 = (bf16[4,512,128]{2,1,0:T(8,128)(2,1)S(1)}, bf16[4,512,128]{2,1,0:T(8,128)(2,1)}, u32[]{:S(2)}, u32[]{:S(2)}) collective-permute-start(bf16[4,512,128]{2,1,0:T(8,128)(2,1)S(1)} %collective-permute-done.3.refs_5_), channel_id=1, source_target_pairs={{0,1},{1,0},{2,3},{3,2},{4,5},{5,4},{6,7},{7,6},{8,9},{9,8},{10,11... | collective-permute-start | bytes 1572872 | tf_op jit(solution)/shard_map/ppermute | solution.py:259
  49.9 3.9 %collective-permute-done.4.refs_6_ = bf16[4,512,128]{2,1,0:T(8,128)(2,1)S(1)} collective-permute-done((bf16[4,512,128]{2,1,0:T(8,128)(2,1)S(1)}, bf16[4,512,128]{2,1,0:T(8,128)(2,1)S(1)}, u32[]{:S(2)}, u32[]{:S(2)}) %collective-permute-start.4) | collective-permute-done | bytes 524320 | tf_op jit(solution)/shard_map/ppermute | solution.py:259
  53.8 5.1 %collective-permute-start.8 = (bf16[4,512,128]{2,1,0:T(8,128)(2,1)S(1)}, bf16[4,512,128]{2,1,0:T(8,128)(2,1)}, u32[]{:S(2)}, u32[]{:S(2)}) collective-permute-start(bf16[4,512,128]{2,1,0:T(8,128)(2,1)S(1)} %collective-permute-done.4.refs_6_), channel_id=1, source_target_pairs={{0,1},{1,0},{2,3},{3,2},{4,5},{5,4},{6,7},{7,6},{8,9},{9,8},{10,11... | collective-permute-start | bytes 1572872 | tf_op jit(solution)/shard_map/ppermute | solution.py:259
  60.6 4.2 %collective-permute-start.13 = (bf16[504,512]{1,0:T(8,128)(2,1)}, bf16[504,512]{1,0:T(8,128)(2,1)S(1)}, u32[]{:S(2)}, u32[]{:S(2)}) collective-permute-start(bf16[504,512]{1,0:T(8,128)(2,1)} %get-tuple-element.20), channel_id=1, source_target_pairs={{0,96},{32,128},{64,160},{96,192},{128,224},{160,0},{192,32},{224,... | collective-permute-start | bytes 1548296 | tf_op jit(solution)/shard_map/ppermute | solution.py:247
  66.2 5.2 %shard_map.109 = (bf16[640,4096]{1,0:T(8,128)(2,1)S(1)}, f32[16,256]{1,0:T(8,128)S(1)}) custom-call(s32[3]{0:T(128)S(1)} %pad_add_fusion.1.refs_0_, f32[1,4096]{1,0:T(1,128)S(1)} %bitcast.51, bf16[64,4096]{1,0:T(8,128)(2,1)S(1)} %bitcast.49, bf16[64,4096]{1,0:T(8,128)(2,1)S(1)} %bitcast.50, ...), custom_call_target="tpu_custom_call" | custom-call | tf_op jit(solution)/shard_map/pallas_call | solution.py:272
  71.4 3.5 %collective-permute-start.15 = (bf16[504,512]{1,0:T(8,128)(2,1)}, bf16[504,512]{1,0:T(8,128)(2,1)S(1)}, u32[]{:S(2)}, u32[]{:S(2)}) collective-permute-start(bf16[504,512]{1,0:T(8,128)(2,1)} %get-tuple-element.18), channel_id=1, source_target_pairs={{0,64},{32,96},{64,128},{96,160},{128,192},{160,224},{192,0},{224,... | collective-permute-start | bytes 1548296 | tf_op jit(solution)/shard_map/ppermute | solution.py:247
  74.9 1.6 fusion.11
  76.5 2.8 %convolution_add_fusion.1 = f32[640,504]{0,1:T(8,128)} fusion(f32[640,504]{0,1:T(8,128)S(1)} %fusion.11, bf16[640,4096]{1,0:T(8,128)(2,1)S(1)} %get-tuple-element.12.lhs_ref, s32[]{:T(128)S(6)} %select_n.213, bf16[4008,512]{1,0:T(8,128)(2,1)} %bitcast.53, s32[]{:T(128)S(6)} %select_n.214), kind=kOutput, calls=%fused_computation.4 | convolution fusion | flops 330624000 | bytes 3751944 | tf_op jit(solution)/shard_map/dot_general | solution.py:305
  79.3 3.1 %collective-permute-done.12 = bf16[504,512]{1,0:T(8,128)(2,1)S(1)} collective-permute-done((bf16[504,512]{1,0:T(8,128)(2,1)}, bf16[504,512]{1,0:T(8,128)(2,1)S(1)}, u32[]{:S(2)}, u32[]{:S(2)}) %collective-permute-start.12) | collective-permute-done | bytes 516128 | tf_op jit(solution)/shard_map/ppermute | solution.py:247
  82.4 9.2 %collective-permute-start.16 = (bf16[504,512]{1,0:T(8,128)(2,1)S(1)}, bf16[504,512]{1,0:T(8,128)(2,1)S(1)}, u32[]{:S(2)}, u32[]{:S(2)}) collective-permute-start(bf16[504,512]{1,0:T(8,128)(2,1)S(1)} %copy-done.5), channel_id=1, source_target_pairs={{0,192},{32,224},{64,0},{96,32},{128,64},{160,96},{192,128},{224,1... | collective-permute-start | bytes 1548296 | tf_op jit(solution)/shard_map/ppermute | solution.py:247
  93.2 27.9 %collective-permute-done.13 = bf16[504,512]{1,0:T(8,128)(2,1)S(1)} collective-permute-done((bf16[504,512]{1,0:T(8,128)(2,1)}, bf16[504,512]{1,0:T(8,128)(2,1)S(1)}, u32[]{:S(2)}, u32[]{:S(2)}) %collective-permute-start.13) | collective-permute-done | bytes 516128 | tf_op jit(solution)/shard_map/ppermute | solution.py:247
  122.7 1.7 fusion.4
  124.4 2.9 %copy.27 = f32[640,504]{1,0:T(8,128)} copy(f32[640,504]{0,1:T(8,128)} %convolution_add_fusion.1) | data formatting | bytes 2580480 | tf_op jit(solution)/shard_map/add | solution.py:306
  127.3 3.7 %collective-permute-done.11 = bf16[504,512]{1,0:T(8,128)(2,1)} collective-permute-done((bf16[504,512]{1,0:T(8,128)(2,1)}, bf16[504,512]{1,0:T(8,128)(2,1)}, u32[]{:S(2)}, u32[]{:S(2)}) %collective-permute-start.11) | collective-permute-done | bytes 516128 | tf_op jit(solution)/shard_map/ppermute | solution.py:247
  131.0 3.5 %fusion.2.sums_ref = f32[640,504]{1,0:T(8,128)S(1)} fusion(f32[640,504]{1,0:T(8,128)} %fusion.4, f32[640,504]{1,0:T(8,128)} %fusion.6, f32[640,504]{1,0:T(8,128)} %fusion.8, f32[640,504]{1,0:T(8,128)} %copy.27, bf16[504,512]{1,0:T(8,128)(2,1)} %collective-permute-done.11, bf16[640,4096]{1,0:T(8,128)(2,1)} %copy-done.1, s32[]{:T(128)S(6)} %select_n.220), kind=kOutput, calls=%fused_computation.3 | convolution fusion | flops 331591680 | bytes 7704580 | tf_op jit(solution)/shard_map/dot_general | solution.py:305
  134.5 20.3 %collective-permute-done.16.last_ref = bf16[504,512]{1,0:T(8,128)(2,1)S(1)} collective-permute-done((bf16[504,512]{1,0:T(8,128)(2,1)S(1)}, bf16[504,512]{1,0:T(8,128)(2,1)S(1)}, u32[]{:S(2)}, u32[]{:S(2)}) %collective-permute-start.16) | collective-permute-done | bytes 516128 | tf_op jit(solution)/shard_map/ppermute | solution.py:247
  154.7 3.7 %shard_map.110 = (f32[16,16,384]{2,1,0:T(8,128)S(1)}, f32[16,16,384]{2,1,0:T(8,128)S(1)}) custom-call(s32[6]{0:T(128)S(1)} %stack.46.info, f32[640,504]{1,0:T(8,128)S(1)} %fusion.2.sums_ref, bf16[640,4096]{1,0:T(8,128)(2,1)S(1)} %bitcast.47, bf16[504,512]{1,0:T(8,128)(2,1)S(1)} %collective-permute-done.15.first_ref, ...), custom_call_target="tpu_custom_call" | custom-call | tf_op jit(solution)/shard_map/pallas_call | solution.py:311
  160.5 15.1 %all_to_all.25.x_ref = f32[16,16,384]{2,1,0:T(8,128)S(1)} all-to-all(f32[16,16,384]{2,1,0:T(8,128)S(1)} %shard_map.111), channel_id=1, replica_groups={{0,2,4,6,8,10,12,14,16,18,20,22,24,26,28,30},{1,3,5,7,9,11,13,15,17,19,..., dimensions={0} | all-to-all | bytes 786432 | tf_op jit(solution)/shard_map/all_to_all | solution.py:26
  176.4 3.5 %all-to-all-start.2 = ((f32[8,16,384]{2,1,0:T(8,128)}), f32[8,16,384]{2,1,0:T(8,128)S(1)}, u32[]{:S(2)}, u32[]{:S(2)}) async-start(f32[8,16,384]{2,1,0:T(8,128)} %shard_map.112), calls=%async_computation.2 | async-start | bytes 393216 | tf_op jit(solution)/shard_map/all_to_all | solution.py:26
  180.4 8.2 %all-to-all-done.2.refs_0_ = f32[8,16,384]{2,1,0:T(8,128)S(1)} async-done(((f32[8,16,384]{2,1,0:T(8,128)}), f32[8,16,384]{2,1,0:T(8,128)S(1)}, u32[]{:S(2)}, u32[]{:S(2)}) %all-to-all-start.2) | async-done | bytes 196640 | tf_op jit(solution)/shard_map/all_to_all | solution.py:26
  189.6 6.4 %all-to-all-start.3 = ((bf16[32,16,128]{2,1,0:T(8,128)(2,1)}), bf16[32,16,128]{2,1,0:T(8,128)(2,1)S(1)}, u32[]{:S(2)}, u32[]{:S(2)}) async-start(bf16[32,16,128]{2,1,0:T(8,128)(2,1)} %shard_map.113), calls=%async_computation.3 | async-start | bytes 262144 | tf_op jit(solution)/shard_map/all_to_all | solution.py:26
  196.1 7.6 %all-to-all-done.3 = bf16[32,16,128]{2,1,0:T(8,128)(2,1)S(1)} async-done(((bf16[32,16,128]{2,1,0:T(8,128)(2,1)}), bf16[32,16,128]{2,1,0:T(8,128)(2,1)S(1)}, u32[]{:S(2)}, u32[]{:S(2)}) %all-to-all-start.3) | async-done | bytes 131104 | tf_op jit(solution)/shard_map/all_to_all | solution.py:26
  205.0 3.6 %fusion.38 = f32[64,8192]{1,0:T(8,128)S(1)} fusion(bf16[64,256]{1,0:T(8,128)(2,1)S(1)} %shard_map.114, bf16[8192,256]{1,0:T(8,128)(2,1)} %param.21), kind=kOutput, calls=%fused_computation.79 | convolution fusion | flops 268435456 | bytes 6324224 | tf_op jit(solution)/shard_map/dot_general | solution.py:354
  211.1 13.6 %all_to_all.26 = bf16[16,2,8192]{2,1,0:T(2,128)(2,1)S(1)} all-to-all(bf16[16,2,8192]{2,1,0:T(2,128)(2,1)S(1)} %reshape.95), channel_id=1, replica_groups={{0,2,4,6,8,10,12,14,16,18,20,22,24,26,28,30},{1,3,5,7,9,11,13,15,17,19,..., dimensions={0} | all-to-all | bytes 1048576 | tf_op jit(solution)/shard_map/all_to_all | solution.py:26
  (85 shorter events, 24.8 us)
Async XLA Ops:
  0.0 36.1 %copy-start = (bf16[4008,64]{0,1:T(8,128)(2,1)S(1)}, bf16[4008,64]{0,1:T(8,128)(2,1)}, u32[]{:S(2)}) copy-start(bf16[4008,64]{0,1:T(8,128)(2,1)} %param.18) | copy-start | bytes 1539076
  2.9 17.2 %all-to-all-start = ((bf16[8,80,128]{2,1,0:T(8,128)(2,1)}), bf16[8,80,128]{2,1,0:T(8,128)(2,1)S(1)}, u32[]{:S(2)}, u32[]{:S(2)}) async-start(bf16[8,80,128]{2,1,0:T(8,128)(2,1)} %broadcast_in_dim.28), calls=%async_computation | async-start | bytes 327680 | tf_op jit(solution)/shard_map/all_to_all | solution.py:26
  20.1 15.7 %copy-start.6 = (bf16[64,448]{1,0:T(8,128)(2,1)S(1)}, bf16[64,448]{1,0:T(8,128)(2,1)}, u32[]{:S(2)}) copy-start(bf16[64,448]{1,0:T(8,128)(2,1)} %param.14) | copy-start | bytes 172036
  20.1 15.7 %copy-start.7 = (bf16[448,64]{0,1:T(8,128)(2,1)S(1)}, bf16[448,64]{0,1:T(8,128)(2,1)}, u32[]{:S(2)}) copy-start(bf16[448,64]{0,1:T(8,128)(2,1)} %param.19) | copy-start | bytes 172036
  20.1 8.0 %collective-permute-start = (bf16[512,128]{1,0:T(8,128)(2,1)S(1)}, bf16[512,128]{1,0:T(8,128)(2,1)S(1)}, u32[]{:S(2)}, u32[]{:S(2)}) collective-permute-start(bf16[512,128]{1,0:T(8,128)(2,1)S(1)} %bitcast.54), channel_id=1, source_target_pairs={{0,2},{1,3},{2,4},{3,5},{4,6},{5,7},{6,0},{7,1},{8,10},{9,11},{10,... | collective-permute-start | bytes 393224 | tf_op jit(solution)/shard_map/ppermute | solution.py:259
  23.9 47.5 %collective-permute-start.10 = (bf16[504,512]{1,0:T(8,128)(2,1)}, bf16[504,512]{1,0:T(8,128)(2,1)}, u32[]{:S(2)}, u32[]{:S(2)}) collective-permute-start(bf16[504,512]{1,0:T(8,128)(2,1)} %get-tuple-element.23), channel_id=1, source_target_pairs={{0,32},{32,64},{64,96},{96,128},{128,160},{160,192},{192,224},{224... | collective-permute-start | bytes 1548296 | tf_op jit(solution)/shard_map/ppermute | solution.py:247
  24.4 6.2 %collective-permute-start.1 = (bf16[512,128]{1,0:T(8,128)(2,1)S(1)}, bf16[512,128]{1,0:T(8,128)(2,1)S(1)}, u32[]{:S(2)}, u32[]{:S(2)}) collective-permute-start(bf16[512,128]{1,0:T(8,128)(2,1)S(1)} %bitcast.55), channel_id=1, source_target_pairs={{0,4},{1,5},{2,6},{3,7},{4,0},{5,1},{6,2},{7,3},{8,12},{9,13},{10,... | collective-permute-start | bytes 393224 | tf_op jit(solution)/shard_map/ppermute | solution.py:259
  26.9 3.8 %collective-permute-start.2 = (bf16[512,128]{1,0:T(8,128)(2,1)S(1)}, bf16[512,128]{1,0:T(8,128)(2,1)S(1)}, u32[]{:S(2)}, u32[]{:S(2)}) collective-permute-start(bf16[512,128]{1,0:T(8,128)(2,1)S(1)} %bitcast.56), channel_id=1, source_target_pairs={{0,6},{1,7},{2,0},{3,1},{4,2},{5,3},{6,4},{7,5},{8,14},{9,15},{10,... | collective-permute-start | bytes 393224 | tf_op jit(solution)/shard_map/ppermute | solution.py:259
  30.7 14.1 %collective-permute-start.3 = (bf16[4,512,128]{2,1,0:T(8,128)(2,1)S(1)}, bf16[4,512,128]{2,1,0:T(8,128)(2,1)S(1)}, u32[]{:S(2)}, u32[]{:S(2)}) collective-permute-start(bf16[4,512,128]{2,1,0:T(8,128)(2,1)S(1)} %bitcast_dynamic-update-slice_fusion.refs_4_), channel_id=1, source_target_pairs={{0,8},{1,9},{2,10},{3,11},{4,12},{5,13},{6,14},{7,15},{8,16},{9,17... | collective-permute-start | bytes 1572872 | tf_op jit(solution)/shard_map/ppermute | solution.py:259
  32.1 21.7 %collective-permute-start.4 = (bf16[4,512,128]{2,1,0:T(8,128)(2,1)S(1)}, bf16[4,512,128]{2,1,0:T(8,128)(2,1)S(1)}, u32[]{:S(2)}, u32[]{:S(2)}) collective-permute-start(bf16[4,512,128]{2,1,0:T(8,128)(2,1)S(1)} %bitcast_dynamic-update-slice_fusion.refs_4_), channel_id=1, source_target_pairs={{0,16},{1,17},{2,18},{3,19},{4,20},{5,21},{6,22},{7,23},{8,24},{9,... | collective-permute-start | bytes 1572872 | tf_op jit(solution)/shard_map/ppermute | solution.py:259
  34.7 24.1 %collective-permute-start.5 = (bf16[4,512,128]{2,1,0:T(8,128)(2,1)S(1)}, bf16[4,512,128]{2,1,0:T(8,128)(2,1)}, u32[]{:S(2)}, u32[]{:S(2)}) collective-permute-start(bf16[4,512,128]{2,1,0:T(8,128)(2,1)S(1)} %bitcast_dynamic-update-slice_fusion.refs_4_), channel_id=1, source_target_pairs={{0,24},{1,25},{2,26},{3,27},{4,28},{5,29},{6,30},{7,31},{8,0},{9,1... | collective-permute-start | bytes 1572872 | tf_op jit(solution)/shard_map/ppermute | solution.py:259
  36.2 29.9 %copy-start.2 = (bf16[4096,64]{0,1:T(8,128)(2,1)S(1)}, bf16[4096,64]{0,1:T(8,128)(2,1)}, u32[]{:S(2)}) copy-start(bf16[4096,64]{0,1:T(8,128)(2,1)} %param.20) | copy-start | bytes 1572868
  36.2 29.9 %copy-start.3 = (bf16[4096,64]{0,1:T(8,128)(2,1)S(1)}, bf16[4096,64]{0,1:T(8,128)(2,1)}, u32[]{:S(2)}) copy-start(bf16[4096,64]{0,1:T(8,128)(2,1)} %param.17) | copy-start | bytes 1572868
  36.3 29.9 %copy-start.4 = (f32[4096]{0:T(1024)S(1)}, f32[4096]{0:T(1024)}, u32[]{:S(2)}) copy-start(f32[4096]{0:T(1024)} %param.12) | copy-start | bytes 49156
  39.8 19.4 %collective-permute-start.6 = (bf16[4,512,128]{2,1,0:T(8,128)(2,1)S(1)}, bf16[4,512,128]{2,1,0:T(8,128)(2,1)}, u32[]{:S(2)}, u32[]{:S(2)}) collective-permute-start(bf16[4,512,128]{2,1,0:T(8,128)(2,1)S(1)} %bitcast_dynamic-update-slice_fusion.refs_4_), channel_id=1, source_target_pairs={{0,1},{1,0},{2,3},{3,2},{4,5},{5,4},{6,7},{7,6},{8,9},{9,8},{10,11... | collective-permute-start | bytes 1572872 | tf_op jit(solution)/shard_map/ppermute | solution.py:259
  44.9 15.7 %collective-permute-start.7 = (bf16[4,512,128]{2,1,0:T(8,128)(2,1)S(1)}, bf16[4,512,128]{2,1,0:T(8,128)(2,1)}, u32[]{:S(2)}, u32[]{:S(2)}) collective-permute-start(bf16[4,512,128]{2,1,0:T(8,128)(2,1)S(1)} %collective-permute-done.3.refs_5_), channel_id=1, source_target_pairs={{0,1},{1,0},{2,3},{3,2},{4,5},{5,4},{6,7},{7,6},{8,9},{9,8},{10,11... | collective-permute-start | bytes 1572872 | tf_op jit(solution)/shard_map/ppermute | solution.py:259
  53.8 11.0 %collective-permute-start.8 = (bf16[4,512,128]{2,1,0:T(8,128)(2,1)S(1)}, bf16[4,512,128]{2,1,0:T(8,128)(2,1)}, u32[]{:S(2)}, u32[]{:S(2)}) collective-permute-start(bf16[4,512,128]{2,1,0:T(8,128)(2,1)S(1)} %collective-permute-done.4.refs_6_), channel_id=1, source_target_pairs={{0,1},{1,0},{2,3},{3,2},{4,5},{5,4},{6,7},{7,6},{8,9},{9,8},{10,11... | collective-permute-start | bytes 1572872 | tf_op jit(solution)/shard_map/ppermute | solution.py:259
  58.8 6.3 %collective-permute-start.9 = (bf16[4,512,128]{2,1,0:T(8,128)(2,1)}, bf16[4,512,128]{2,1,0:T(8,128)(2,1)}, u32[]{:S(2)}, u32[]{:S(2)}) collective-permute-start(bf16[4,512,128]{2,1,0:T(8,128)(2,1)} %collective-permute-done.5.refs_7_), channel_id=1, source_target_pairs={{0,1},{1,0},{2,3},{3,2},{4,5},{5,4},{6,7},{7,6},{8,9},{9,8},{10,11... | collective-permute-start | bytes 1572872 | tf_op jit(solution)/shard_map/ppermute | solution.py:259
  59.2 23.1 %collective-permute-start.12 = (bf16[504,512]{1,0:T(8,128)(2,1)}, bf16[504,512]{1,0:T(8,128)(2,1)S(1)}, u32[]{:S(2)}, u32[]{:S(2)}) collective-permute-start(bf16[504,512]{1,0:T(8,128)(2,1)} %get-tuple-element.21), channel_id=1, source_target_pairs={{0,128},{32,160},{64,192},{96,224},{128,0},{160,32},{192,64},{224,... | collective-permute-start | bytes 1548296 | tf_op jit(solution)/shard_map/ppermute | solution.py:247
  60.6 60.5 %collective-permute-start.13 = (bf16[504,512]{1,0:T(8,128)(2,1)}, bf16[504,512]{1,0:T(8,128)(2,1)S(1)}, u32[]{:S(2)}, u32[]{:S(2)}) collective-permute-start(bf16[504,512]{1,0:T(8,128)(2,1)} %get-tuple-element.20), channel_id=1, source_target_pairs={{0,96},{32,128},{64,160},{96,192},{128,224},{160,0},{192,32},{224,... | collective-permute-start | bytes 1548296 | tf_op jit(solution)/shard_map/ppermute | solution.py:247
  64.8 57.9 %collective-permute-start.14 = (bf16[504,512]{1,0:T(8,128)(2,1)}, bf16[504,512]{1,0:T(8,128)(2,1)S(1)}, u32[]{:S(2)}, u32[]{:S(2)}) collective-permute-start(bf16[504,512]{1,0:T(8,128)(2,1)} %get-tuple-element.19), channel_id=1, source_target_pairs={{0,160},{32,192},{64,224},{96,0},{128,32},{160,64},{192,96},{224,1... | collective-permute-start | bytes 1548296 | tf_op jit(solution)/shard_map/ppermute | solution.py:247
  65.1 65.9 %collective-permute-start.11 = (bf16[504,512]{1,0:T(8,128)(2,1)}, bf16[504,512]{1,0:T(8,128)(2,1)}, u32[]{:S(2)}, u32[]{:S(2)}) collective-permute-start(bf16[504,512]{1,0:T(8,128)(2,1)} %get-tuple-element.22), channel_id=1, source_target_pairs={{0,224},{32,0},{64,32},{96,64},{128,96},{160,128},{192,160},{224,1... | collective-permute-start | bytes 1548296 | tf_op jit(solution)/shard_map/ppermute | solution.py:247
  71.4 51.3 %copy-start.1 = (bf16[640,4096]{1,0:T(8,128)(2,1)}, bf16[640,4096]{1,0:T(8,128)(2,1)S(1)}, u32[]{:S(2)}) copy-start(bf16[640,4096]{1,0:T(8,128)(2,1)S(1)} %get-tuple-element.12.lhs_ref) | copy-start | bytes 15728644
  71.4 63.0 %collective-permute-start.15 = (bf16[504,512]{1,0:T(8,128)(2,1)}, bf16[504,512]{1,0:T(8,128)(2,1)S(1)}, u32[]{:S(2)}, u32[]{:S(2)}) collective-permute-start(bf16[504,512]{1,0:T(8,128)(2,1)} %get-tuple-element.18), channel_id=1, source_target_pairs={{0,64},{32,96},{64,128},{96,160},{128,192},{160,224},{192,0},{224,... | collective-permute-start | bytes 1548296 | tf_op jit(solution)/shard_map/ppermute | solution.py:247
  76.5 5.9 %copy-start.5 = (bf16[504,512]{1,0:T(8,128)(2,1)S(1)}, bf16[504,512]{1,0:T(8,128)(2,1)}, u32[]{:S(2)}) copy-start(bf16[504,512]{1,0:T(8,128)(2,1)} %get-tuple-element.17) | copy-start | bytes 1548292
  82.4 72.3 %collective-permute-start.16 = (bf16[504,512]{1,0:T(8,128)(2,1)S(1)}, bf16[504,512]{1,0:T(8,128)(2,1)S(1)}, u32[]{:S(2)}, u32[]{:S(2)}) collective-permute-start(bf16[504,512]{1,0:T(8,128)(2,1)S(1)} %copy-done.5), channel_id=1, source_target_pairs={{0,192},{32,224},{64,0},{96,32},{128,64},{160,96},{192,128},{224,1... | collective-permute-start | bytes 1548296 | tf_op jit(solution)/shard_map/ppermute | solution.py:247
  124.4 30.3 %slice-start = ((s8[5242880]{0:T(1024)(128)(4,1)}), s8[1048576]{0:T(1024)(128)(4,1)S(1)}, s32[]{:S(2)}) async-start(s8[5242880]{0:T(1024)(128)(4,1)} %bitcast.46), calls=%async_computation.5 | async-start | bytes 2097152
  127.3 27.4 %slice-start.1 = ((s8[5242880]{0:T(1024)(128)(4,1)}), s8[4194304]{0:T(1024)(128)(4,1)S(1)}, s32[]{:S(2)}) async-start(s8[5242880]{0:T(1024)(128)(4,1)} %bitcast.46), calls=%async_computation.6 | async-start | bytes 8388608
  158.4 1.9 collective-permute-start.17
  176.4 12.2 %all-to-all-start.2 = ((f32[8,16,384]{2,1,0:T(8,128)}), f32[8,16,384]{2,1,0:T(8,128)S(1)}, u32[]{:S(2)}, u32[]{:S(2)}) async-start(f32[8,16,384]{2,1,0:T(8,128)} %shard_map.112), calls=%async_computation.2 | async-start | bytes 393216 | tf_op jit(solution)/shard_map/all_to_all | solution.py:26
  189.6 14.1 %all-to-all-start.3 = ((bf16[32,16,128]{2,1,0:T(8,128)(2,1)}), bf16[32,16,128]{2,1,0:T(8,128)(2,1)S(1)}, u32[]{:S(2)}, u32[]{:S(2)}) async-start(bf16[32,16,128]{2,1,0:T(8,128)(2,1)} %shard_map.113), calls=%async_computation.3 | async-start | bytes 262144 | tf_op jit(solution)/shard_map/all_to_all | solution.py:26
  208.6 2.0 collective-permute-start.18

commit v2 on v1

--- a/solution.py
+++ b/solution.py
@@ -76,33 +76,27 @@
 
 
 def soft_kernel(
-    info, sums_ref, lhs_ref, first_ref, last_ref, vocab_ref, label_ref, ffn_ref, keep_ref, send_ref, out_ref
+    info, sums_ref, lhs_ref, first_ref, last_ref, vocab_ref, label_ref, ffn_ref, keep_ref, send_ref,
+    logits_ref, rows_ref, stats_ref,
 ):
     tokens, rank = label_ref.shape[0], vocab_ref.shape[0]
     columns, depth = last_ref.shape
-
-    def finished(first, count):
-        total = sums_ref[first : first + count]
-        for n, ref in enumerate((first_ref, last_ref)):
-            at = pl.ds(pl.multiple_of(info[4 + n], depth), depth)
-            total += lax.dot_general(
-                lhs_ref[first : first + count, at], ref[...], by_last, preferred_element_type=f32
-            )
-        return total
-
-    fold = finished(tokens, 2 * rank)
-    fold = fold[:rank] + fold[rank:]
+    total = sums_ref[...]
+    for n, ref in enumerate((first_ref, last_ref)):
+        at = pl.ds(pl.multiple_of(info[4 + n], depth), depth)
+        total += lax.dot_general(lhs_ref[:, at], ref[...], by_last, preferred_element_type=f32)
+    logits_ref[...] = total
+    fold = logits_ref[tokens : tokens + rank] + logits_ref[tokens + rank :]
     fold_high = fold.astype(bf16)
     fold_low = (fold - fold_high.astype(f32)).astype(bf16)
     right = jnp.concatenate([vocab_ref[...], fold_high, fold_low, fold_low], axis=0)
-    keep = lax.broadcasted_iota(jnp.int32, (1, 2 * rank), 1) >= rank
     spot = lax.broadcasted_iota(jnp.int32, (1, columns), 1)
     counted = spot >= info[1]
-    count = 128
+    count = 64
     lane = lax.broadcasted_iota(jnp.int32, (count, 2 * rank), 1)
     for first in range(0, tokens, count):
         rows = slice(first, first + count)
-        logits = finished(first, count)
+        logits = logits_ref[rows]
         peak = jnp.max(jnp.where(counted, logits, -jnp.inf), axis=1, keepdims=True)
         grown = jnp.where(counted, jnp.exp(jnp.minimum(logits - peak, 0.0)), 0.0)
         total = jnp.sum(grown, axis=1, keepdims=True)
@@ -110,25 +104,29 @@
         hit = counted & (label_ref[rows] == spot + info[0])
         dot_all = jnp.sum(rounded.astype(f32) * logits, axis=1, keepdims=True)
         dot_hit = jnp.sum(jnp.where(hit, logits, 0.0), axis=1, keepdims=True)
-        soft = lax.dot_general(rounded, right, by_last, preferred_element_type=f32)
-        mark = lax.dot_general(hit.astype(f32).astype(bf16), right, by_last, preferred_element_type=f32)
-        out_ref[rows, : 2 * rank] = soft[:, : 2 * rank] + jnp.where(keep, soft[:, 2 * rank :], 0.0)
-        out_ref[rows, 2 * rank : 4 * rank] = mark[:, : 2 * rank] + jnp.where(keep, mark[:, 2 * rank :], 0.0)
+        rows_ref[rows] = rounded
+        rows_ref[tokens + first : tokens + first + count] = hit.astype(f32).astype(bf16)
         stats = jnp.where(lane == 0, peak, jnp.where(lane == 1, total, jnp.where(lane == 2, dot_all, dot_hit)))
-        out_ref[rows, 4 * rank :] = jnp.where(lane < 4, stats, 0.0)
+        stats_ref[rows] = jnp.where(lane < 4, stats, 0.0)
     here = ffn_ref.shape[0]
     own = pl.ds(pl.multiple_of(info[2], here), here)
     lane = lax.broadcasted_iota(jnp.int32, (here, 2 * rank), 1)
-    out_ref[own, 4 * rank :] = jnp.where(lane < rank, out_ref[own, 4 * rank :], ffn_ref[...])
+    stats_ref[own] = jnp.where(lane < rank, stats_ref[own], ffn_ref[...])
+    both = lax.dot_general(rows_ref[...], right, by_last, preferred_element_type=f32)
+    lane = lax.broadcasted_iota(jnp.int32, (1, 2 * rank), 1)
+    both = both[:, : 2 * rank] + jnp.where(lane >= rank, both[:, 2 * rank :], 0.0)
+    soft, mark = both[:tokens], both[tokens:]
     mine = keep_ref.shape[1]
     for core in range(2):
 
         @pl.when(info[3] == core)
         def _():
             for pair in range(keep_ref.shape[0]):
-                first, second = 2 * pair + core, 2 * pair + 1 - core
-                keep_ref[pair] = out_ref[mine * first : mine * (first + 1)]
-                send_ref[pair] = out_ref[mine * second : mine * (second + 1)]
+                for ref, place in ((keep_ref, 2 * pair + core), (send_ref, 2 * pair + 1 - core)):
+                    rows = slice(mine * place, mine * (place + 1))
+                    ref[pair, :, : 2 * rank] = soft[rows]
+                    ref[pair, :, 2 * rank : 4 * rank] = mark[rows]
+                    ref[pair, :, 4 * rank :] = stats_ref[rows]
 
 
 def merged(x):
@@ -179,9 +177,16 @@
         out_ref[half + copy] = second
 
 
-def query_kernel(info, sides_ref, out_ref, *, span):
+def query_kernel(info, sides_ref, out_ref, *, span, each):
     rank = sides_ref.shape[1] // 2
-    sides = sides_ref[...]
+    blocks = sides_ref.shape[0] // (each * span)
+    sides = []
+    for far in range(2):
+        core = info[1] + far - 2 * info[1] * far
+        for n in range(blocks // 2):
+            start = pl.multiple_of((2 * n + core) * each * span, each * span)
+            sides.append(sides_ref[pl.ds(start, each * span), :])
+    sides = jnp.concatenate(sides, axis=0)
     features = out_ref.shape[1]
     column = lax.broadcasted_iota(jnp.int32, (2 * rank, features), 0)
     wanted = rank + info[0] + lax.broadcasted_iota(jnp.int32, (2 * rank, features), 1) // rank
@@ -189,17 +194,7 @@
     left = jnp.dot(sides, chosen, preferred_element_type=f32)
     right = sides[:, :rank].astype(f32)
     product = left * jnp.concatenate([right] * (features // rank), axis=1)
-    query = jnp.sum(product.reshape(-1, span, features), axis=1).astype(bf16)
-    count = query.shape[0]
-    spot = lax.broadcasted_iota(jnp.int32, (count, count), 0)
-    source = lax.broadcasted_iota(jnp.int32, (count, count), 1)
-    half, each = count // 2, info[1]
-    far = spot // half
-    near = spot - far * half
-    core = info[2] + far - 2 * info[2] * far
-    wanted = (2 * (near // each) + core) * each + lax.rem(near, each)
-    order = (source == wanted).astype(f32).astype(bf16)
-    out_ref[...] = jnp.dot(order, query, preferred_element_type=f32).astype(bf16)
+    out_ref[...] = jnp.sum(product.reshape(-1, span, features), axis=1).astype(bf16)
 
 
 def per_device(
@@ -313,7 +308,11 @@
         out_shape=(jax.ShapeDtypeStruct(by_core, f32), jax.ShapeDtypeStruct(by_core, f32)),
         in_specs=[in_smem, *vmem(7)],
         out_specs=(in_vmem, in_vmem),
-        scratch_shapes=[pltpu.VMEM((tokens, 6 * rank), f32)],
+        scratch_shapes=[
+            pltpu.VMEM((tokens + 2 * rank, block), f32),
+            pltpu.VMEM((2 * tokens, block), bf16),
+            pltpu.VMEM((tokens, 2 * rank), f32),
+        ],
         compiler_params=small,
     )(info, sums, lhs, came[last[0]], came[last[1]], vocab_turned, all_labels, ffn)
     packed = pl.pallas_call(
@@ -345,12 +344,12 @@
     queries = tokens // seq_span
     per = features // rank
     query = pl.pallas_call(
-        lambda *refs: query_kernel(*refs, span=seq_span),
+        lambda *refs: query_kernel(*refs, span=seq_span, each=queries // lanes),
         out_shape=jax.ShapeDtypeStruct((queries, features), bf16),
         in_specs=[in_smem, *vmem(1)],
         out_specs=in_vmem,
         compiler_params=small,
-    )(jnp.stack([j % (lanes // 2) * per, queries // lanes, core_at]).astype(jnp.int32), sides)
+    )(jnp.stack([j % (lanes // 2) * per, core_at]).astype(jnp.int32), sides)
     partial = lax.dot_general(query, store, by_last, preferred_element_type=f32)
     half = queries // 2
     other = moved(partial[half:].astype(bf16), lambda i: i ^ 1)

time: 226 us -> 225 us (level)
  no operation moved by 1% of the time
where the time goes in v2:
time: 225 us; the launch traced here: 224 us
  waiting for transfers between devices  88.3 us (39%)
  starting transfers between devices  65.1 us (29%)
  blocking collectives  28.7 us (13%)
  matrix products  16.5 us (7%)
  local copies, waits for them, and re-layouts  11.8 us (5%)
  Pallas kernels  10.4 us (5%)
  other arithmetic  2.92 us (1%)
    ppermute x7, waiting for transfers between devices, head_moves(): lax.ppermute(cut, 'grp', [(i, (i + s) % groups) for i in range(groups)])  54.9 us
    all_to_all x2, blocking collectives, traded(): lax.all_to_all(value, axis, split_axis=0, concat_axis=0, tiled=True, axis...  28.7 us
    ppermute x12, starting transfers between devices, moved(): return lax.ppermute(value, 'tp', [(i, move(i)) for i in range(lanes)])  26.1 us
    all_to_all x3, waiting for transfers between devices, traded(): lax.all_to_all(value, axis, split_axis=0, concat_axis=0, tiled=True, axis...  24 us
    ppermute x7, starting transfers between devices, head_moves(): lax.ppermute(cut, 'grp', [(i, (i + s) % groups) for i in range(groups)])  20.1 us
    all_to_all x3, starting transfers between devices, traded(): lax.all_to_all(value, axis, split_axis=0, concat_axis=0, tiled=True, axis...  18.8 us
    dot_general x6, matrix products, per_device(): term = lax.dot_general(depth, came[s], by_last, preferred_element_type=f32)  12.8 us
    ppermute x12, waiting for transfers between devices, moved(): return lax.ppermute(value, 'tp', [(i, move(i)) for i in range(lanes)])  9.3 us
  transfers between devices with their start and end apart: 22, of which 12 were waited for; matrix products, arithmetic and copies ran while one was open for 10% of the time, Pallas kernels for 2%

profile of v2, /device:TPU:1, one launch (start us, length us, event | category | flops | bytes accessed | tf_op | source)
XLA Modules:
  0.0 224.0 jit_solution(13050814576227986495)
XLA Ops:
  2.9 9.0 %all-to-all-start = ((bf16[8,80,128]{2,1,0:T(8,128)(2,1)}), bf16[8,80,128]{2,1,0:T(8,128)(2,1)S(1)}, u32[]{:S(2)}, u32[]{:S(2)}) async-start(bf16[8,80,128]{2,1,0:T(8,128)(2,1)} %broadcast_in_dim.28), calls=%async_computation | async-start | bytes 327680 | tf_op jit(solution)/shard_map/all_to_all | solution.py:26
  11.9 8.2 %all-to-all-done = bf16[8,80,128]{2,1,0:T(8,128)(2,1)S(1)} async-done(((bf16[8,80,128]{2,1,0:T(8,128)(2,1)}), bf16[8,80,128]{2,1,0:T(8,128)(2,1)S(1)}, u32[]{:S(2)}, u32[]{:S(2)}) %all-to-all-start) | async-done | bytes 163872 | tf_op jit(solution)/shard_map/all_to_all | solution.py:26
  21.4 2.4 %dynamic-slice_bitcast_fusion = (bf16[504,512]{1,0:T(8,128)(2,1)}, bf16[504,512]{1,0:T(8,128)(2,1)}) fusion(bf16[512,4008]{0,1:T(8,128)(2,1)} %param.13, s32[]{:T(128)S(6)} %select_n.222, s32[]{:T(128)S(6)} %select_n.218), kind=kLoop, calls=%fused_computation.19 | loop fusion | bytes 2064392 | tf_op jit(solution)/shard_map/dynamic_slice | solution.py:241
  24.4 2.5 %collective-permute-start.1 = (bf16[512,128]{1,0:T(8,128)(2,1)S(1)}, bf16[512,128]{1,0:T(8,128)(2,1)S(1)}, u32[]{:S(2)}, u32[]{:S(2)}) collective-permute-start(bf16[512,128]{1,0:T(8,128)(2,1)S(1)} %bitcast.55), channel_id=1, source_target_pairs={{0,4},{1,5},{2,6},{3,7},{4,0},{5,1},{6,2},{7,3},{8,12},{9,13},{10,... | collective-permute-start | bytes 393224 | tf_op jit(solution)/shard_map/ppermute | solution.py:254
  28.2 2.4 %collective-permute-done.1 = bf16[512,128]{1,0:T(8,128)(2,1)S(1)} collective-permute-done((bf16[512,128]{1,0:T(8,128)(2,1)S(1)}, bf16[512,128]{1,0:T(8,128)(2,1)S(1)}, u32[]{:S(2)}, u32[]{:S(2)}) %collective-permute-start.1) | collective-permute-done | bytes 131104 | tf_op jit(solution)/shard_map/ppermute | solution.py:254
  32.1 2.6 %collective-permute-start.4 = (bf16[4,512,128]{2,1,0:T(8,128)(2,1)S(1)}, bf16[4,512,128]{2,1,0:T(8,128)(2,1)S(1)}, u32[]{:S(2)}, u32[]{:S(2)}) collective-permute-start(bf16[4,512,128]{2,1,0:T(8,128)(2,1)S(1)} %bitcast_dynamic-update-slice_fusion.refs_4_), channel_id=1, source_target_pairs={{0,16},{1,17},{2,18},{3,19},{4,20},{5,21},{6,22},{7,23},{8,24},{9,... | collective-permute-start | bytes 1572872 | tf_op jit(solution)/shard_map/ppermute | solution.py:254
  36.3 3.6 %constant_dynamic-slice_fusion = (bf16[504,512]{1,0:T(8,128)(2,1)}, bf16[504,512]{1,0:T(8,128)(2,1)}, bf16[504,512]{1,0:T(8,128)(2,1)}, bf16[504,512]{1,0:T(8,128)(2,1)}, bf16[504,512]{1,0:T(8,128)(2,1)}) fusion(bf16[4008,512]{1,0:T(8,128)(2,1)} %bitcast.52, s32[]{:T(128)S(6)} %select_n.238, s32[]{:T(128)S(6)} %select_n.236, s32[]{:T(128)S(6)} %select_n.234, ...), kind=kLoop, calls=%fused_computation.35 | loop fusion | bytes 5160980 | tf_op jit(solution)/shard_map/dynamic_slice | solution.py:241
  39.8 5.0 %collective-permute-start.6 = (bf16[4,512,128]{2,1,0:T(8,128)(2,1)S(1)}, bf16[4,512,128]{2,1,0:T(8,128)(2,1)}, u32[]{:S(2)}, u32[]{:S(2)}) collective-permute-start(bf16[4,512,128]{2,1,0:T(8,128)(2,1)S(1)} %bitcast_dynamic-update-slice_fusion.refs_4_), channel_id=1, source_target_pairs={{0,1},{1,0},{2,3},{3,2},{4,5},{5,4},{6,7},{7,6},{8,9},{9,8},{10,11... | collective-permute-start | bytes 1572872 | tf_op jit(solution)/shard_map/ppermute | solution.py:254
  44.9 5.0 %collective-permute-start.7 = (bf16[4,512,128]{2,1,0:T(8,128)(2,1)S(1)}, bf16[4,512,128]{2,1,0:T(8,128)(2,1)}, u32[]{:S(2)}, u32[]{:S(2)}) collective-permute-start(bf16[4,512,128]{2,1,0:T(8,128)(2,1)S(1)} %collective-permute-done.3.refs_5_), channel_id=1, source_target_pairs={{0,1},{1,0},{2,3},{3,2},{4,5},{5,4},{6,7},{7,6},{8,9},{9,8},{10,11... | collective-permute-start | bytes 1572872 | tf_op jit(solution)/shard_map/ppermute | solution.py:254
  49.9 3.9 %collective-permute-done.4.refs_6_ = bf16[4,512,128]{2,1,0:T(8,128)(2,1)S(1)} collective-permute-done((bf16[4,512,128]{2,1,0:T(8,128)(2,1)S(1)}, bf16[4,512,128]{2,1,0:T(8,128)(2,1)S(1)}, u32[]{:S(2)}, u32[]{:S(2)}) %collective-permute-start.4) | collective-permute-done | bytes 524320 | tf_op jit(solution)/shard_map/ppermute | solution.py:254
  53.8 5.1 %collective-permute-start.8 = (bf16[4,512,128]{2,1,0:T(8,128)(2,1)S(1)}, bf16[4,512,128]{2,1,0:T(8,128)(2,1)}, u32[]{:S(2)}, u32[]{:S(2)}) collective-permute-start(bf16[4,512,128]{2,1,0:T(8,128)(2,1)S(1)} %collective-permute-done.4.refs_6_), channel_id=1, source_target_pairs={{0,1},{1,0},{2,3},{3,2},{4,5},{5,4},{6,7},{7,6},{8,9},{9,8},{10,11... | collective-permute-start | bytes 1572872 | tf_op jit(solution)/shard_map/ppermute | solution.py:254
  60.6 4.2 %collective-permute-start.13 = (bf16[504,512]{1,0:T(8,128)(2,1)}, bf16[504,512]{1,0:T(8,128)(2,1)S(1)}, u32[]{:S(2)}, u32[]{:S(2)}) collective-permute-start(bf16[504,512]{1,0:T(8,128)(2,1)} %get-tuple-element.20), channel_id=1, source_target_pairs={{0,96},{32,128},{64,160},{96,192},{128,224},{160,0},{192,32},{224,... | collective-permute-start | bytes 1548296 | tf_op jit(solution)/shard_map/ppermute | solution.py:242
  66.2 5.2 %shard_map.109 = (bf16[640,4096]{1,0:T(8,128)(2,1)S(1)}, f32[16,256]{1,0:T(8,128)S(1)}) custom-call(s32[3]{0:T(128)S(1)} %pad_add_fusion.1.refs_0_, f32[1,4096]{1,0:T(1,128)S(1)} %bitcast.51, bf16[64,4096]{1,0:T(8,128)(2,1)S(1)} %bitcast.49, bf16[64,4096]{1,0:T(8,128)(2,1)S(1)} %bitcast.50, ...), custom_call_target="tpu_custom_call" | custom-call | tf_op jit(solution)/shard_map/pallas_call | solution.py:267
  71.4 3.5 %collective-permute-start.15 = (bf16[504,512]{1,0:T(8,128)(2,1)}, bf16[504,512]{1,0:T(8,128)(2,1)S(1)}, u32[]{:S(2)}, u32[]{:S(2)}) collective-permute-start(bf16[504,512]{1,0:T(8,128)(2,1)} %get-tuple-element.18), channel_id=1, source_target_pairs={{0,64},{32,96},{64,128},{96,160},{128,192},{160,224},{192,0},{224,... | collective-permute-start | bytes 1548296 | tf_op jit(solution)/shard_map/ppermute | solution.py:242
  74.9 1.6 fusion.11
  76.5 2.8 %convolution_add_fusion.1 = f32[640,504]{0,1:T(8,128)} fusion(f32[640,504]{0,1:T(8,128)S(1)} %fusion.11, bf16[640,4096]{1,0:T(8,128)(2,1)S(1)} %get-tuple-element.12.lhs_ref, s32[]{:T(128)S(6)} %select_n.213, bf16[4008,512]{1,0:T(8,128)(2,1)} %bitcast.53, s32[]{:T(128)S(6)} %select_n.214), kind=kOutput, calls=%fused_computation.4 | convolution fusion | flops 330624000 | bytes 3751944 | tf_op jit(solution)/shard_map/dot_general | solution.py:300
  79.3 3.1 %collective-permute-done.12 = bf16[504,512]{1,0:T(8,128)(2,1)S(1)} collective-permute-done((bf16[504,512]{1,0:T(8,128)(2,1)}, bf16[504,512]{1,0:T(8,128)(2,1)S(1)}, u32[]{:S(2)}, u32[]{:S(2)}) %collective-permute-start.12) | collective-permute-done | bytes 516128 | tf_op jit(solution)/shard_map/ppermute | solution.py:242
  82.4 9.2 %collective-permute-start.16 = (bf16[504,512]{1,0:T(8,128)(2,1)S(1)}, bf16[504,512]{1,0:T(8,128)(2,1)S(1)}, u32[]{:S(2)}, u32[]{:S(2)}) collective-permute-start(bf16[504,512]{1,0:T(8,128)(2,1)S(1)} %copy-done.5), channel_id=1, source_target_pairs={{0,192},{32,224},{64,0},{96,32},{128,64},{160,96},{192,128},{224,1... | collective-permute-start | bytes 1548296 | tf_op jit(solution)/shard_map/ppermute | solution.py:242
  93.2 27.9 %collective-permute-done.13 = bf16[504,512]{1,0:T(8,128)(2,1)S(1)} collective-permute-done((bf16[504,512]{1,0:T(8,128)(2,1)}, bf16[504,512]{1,0:T(8,128)(2,1)S(1)}, u32[]{:S(2)}, u32[]{:S(2)}) %collective-permute-start.13) | collective-permute-done | bytes 516128 | tf_op jit(solution)/shard_map/ppermute | solution.py:242
  122.7 1.7 fusion.4
  124.4 2.9 %copy.27 = f32[640,504]{1,0:T(8,128)} copy(f32[640,504]{0,1:T(8,128)} %convolution_add_fusion.1) | data formatting | bytes 2580480 | tf_op jit(solution)/shard_map/add | solution.py:301
  127.3 3.7 %collective-permute-done.11 = bf16[504,512]{1,0:T(8,128)(2,1)} collective-permute-done((bf16[504,512]{1,0:T(8,128)(2,1)}, bf16[504,512]{1,0:T(8,128)(2,1)}, u32[]{:S(2)}, u32[]{:S(2)}) %collective-permute-start.11) | collective-permute-done | bytes 516128 | tf_op jit(solution)/shard_map/ppermute | solution.py:242
  131.0 3.5 %fusion.2.sums_ref = f32[640,504]{1,0:T(8,128)S(1)} fusion(f32[640,504]{1,0:T(8,128)} %fusion.4, f32[640,504]{1,0:T(8,128)} %fusion.6, f32[640,504]{1,0:T(8,128)} %fusion.8, f32[640,504]{1,0:T(8,128)} %copy.27, bf16[504,512]{1,0:T(8,128)(2,1)} %collective-permute-done.11, bf16[640,4096]{1,0:T(8,128)(2,1)} %copy-done.1, s32[]{:T(128)S(6)} %select_n.220), kind=kOutput, calls=%fused_computation.3 | convolution fusion | flops 331591680 | bytes 7704580 | tf_op jit(solution)/shard_map/dot_general | solution.py:300
  134.5 20.3 %collective-permute-done.16.last_ref = bf16[504,512]{1,0:T(8,128)(2,1)S(1)} collective-permute-done((bf16[504,512]{1,0:T(8,128)(2,1)S(1)}, bf16[504,512]{1,0:T(8,128)(2,1)S(1)}, u32[]{:S(2)}, u32[]{:S(2)}) %collective-permute-start.16) | collective-permute-done | bytes 516128 | tf_op jit(solution)/shard_map/ppermute | solution.py:242
  154.7 2.2 shard_map.110
  159.1 15.1 %all_to_all.25.x_ref = f32[16,16,384]{2,1,0:T(8,128)S(1)} all-to-all(f32[16,16,384]{2,1,0:T(8,128)S(1)} %shard_map.111), channel_id=1, replica_groups={{0,2,4,6,8,10,12,14,16,18,20,22,24,26,28,30},{1,3,5,7,9,11,13,15,17,19,..., dimensions={0} | all-to-all | bytes 786432 | tf_op jit(solution)/shard_map/all_to_all | solution.py:26
  175.0 3.5 %all-to-all-start.2 = ((f32[8,16,384]{2,1,0:T(8,128)}), f32[8,16,384]{2,1,0:T(8,128)S(1)}, u32[]{:S(2)}, u32[]{:S(2)}) async-start(f32[8,16,384]{2,1,0:T(8,128)} %shard_map.112), calls=%async_computation.2 | async-start | bytes 393216 | tf_op jit(solution)/shard_map/all_to_all | solution.py:26
  179.0 8.2 %all-to-all-done.2.refs_0_ = f32[8,16,384]{2,1,0:T(8,128)S(1)} async-done(((f32[8,16,384]{2,1,0:T(8,128)}), f32[8,16,384]{2,1,0:T(8,128)S(1)}, u32[]{:S(2)}, u32[]{:S(2)}) %all-to-all-start.2) | async-done | bytes 196640 | tf_op jit(solution)/shard_map/all_to_all | solution.py:26
  188.2 6.4 %all-to-all-start.3 = ((bf16[32,16,128]{2,1,0:T(8,128)(2,1)}), bf16[32,16,128]{2,1,0:T(8,128)(2,1)S(1)}, u32[]{:S(2)}, u32[]{:S(2)}) async-start(bf16[32,16,128]{2,1,0:T(8,128)(2,1)} %shard_map.113), calls=%async_computation.3 | async-start | bytes 262144 | tf_op jit(solution)/shard_map/all_to_all | solution.py:26
  194.6 7.6 %all-to-all-done.3 = bf16[32,16,128]{2,1,0:T(8,128)(2,1)S(1)} async-done(((bf16[32,16,128]{2,1,0:T(8,128)(2,1)}), bf16[32,16,128]{2,1,0:T(8,128)(2,1)S(1)}, u32[]{:S(2)}, u32[]{:S(2)}) %all-to-all-start.3) | async-done | bytes 131104 | tf_op jit(solution)/shard_map/all_to_all | solution.py:26
  203.2 3.6 %fusion.38 = f32[64,8192]{1,0:T(8,128)S(1)} fusion(bf16[64,256]{1,0:T(8,128)(2,1)S(1)} %shard_map.114, bf16[8192,256]{1,0:T(8,128)(2,1)} %param.21), kind=kOutput, calls=%fused_computation.79 | convolution fusion | flops 268435456 | bytes 6324224 | tf_op jit(solution)/shard_map/dot_general | solution.py:353
  209.3 13.6 %all_to_all.26 = bf16[16,2,8192]{2,1,0:T(2,128)(2,1)S(1)} all-to-all(bf16[16,2,8192]{2,1,0:T(2,128)(2,1)S(1)} %reshape.95), channel_id=1, replica_groups={{0,2,4,6,8,10,12,14,16,18,20,22,24,26,28,30},{1,3,5,7,9,11,13,15,17,19,..., dimensions={0} | all-to-all | bytes 1048576 | tf_op jit(solution)/shard_map/all_to_all | solution.py:26
  (85 shorter events, 24.4 us)
Async XLA Ops:
  0.0 36.1 %copy-start = (bf16[4008,64]{0,1:T(8,128)(2,1)S(1)}, bf16[4008,64]{0,1:T(8,128)(2,1)}, u32[]{:S(2)}) copy-start(bf16[4008,64]{0,1:T(8,128)(2,1)} %param.18) | copy-start | bytes 1539076
  2.9 17.2 %all-to-all-start = ((bf16[8,80,128]{2,1,0:T(8,128)(2,1)}), bf16[8,80,128]{2,1,0:T(8,128)(2,1)S(1)}, u32[]{:S(2)}, u32[]{:S(2)}) async-start(bf16[8,80,128]{2,1,0:T(8,128)(2,1)} %broadcast_in_dim.28), calls=%async_computation | async-start | bytes 327680 | tf_op jit(solution)/shard_map/all_to_all | solution.py:26
  20.1 15.7 %copy-start.6 = (bf16[64,448]{1,0:T(8,128)(2,1)S(1)}, bf16[64,448]{1,0:T(8,128)(2,1)}, u32[]{:S(2)}) copy-start(bf16[64,448]{1,0:T(8,128)(2,1)} %param.14) | copy-start | bytes 172036
  20.1 15.7 %copy-start.7 = (bf16[448,64]{0,1:T(8,128)(2,1)S(1)}, bf16[448,64]{0,1:T(8,128)(2,1)}, u32[]{:S(2)}) copy-start(bf16[448,64]{0,1:T(8,128)(2,1)} %param.19) | copy-start | bytes 172036
  20.1 8.0 %collective-permute-start = (bf16[512,128]{1,0:T(8,128)(2,1)S(1)}, bf16[512,128]{1,0:T(8,128)(2,1)S(1)}, u32[]{:S(2)}, u32[]{:S(2)}) collective-permute-start(bf16[512,128]{1,0:T(8,128)(2,1)S(1)} %bitcast.54), channel_id=1, source_target_pairs={{0,2},{1,3},{2,4},{3,5},{4,6},{5,7},{6,0},{7,1},{8,10},{9,11},{10,... | collective-permute-start | bytes 393224 | tf_op jit(solution)/shard_map/ppermute | solution.py:254
  23.9 47.5 %collective-permute-start.10 = (bf16[504,512]{1,0:T(8,128)(2,1)}, bf16[504,512]{1,0:T(8,128)(2,1)}, u32[]{:S(2)}, u32[]{:S(2)}) collective-permute-start(bf16[504,512]{1,0:T(8,128)(2,1)} %get-tuple-element.23), channel_id=1, source_target_pairs={{0,32},{32,64},{64,96},{96,128},{128,160},{160,192},{192,224},{224... | collective-permute-start | bytes 1548296 | tf_op jit(solution)/shard_map/ppermute | solution.py:242
  24.4 6.2 %collective-permute-start.1 = (bf16[512,128]{1,0:T(8,128)(2,1)S(1)}, bf16[512,128]{1,0:T(8,128)(2,1)S(1)}, u32[]{:S(2)}, u32[]{:S(2)}) collective-permute-start(bf16[512,128]{1,0:T(8,128)(2,1)S(1)} %bitcast.55), channel_id=1, source_target_pairs={{0,4},{1,5},{2,6},{3,7},{4,0},{5,1},{6,2},{7,3},{8,12},{9,13},{10,... | collective-permute-start | bytes 393224 | tf_op jit(solution)/shard_map/ppermute | solution.py:254
  26.9 3.8 %collective-permute-start.2 = (bf16[512,128]{1,0:T(8,128)(2,1)S(1)}, bf16[512,128]{1,0:T(8,128)(2,1)S(1)}, u32[]{:S(2)}, u32[]{:S(2)}) collective-permute-start(bf16[512,128]{1,0:T(8,128)(2,1)S(1)} %bitcast.56), channel_id=1, source_target_pairs={{0,6},{1,7},{2,0},{3,1},{4,2},{5,3},{6,4},{7,5},{8,14},{9,15},{10,... | collective-permute-start | bytes 393224 | tf_op jit(solution)/shard_map/ppermute | solution.py:254
  30.7 14.1 %collective-permute-start.3 = (bf16[4,512,128]{2,1,0:T(8,128)(2,1)S(1)}, bf16[4,512,128]{2,1,0:T(8,128)(2,1)S(1)}, u32[]{:S(2)}, u32[]{:S(2)}) collective-permute-start(bf16[4,512,128]{2,1,0:T(8,128)(2,1)S(1)} %bitcast_dynamic-update-slice_fusion.refs_4_), channel_id=1, source_target_pairs={{0,8},{1,9},{2,10},{3,11},{4,12},{5,13},{6,14},{7,15},{8,16},{9,17... | collective-permute-start | bytes 1572872 | tf_op jit(solution)/shard_map/ppermute | solution.py:254
  32.1 21.7 %collective-permute-start.4 = (bf16[4,512,128]{2,1,0:T(8,128)(2,1)S(1)}, bf16[4,512,128]{2,1,0:T(8,128)(2,1)S(1)}, u32[]{:S(2)}, u32[]{:S(2)}) collective-permute-start(bf16[4,512,128]{2,1,0:T(8,128)(2,1)S(1)} %bitcast_dynamic-update-slice_fusion.refs_4_), channel_id=1, source_target_pairs={{0,16},{1,17},{2,18},{3,19},{4,20},{5,21},{6,22},{7,23},{8,24},{9,... | collective-permute-start | bytes 1572872 | tf_op jit(solution)/shard_map/ppermute | solution.py:254
  34.7 24.1 %collective-permute-start.5 = (bf16[4,512,128]{2,1,0:T(8,128)(2,1)S(1)}, bf16[4,512,128]{2,1,0:T(8,128)(2,1)}, u32[]{:S(2)}, u32[]{:S(2)}) collective-permute-start(bf16[4,512,128]{2,1,0:T(8,128)(2,1)S(1)} %bitcast_dynamic-update-slice_fusion.refs_4_), channel_id=1, source_target_pairs={{0,24},{1,25},{2,26},{3,27},{4,28},{5,29},{6,30},{7,31},{8,0},{9,1... | collective-permute-start | bytes 1572872 | tf_op jit(solution)/shard_map/ppermute | solution.py:254
  36.2 29.9 %copy-start.2 = (bf16[4096,64]{0,1:T(8,128)(2,1)S(1)}, bf16[4096,64]{0,1:T(8,128)(2,1)}, u32[]{:S(2)}) copy-start(bf16[4096,64]{0,1:T(8,128)(2,1)} %param.20) | copy-start | bytes 1572868
  36.2 29.9 %copy-start.3 = (bf16[4096,64]{0,1:T(8,128)(2,1)S(1)}, bf16[4096,64]{0,1:T(8,128)(2,1)}, u32[]{:S(2)}) copy-start(bf16[4096,64]{0,1:T(8,128)(2,1)} %param.17) | copy-start | bytes 1572868
  36.3 29.9 %copy-start.4 = (f32[4096]{0:T(1024)S(1)}, f32[4096]{0:T(1024)}, u32[]{:S(2)}) copy-start(f32[4096]{0:T(1024)} %param.12) | copy-start | bytes 49156
  39.8 19.4 %collective-permute-start.6 = (bf16[4,512,128]{2,1,0:T(8,128)(2,1)S(1)}, bf16[4,512,128]{2,1,0:T(8,128)(2,1)}, u32[]{:S(2)}, u32[]{:S(2)}) collective-permute-start(bf16[4,512,128]{2,1,0:T(8,128)(2,1)S(1)} %bitcast_dynamic-update-slice_fusion.refs_4_), channel_id=1, source_target_pairs={{0,1},{1,0},{2,3},{3,2},{4,5},{5,4},{6,7},{7,6},{8,9},{9,8},{10,11... | collective-permute-start | bytes 1572872 | tf_op jit(solution)/shard_map/ppermute | solution.py:254
  44.9 15.7 %collective-permute-start.7 = (bf16[4,512,128]{2,1,0:T(8,128)(2,1)S(1)}, bf16[4,512,128]{2,1,0:T(8,128)(2,1)}, u32[]{:S(2)}, u32[]{:S(2)}) collective-permute-start(bf16[4,512,128]{2,1,0:T(8,128)(2,1)S(1)} %collective-permute-done.3.refs_5_), channel_id=1, source_target_pairs={{0,1},{1,0},{2,3},{3,2},{4,5},{5,4},{6,7},{7,6},{8,9},{9,8},{10,11... | collective-permute-start | bytes 1572872 | tf_op jit(solution)/shard_map/ppermute | solution.py:254
  53.8 11.0 %collective-permute-start.8 = (bf16[4,512,128]{2,1,0:T(8,128)(2,1)S(1)}, bf16[4,512,128]{2,1,0:T(8,128)(2,1)}, u32[]{:S(2)}, u32[]{:S(2)}) collective-permute-start(bf16[4,512,128]{2,1,0:T(8,128)(2,1)S(1)} %collective-permute-done.4.refs_6_), channel_id=1, source_target_pairs={{0,1},{1,0},{2,3},{3,2},{4,5},{5,4},{6,7},{7,6},{8,9},{9,8},{10,11... | collective-permute-start | bytes 1572872 | tf_op jit(solution)/shard_map/ppermute | solution.py:254
  58.8 6.3 %collective-permute-start.9 = (bf16[4,512,128]{2,1,0:T(8,128)(2,1)}, bf16[4,512,128]{2,1,0:T(8,128)(2,1)}, u32[]{:S(2)}, u32[]{:S(2)}) collective-permute-start(bf16[4,512,128]{2,1,0:T(8,128)(2,1)} %collective-permute-done.5.refs_7_), channel_id=1, source_target_pairs={{0,1},{1,0},{2,3},{3,2},{4,5},{5,4},{6,7},{7,6},{8,9},{9,8},{10,11... | collective-permute-start | bytes 1572872 | tf_op jit(solution)/shard_map/ppermute | solution.py:254
  59.2 23.1 %collective-permute-start.12 = (bf16[504,512]{1,0:T(8,128)(2,1)}, bf16[504,512]{1,0:T(8,128)(2,1)S(1)}, u32[]{:S(2)}, u32[]{:S(2)}) collective-permute-start(bf16[504,512]{1,0:T(8,128)(2,1)} %get-tuple-element.21), channel_id=1, source_target_pairs={{0,128},{32,160},{64,192},{96,224},{128,0},{160,32},{192,64},{224,... | collective-permute-start | bytes 1548296 | tf_op jit(solution)/shard_map/ppermute | solution.py:242
  60.6 60.5 %collective-permute-start.13 = (bf16[504,512]{1,0:T(8,128)(2,1)}, bf16[504,512]{1,0:T(8,128)(2,1)S(1)}, u32[]{:S(2)}, u32[]{:S(2)}) collective-permute-start(bf16[504,512]{1,0:T(8,128)(2,1)} %get-tuple-element.20), channel_id=1, source_target_pairs={{0,96},{32,128},{64,160},{96,192},{128,224},{160,0},{192,32},{224,... | collective-permute-start | bytes 1548296 | tf_op jit(solution)/shard_map/ppermute | solution.py:242
  64.8 57.9 %collective-permute-start.14 = (bf16[504,512]{1,0:T(8,128)(2,1)}, bf16[504,512]{1,0:T(8,128)(2,1)S(1)}, u32[]{:S(2)}, u32[]{:S(2)}) collective-permute-start(bf16[504,512]{1,0:T(8,128)(2,1)} %get-tuple-element.19), channel_id=1, source_target_pairs={{0,160},{32,192},{64,224},{96,0},{128,32},{160,64},{192,96},{224,1... | collective-permute-start | bytes 1548296 | tf_op jit(solution)/shard_map/ppermute | solution.py:242
  65.1 65.9 %collective-permute-start.11 = (bf16[504,512]{1,0:T(8,128)(2,1)}, bf16[504,512]{1,0:T(8,128)(2,1)}, u32[]{:S(2)}, u32[]{:S(2)}) collective-permute-start(bf16[504,512]{1,0:T(8,128)(2,1)} %get-tuple-element.22), channel_id=1, source_target_pairs={{0,224},{32,0},{64,32},{96,64},{128,96},{160,128},{192,160},{224,1... | collective-permute-start | bytes 1548296 | tf_op jit(solution)/shard_map/ppermute | solution.py:242
  71.4 51.3 %copy-start.1 = (bf16[640,4096]{1,0:T(8,128)(2,1)}, bf16[640,4096]{1,0:T(8,128)(2,1)S(1)}, u32[]{:S(2)}) copy-start(bf16[640,4096]{1,0:T(8,128)(2,1)S(1)} %get-tuple-element.12.lhs_ref) | copy-start | bytes 15728644
  71.4 63.0 %collective-permute-start.15 = (bf16[504,512]{1,0:T(8,128)(2,1)}, bf16[504,512]{1,0:T(8,128)(2,1)S(1)}, u32[]{:S(2)}, u32[]{:S(2)}) collective-permute-start(bf16[504,512]{1,0:T(8,128)(2,1)} %get-tuple-element.18), channel_id=1, source_target_pairs={{0,64},{32,96},{64,128},{96,160},{128,192},{160,224},{192,0},{224,... | collective-permute-start | bytes 1548296 | tf_op jit(solution)/shard_map/ppermute | solution.py:242
  76.5 5.9 %copy-start.5 = (bf16[504,512]{1,0:T(8,128)(2,1)S(1)}, bf16[504,512]{1,0:T(8,128)(2,1)}, u32[]{:S(2)}) copy-start(bf16[504,512]{1,0:T(8,128)(2,1)} %get-tuple-element.17) | copy-start | bytes 1548292
  82.4 72.3 %collective-permute-start.16 = (bf16[504,512]{1,0:T(8,128)(2,1)S(1)}, bf16[504,512]{1,0:T(8,128)(2,1)S(1)}, u32[]{:S(2)}, u32[]{:S(2)}) collective-permute-start(bf16[504,512]{1,0:T(8,128)(2,1)S(1)} %copy-done.5), channel_id=1, source_target_pairs={{0,192},{32,224},{64,0},{96,32},{128,64},{160,96},{192,128},{224,1... | collective-permute-start | bytes 1548296 | tf_op jit(solution)/shard_map/ppermute | solution.py:242
  124.4 30.3 %slice-start = ((s8[5242880]{0:T(1024)(128)(4,1)}), s8[1048576]{0:T(1024)(128)(4,1)S(1)}, s32[]{:S(2)}) async-start(s8[5242880]{0:T(1024)(128)(4,1)} %bitcast.46), calls=%async_computation.5 | async-start | bytes 2097152
  127.3 27.4 %slice-start.1 = ((s8[5242880]{0:T(1024)(128)(4,1)}), s8[4194304]{0:T(1024)(128)(4,1)S(1)}, s32[]{:S(2)}) async-start(s8[5242880]{0:T(1024)(128)(4,1)} %bitcast.46), calls=%async_computation.6 | async-start | bytes 8388608
  157.0 1.9 collective-permute-start.17
  175.0 12.2 %all-to-all-start.2 = ((f32[8,16,384]{2,1,0:T(8,128)}), f32[8,16,384]{2,1,0:T(8,128)S(1)}, u32[]{:S(2)}, u32[]{:S(2)}) async-start(f32[8,16,384]{2,1,0:T(8,128)} %shard_map.112), calls=%async_computation.2 | async-start | bytes 393216 | tf_op jit(solution)/shard_map/all_to_all | solution.py:26
  188.2 14.1 %all-to-all-start.3 = ((bf16[32,16,128]{2,1,0:T(8,128)(2,1)}), bf16[32,16,128]{2,1,0:T(8,128)(2,1)S(1)}, u32[]{:S(2)}, u32[]{:S(2)}) async-start(bf16[32,16,128]{2,1,0:T(8,128)(2,1)} %shard_map.113), calls=%async_computation.3 | async-start | bytes 262144 | tf_op jit(solution)/shard_map/all_to_all | solution.py:26
  206.8 2.0 collective-permute-start.18

commit v3 on v2

--- a/solution.py
+++ b/solution.py
@@ -28,7 +28,7 @@
     )
 
 
-def norm_kernel(info, gain_ref, down_ref, hidden_proj_ref, *refs, width):
+def norm_kernel(info, valid_ref, gain_ref, down_ref, hidden_proj_ref, *refs, width):
     pieces, (lhs_ref, side_ref, own_ref) = refs[:-3], refs[-3:]
     xs, tokens, lane = pieces[0].shape
     rank = down_ref.shape[0]
@@ -72,7 +72,8 @@
     )
     side_ref[:, :rank] = unit_down
     side_ref[:, rank : 2 * rank] = hidden_side
-    side_ref[:, 2 * rank :] = jnp.broadcast_to(inverse, (mine, side_ref.shape[1] - 2 * rank))
+    side_ref[:, 2 * rank : 3 * rank] = jnp.broadcast_to(inverse, (mine, rank))
+    side_ref[:, 3 * rank :] = jnp.broadcast_to(valid_ref[...], (mine, rank)).astype(f32)
 
 
 def soft_kernel(
@@ -83,7 +84,7 @@
     columns, depth = last_ref.shape
     total = sums_ref[...]
     for n, ref in enumerate((first_ref, last_ref)):
-        at = pl.ds(pl.multiple_of(info[4 + n], depth), depth)
+        at = pl.ds(pl.multiple_of(info[6 + n], depth), depth)
         total += lax.dot_general(lhs_ref[:, at], ref[...], by_last, preferred_element_type=f32)
     logits_ref[...] = total
     fold = logits_ref[tokens : tokens + rank] + logits_ref[tokens + rank :]
@@ -91,7 +92,7 @@
     fold_low = (fold - fold_high.astype(f32)).astype(bf16)
     right = jnp.concatenate([vocab_ref[...], fold_high, fold_low, fold_low], axis=0)
     spot = lax.broadcasted_iota(jnp.int32, (1, columns), 1)
-    counted = spot >= info[1]
+    counted = spot >= info[4]
     count = 64
     lane = lax.broadcasted_iota(jnp.int32, (count, 2 * rank), 1)
     for first in range(0, tokens, count):
@@ -101,7 +102,7 @@
         grown = jnp.where(counted, jnp.exp(jnp.minimum(logits - peak, 0.0)), 0.0)
         total = jnp.sum(grown, axis=1, keepdims=True)
         rounded = grown.astype(bf16)
-        hit = counted & (label_ref[rows] == spot + info[0])
+        hit = counted & (label_ref[rows] == spot + info[3])
         dot_all = jnp.sum(rounded.astype(f32) * logits, axis=1, keepdims=True)
         dot_hit = jnp.sum(jnp.where(hit, logits, 0.0), axis=1, keepdims=True)
         rows_ref[rows] = rounded
@@ -109,7 +110,7 @@
         stats = jnp.where(lane == 0, peak, jnp.where(lane == 1, total, jnp.where(lane == 2, dot_all, dot_hit)))
         stats_ref[rows] = jnp.where(lane < 4, stats, 0.0)
     here = ffn_ref.shape[0]
-    own = pl.ds(pl.multiple_of(info[2], here), here)
+    own = pl.ds(pl.multiple_of(info[5], here), here)
     lane = lax.broadcasted_iota(jnp.int32, (here, 2 * rank), 1)
     stats_ref[own] = jnp.where(lane < rank, stats_ref[own], ffn_ref[...])
     both = lax.dot_general(rows_ref[...], right, by_last, preferred_element_type=f32)
@@ -119,7 +120,7 @@
     mine = keep_ref.shape[1]
     for core in range(2):
 
-        @pl.when(info[3] == core)
+        @pl.when(info[1] == core)
         def _():
             for pair in range(keep_ref.shape[0]):
                 for ref, place in ((keep_ref, 2 * pair + core), (send_ref, 2 * pair + 1 - core)):
@@ -159,13 +160,13 @@
         out_ref[copy, :, 256:] = kept
 
 
-def last_merge_kernel(x_ref, side_ref, valid_ref, out_ref, *, width):
+def last_merge_kernel(x_ref, side_ref, out_ref, *, width):
     soft, mark, kept = merged(x_ref[...])
     total, dot_all, dot_hit = kept[:, 1:2], kept[:, 2:3], kept[:, 3:4]
     both = soft / total - mark
     label_dot = dot_all / total - dot_hit
     rank = both.shape[1] // 2
-    inverse, valid = side_ref[:, 2 * rank : 2 * rank + 1], valid_ref[...] > 0
+    inverse, valid = side_ref[:, 2 * rank : 2 * rank + 1], side_ref[:, 3 * rank : 3 * rank + 1] > 0.0
     down_side = inverse * (both[:, rank:] - (label_dot / width) * side_ref[:, :rank])
     head_side = jnp.where(valid, both[:, :rank], 0.0)
     down_side = jnp.where(valid, down_side, 0.0)
@@ -189,7 +190,7 @@
     sides = jnp.concatenate(sides, axis=0)
     features = out_ref.shape[1]
     column = lax.broadcasted_iota(jnp.int32, (2 * rank, features), 0)
-    wanted = rank + info[0] + lax.broadcasted_iota(jnp.int32, (2 * rank, features), 1) // rank
+    wanted = rank + info[8] + lax.broadcasted_iota(jnp.int32, (2 * rank, features), 1) // rank
     chosen = (column == wanted).astype(f32).astype(bf16)
     left = jnp.dot(sides, chosen, preferred_element_type=f32)
     right = sides[:, :rank].astype(f32)
@@ -262,6 +263,18 @@
 
     mine = tokens // lanes
     of_one_core = [[2 * i + core for i in range(lanes // 2)] for core in range(2)]
+    ints = ints.astype(jnp.int32).reshape(groups, 2 * part)
+    all_labels = ints[:, :here] + 128 * ints[:, here : 2 * here] + 16384 * ints[:, 2 * here : 3 * here]
+    all_labels = all_labels.reshape(tokens, 1)
+    all_lengths = ints[:, 3 * here : 3 * here + lengths.shape[0]].reshape(-1)
+    spot = j * mine + lax.broadcasted_iota(jnp.int32, (mine, 1), 0)
+    own_length = lax.dynamic_slice_in_dim(all_lengths, j * (mine // seq_span), mine // seq_span, 0)
+    valid = (spot % seq_span < jnp.repeat(own_length, seq_span)[:, None]).astype(jnp.int32)
+    shifts = (0, *early_shifts, *late_shifts)
+    per = store.shape[1] // rank
+    info = [y_at, core_at, j * mine, j * vocab_owned + start, skipped, z * here]
+    info += [((z - s) % groups) * rows_owned for s in shifts[-2:]]
+    info = jnp.stack([*info, j % (lanes // 2) * per]).astype(jnp.int32)
     in_smem = pl.BlockSpec(memory_space=pltpu.SMEM)
     in_vmem = pl.BlockSpec(memory_space=pltpu.VMEM)
     lhs, side = pl.pallas_call(
@@ -270,38 +283,28 @@
             jax.ShapeDtypeStruct((tokens + 2 * rank, width), bf16),
             jax.ShapeDtypeStruct((mine, 4 * rank), f32),
         ),
-        in_specs=[in_smem, *vmem(3 + len(pieces))],
+        in_specs=[in_smem, *vmem(4 + len(pieces))],
         out_specs=(in_vmem, in_vmem),
         scratch_shapes=[pltpu.VMEM((mine, width), bf16)],
         compiler_params=small,
     )(
-        jnp.stack([y_at, core_at, j * mine]).astype(jnp.int32),
+        info,
+        valid,
         norm_gain[None, :],
         proj_down.T,
         proj_hidden.T,
         *pieces,
     )
 
-    ints = ints.astype(jnp.int32).reshape(groups, 2 * part)
-    all_labels = ints[:, :here] + 128 * ints[:, here : 2 * here] + 16384 * ints[:, 2 * here : 3 * here]
-    all_labels = all_labels.reshape(tokens, 1)
-    all_lengths = ints[:, 3 * here : 3 * here + lengths.shape[0]].reshape(-1)
-    spot = j * mine + lax.broadcasted_iota(jnp.int32, (mine, 1), 0)
-    own_length = lax.dynamic_slice_in_dim(all_lengths, j * (mine // seq_span), mine // seq_span, 0)
-    valid = (spot % seq_span < jnp.repeat(own_length, seq_span)[:, None]).astype(jnp.int32)
     ffn = jnp.dot(ffn_act, proj_ffn, preferred_element_type=f32)
     ffn = jnp.concatenate([jnp.zeros_like(ffn), ffn], axis=1)
     vocab_turned = lax.dynamic_slice_in_dim(proj_vocab, start, block, 0).T
 
     sums = None
-    shifts = (0, *early_shifts, *late_shifts)
     for s in shifts[:-2]:
         depth = lax.dynamic_slice_in_dim(lhs, ((z - s) % groups) * rows_owned, rows_owned, 1)
         term = lax.dot_general(depth, came[s], by_last, preferred_element_type=f32)
         sums = term if sums is None else sums + term
-    last = shifts[-2:]
-    info = [j * vocab_owned + start, skipped, z * here, core_at]
-    info = jnp.stack([*info, *(((z - s) % groups) * rows_owned for s in last)]).astype(jnp.int32)
     by_core = (lanes // 2, mine, 6 * rank)
     keep, send = pl.pallas_call(
         soft_kernel,
@@ -314,7 +317,7 @@
             pltpu.VMEM((tokens, 2 * rank), f32),
         ],
         compiler_params=small,
-    )(info, sums, lhs, came[last[0]], came[last[1]], vocab_turned, all_labels, ffn)
+    )(info, sums, lhs, came[shifts[-2]], came[shifts[-1]], vocab_turned, all_labels, ffn)
     packed = pl.pallas_call(
         pair_merge_kernel,
         out_shape=jax.ShapeDtypeStruct(by_core, f32),
@@ -334,22 +337,21 @@
     sides = pl.pallas_call(
         lambda *refs: last_merge_kernel(*refs, width=width),
         out_shape=jax.ShapeDtypeStruct((lanes, mine, 2 * rank), bf16),
-        in_specs=vmem(3),
+        in_specs=vmem(2),
         out_specs=in_vmem,
         compiler_params=small,
-    )(packed, side, valid)
+    )(packed, side)
     sides = traded(sides, "tp").reshape(tokens, 2 * rank)
 
     stored, features = store.shape
     queries = tokens // seq_span
-    per = features // rank
     query = pl.pallas_call(
         lambda *refs: query_kernel(*refs, span=seq_span, each=queries // lanes),
         out_shape=jax.ShapeDtypeStruct((queries, features), bf16),
         in_specs=[in_smem, *vmem(1)],
         out_specs=in_vmem,
         compiler_params=small,
-    )(jnp.stack([j % (lanes // 2) * per, core_at]).astype(jnp.int32), sides)
+    )(info, sides)
     partial = lax.dot_general(query, store, by_last, preferred_element_type=f32)
     half = queries // 2
     other = moved(partial[half:].astype(bf16), lambda i: i ^ 1)

time: 225 us -> 221 us (0.982)
  blocking collectives: 28.7 us -> 54.2 us
  waiting for transfers between devices: 88.3 us -> 72.4 us
  starting transfers between devices: 65.1 us -> 55.3 us
    all_to_all x2 -> x4, blocking collectives: 28.7 us -> 54.2 us  [traded(): lax.all_to_all(value, axis, split_axis=0, concat_axis=0, tiled=True, axis...]
    all_to_all x3 -> x1, waiting for transfers between devices: 24 us -> 8.23 us  [traded(): lax.all_to_all(value, axis, split_axis=0, concat_axis=0, tiled=True, axis...]
    all_to_all x3 -> x1, starting transfers between devices: 18.8 us -> 9 us  [traded(): lax.all_to_all(value, axis, split_axis=0, concat_axis=0, tiled=True, axis...]
  transfers between devices with their start and end apart: 22 -> 20, of which waited for: 12 -> 10; matrix products, arithmetic and copies ran while one was open for 10% -> 10% of each run, Pallas kernels for 2% -> 2%
where the time goes in v3:
time: 221 us; the launch traced here: 220 us
  waiting for transfers between devices  72.4 us (33%)
  starting transfers between devices  55.3 us (25%)
  blocking collectives  54.2 us (25%)
  matrix products  14.3 us (6%)
  local copies, waits for them, and re-layouts  11.9 us (5%)
  Pallas kernels  9.09 us (4%)
  other arithmetic  2.76 us (1%)
    ppermute x7, waiting for transfers between devices, head_moves(): lax.ppermute(cut, 'grp', [(i, (i + s) % groups) for i in range(groups)])  54.9 us
    all_to_all x4, blocking collectives, traded(): lax.all_to_all(value, axis, split_axis=0, concat_axis=0, tiled=True, axis...  54.2 us
    ppermute x12, starting transfers between devices, moved(): return lax.ppermute(value, 'tp', [(i, move(i)) for i in range(lanes)])  26.1 us
    ppermute x7, starting transfers between devices, head_moves(): lax.ppermute(cut, 'grp', [(i, (i + s) % groups) for i in range(groups)])  20.1 us
    dot_general x6, matrix products, per_device(): term = lax.dot_general(depth, came[s], by_last, preferred_element_type=f32)  12.8 us
    ppermute x12, waiting for transfers between devices, moved(): return lax.ppermute(value, 'tp', [(i, move(i)) for i in range(lanes)])  9.3 us
    all_to_all x1, starting transfers between devices, traded(): lax.all_to_all(value, axis, split_axis=0, concat_axis=0, tiled=True, axis...  9 us
    all_to_all x1, waiting for transfers between devices, traded(): lax.all_to_all(value, axis, split_axis=0, concat_axis=0, tiled=True, axis...  8.23 us
  transfers between devices with their start and end apart: 20, of which 10 were waited for; matrix products, arithmetic and copies ran while one was open for 10% of the time, Pallas kernels for 2%

profile of v3, /device:TPU:1, one launch (start us, length us, event | category | flops | bytes accessed | tf_op | source)
XLA Modules:
  0.0 220.2 jit_solution(17056789177339253256)
XLA Ops:
  2.9 9.0 %all-to-all-start = ((bf16[8,80,128]{2,1,0:T(8,128)(2,1)}), bf16[8,80,128]{2,1,0:T(8,128)(2,1)S(1)}, u32[]{:S(2)}, u32[]{:S(2)}) async-start(bf16[8,80,128]{2,1,0:T(8,128)(2,1)} %broadcast_in_dim.26), calls=%async_computation | async-start | bytes 327680 | tf_op jit(solution)/shard_map/all_to_all | solution.py:26
  11.9 8.2 %all-to-all-done = bf16[8,80,128]{2,1,0:T(8,128)(2,1)S(1)} async-done(((bf16[8,80,128]{2,1,0:T(8,128)(2,1)}), bf16[8,80,128]{2,1,0:T(8,128)(2,1)S(1)}, u32[]{:S(2)}, u32[]{:S(2)}) %all-to-all-start) | async-done | bytes 163872 | tf_op jit(solution)/shard_map/all_to_all | solution.py:26
  21.5 2.4 %dynamic-slice_bitcast_fusion = (bf16[504,512]{1,0:T(8,128)(2,1)}, bf16[504,512]{1,0:T(8,128)(2,1)}) fusion(bf16[512,4008]{0,1:T(8,128)(2,1)} %param.13, s32[]{:T(128)S(6)} %select_n.224, s32[]{:T(128)S(6)} %select_n.220), kind=kLoop, calls=%fused_computation.19 | loop fusion | bytes 2064392 | tf_op jit(solution)/shard_map/dynamic_slice | solution.py:242
  24.4 2.5 %collective-permute-start.1 = (bf16[512,128]{1,0:T(8,128)(2,1)S(1)}, bf16[512,128]{1,0:T(8,128)(2,1)S(1)}, u32[]{:S(2)}, u32[]{:S(2)}) collective-permute-start(bf16[512,128]{1,0:T(8,128)(2,1)S(1)} %bitcast.55), channel_id=1, source_target_pairs={{0,4},{1,5},{2,6},{3,7},{4,0},{5,1},{6,2},{7,3},{8,12},{9,13},{10,... | collective-permute-start | bytes 393224 | tf_op jit(solution)/shard_map/ppermute | solution.py:255
  28.2 2.4 %collective-permute-done.1 = bf16[512,128]{1,0:T(8,128)(2,1)S(1)} collective-permute-done((bf16[512,128]{1,0:T(8,128)(2,1)S(1)}, bf16[512,128]{1,0:T(8,128)(2,1)S(1)}, u32[]{:S(2)}, u32[]{:S(2)}) %collective-permute-start.1) | collective-permute-done | bytes 131104 | tf_op jit(solution)/shard_map/ppermute | solution.py:255
  32.1 2.6 %collective-permute-start.4 = (bf16[4,512,128]{2,1,0:T(8,128)(2,1)S(1)}, bf16[4,512,128]{2,1,0:T(8,128)(2,1)S(1)}, u32[]{:S(2)}, u32[]{:S(2)}) collective-permute-start(bf16[4,512,128]{2,1,0:T(8,128)(2,1)S(1)} %bitcast_dynamic-update-slice_fusion.refs_5_), channel_id=1, source_target_pairs={{0,16},{1,17},{2,18},{3,19},{4,20},{5,21},{6,22},{7,23},{8,24},{9,... | collective-permute-start | bytes 1572872 | tf_op jit(solution)/shard_map/ppermute | solution.py:255
  36.3 3.6 %constant_dynamic-slice_fusion = (bf16[504,512]{1,0:T(8,128)(2,1)}, bf16[504,512]{1,0:T(8,128)(2,1)}, bf16[504,512]{1,0:T(8,128)(2,1)}, bf16[504,512]{1,0:T(8,128)(2,1)}, bf16[504,512]{1,0:T(8,128)(2,1)}) fusion(bf16[4008,512]{1,0:T(8,128)(2,1)} %bitcast.52, s32[]{:T(128)S(6)} %select_n.240, s32[]{:T(128)S(6)} %select_n.238, s32[]{:T(128)S(6)} %select_n.236, ...), kind=kLoop, calls=%fused_computation.35 | loop fusion | bytes 5160980 | tf_op jit(solution)/shard_map/dynamic_slice | solution.py:242
  39.9 5.0 %collective-permute-start.6 = (bf16[4,512,128]{2,1,0:T(8,128)(2,1)S(1)}, bf16[4,512,128]{2,1,0:T(8,128)(2,1)}, u32[]{:S(2)}, u32[]{:S(2)}) collective-permute-start(bf16[4,512,128]{2,1,0:T(8,128)(2,1)S(1)} %bitcast_dynamic-update-slice_fusion.refs_5_), channel_id=1, source_target_pairs={{0,1},{1,0},{2,3},{3,2},{4,5},{5,4},{6,7},{7,6},{8,9},{9,8},{10,11... | collective-permute-start | bytes 1572872 | tf_op jit(solution)/shard_map/ppermute | solution.py:255
  44.9 5.0 %collective-permute-start.7 = (bf16[4,512,128]{2,1,0:T(8,128)(2,1)S(1)}, bf16[4,512,128]{2,1,0:T(8,128)(2,1)}, u32[]{:S(2)}, u32[]{:S(2)}) collective-permute-start(bf16[4,512,128]{2,1,0:T(8,128)(2,1)S(1)} %collective-permute-done.3.refs_6_), channel_id=1, source_target_pairs={{0,1},{1,0},{2,3},{3,2},{4,5},{5,4},{6,7},{7,6},{8,9},{9,8},{10,11... | collective-permute-start | bytes 1572872 | tf_op jit(solution)/shard_map/ppermute | solution.py:255
  49.9 3.9 %collective-permute-done.4.refs_7_ = bf16[4,512,128]{2,1,0:T(8,128)(2,1)S(1)} collective-permute-done((bf16[4,512,128]{2,1,0:T(8,128)(2,1)S(1)}, bf16[4,512,128]{2,1,0:T(8,128)(2,1)S(1)}, u32[]{:S(2)}, u32[]{:S(2)}) %collective-permute-start.4) | collective-permute-done | bytes 524320 | tf_op jit(solution)/shard_map/ppermute | solution.py:255
  53.8 5.1 %collective-permute-start.8 = (bf16[4,512,128]{2,1,0:T(8,128)(2,1)S(1)}, bf16[4,512,128]{2,1,0:T(8,128)(2,1)}, u32[]{:S(2)}, u32[]{:S(2)}) collective-permute-start(bf16[4,512,128]{2,1,0:T(8,128)(2,1)S(1)} %collective-permute-done.4.refs_7_), channel_id=1, source_target_pairs={{0,1},{1,0},{2,3},{3,2},{4,5},{5,4},{6,7},{7,6},{8,9},{9,8},{10,11... | collective-permute-start | bytes 1572872 | tf_op jit(solution)/shard_map/ppermute | solution.py:255
  61.1 4.2 %collective-permute-start.13 = (bf16[504,512]{1,0:T(8,128)(2,1)}, bf16[504,512]{1,0:T(8,128)(2,1)S(1)}, u32[]{:S(2)}, u32[]{:S(2)}) collective-permute-start(bf16[504,512]{1,0:T(8,128)(2,1)} %get-tuple-element.20), channel_id=1, source_target_pairs={{0,96},{32,128},{64,160},{96,192},{128,224},{160,0},{192,32},{224,... | collective-permute-start | bytes 1548296 | tf_op jit(solution)/shard_map/ppermute | solution.py:243
  66.6 5.3 %shard_map.109 = (bf16[640,4096]{1,0:T(8,128)(2,1)S(1)}, f32[16,256]{1,0:T(8,128)S(1)}) custom-call(s32[9]{0:T(128)S(1)} %stack.39.refs_0_.info, s32[16,1]{1,0:T(8,128)S(1)} %convert_element_type.17.refs_1_, f32[1,4096]{1,0:T(1,128)S(1)} %bitcast.51, bf16[64,4096]{1,0:T(8,128)(2,1)S(1)} %bitcast.49, bf16[64,4096]{1,0:T(8,128)(2,1)S(1)} %bitcast.50, ...), custom_call_target="tpu_custom_call" | custom-call | tf_op jit(solution)/shard_map/pallas_call | solution.py:280
  71.9 3.5 %collective-permute-start.15 = (bf16[504,512]{1,0:T(8,128)(2,1)}, bf16[504,512]{1,0:T(8,128)(2,1)S(1)}, u32[]{:S(2)}, u32[]{:S(2)}) collective-permute-start(bf16[504,512]{1,0:T(8,128)(2,1)} %get-tuple-element.18), channel_id=1, source_target_pairs={{0,64},{32,96},{64,128},{96,160},{128,192},{160,224},{192,0},{224,... | collective-permute-start | bytes 1548296 | tf_op jit(solution)/shard_map/ppermute | solution.py:243
  75.4 1.6 fusion.11
  77.0 2.8 %convolution_add_fusion.1 = f32[640,504]{0,1:T(8,128)} fusion(f32[640,504]{0,1:T(8,128)S(1)} %fusion.11, bf16[640,4096]{1,0:T(8,128)(2,1)S(1)} %get-tuple-element.12.lhs_ref, s32[]{:T(128)S(6)} %select_n.215, bf16[4008,512]{1,0:T(8,128)(2,1)} %bitcast.53, s32[]{:T(128)S(6)} %select_n.216), kind=kOutput, calls=%fused_computation.4 | convolution fusion | flops 330624000 | bytes 3751944 | tf_op jit(solution)/shard_map/dot_general | solution.py:306
  79.8 3.1 %collective-permute-done.12 = bf16[504,512]{1,0:T(8,128)(2,1)S(1)} collective-permute-done((bf16[504,512]{1,0:T(8,128)(2,1)}, bf16[504,512]{1,0:T(8,128)(2,1)S(1)}, u32[]{:S(2)}, u32[]{:S(2)}) %collective-permute-start.12) | collective-permute-done | bytes 516128 | tf_op jit(solution)/shard_map/ppermute | solution.py:243
  82.8 9.2 %collective-permute-start.16 = (bf16[504,512]{1,0:T(8,128)(2,1)S(1)}, bf16[504,512]{1,0:T(8,128)(2,1)S(1)}, u32[]{:S(2)}, u32[]{:S(2)}) collective-permute-start(bf16[504,512]{1,0:T(8,128)(2,1)S(1)} %copy-done.6), channel_id=1, source_target_pairs={{0,192},{32,224},{64,0},{96,32},{128,64},{160,96},{192,128},{224,1... | collective-permute-start | bytes 1548296 | tf_op jit(solution)/shard_map/ppermute | solution.py:243
  92.0 1.6 fusion.8
  93.6 27.9 %collective-permute-done.13 = bf16[504,512]{1,0:T(8,128)(2,1)S(1)} collective-permute-done((bf16[504,512]{1,0:T(8,128)(2,1)}, bf16[504,512]{1,0:T(8,128)(2,1)S(1)}, u32[]{:S(2)}, u32[]{:S(2)}) %collective-permute-start.13) | collective-permute-done | bytes 516128 | tf_op jit(solution)/shard_map/ppermute | solution.py:243
  121.6 1.6 fusion.6
  123.2 1.7 fusion.4
  124.9 2.9 %copy.28 = f32[640,504]{1,0:T(8,128)} copy(f32[640,504]{0,1:T(8,128)} %convolution_add_fusion.1) | data formatting | bytes 2580480 | tf_op jit(solution)/shard_map/add | solution.py:307
  127.8 3.7 %collective-permute-done.11 = bf16[504,512]{1,0:T(8,128)(2,1)} collective-permute-done((bf16[504,512]{1,0:T(8,128)(2,1)}, bf16[504,512]{1,0:T(8,128)(2,1)}, u32[]{:S(2)}, u32[]{:S(2)}) %collective-permute-start.11) | collective-permute-done | bytes 516128 | tf_op jit(solution)/shard_map/ppermute | solution.py:243
  131.4 3.5 %fusion.2.sums_ref = f32[640,504]{1,0:T(8,128)S(1)} fusion(f32[640,504]{1,0:T(8,128)} %fusion.4, f32[640,504]{1,0:T(8,128)} %fusion.6, f32[640,504]{1,0:T(8,128)} %fusion.8, f32[640,504]{1,0:T(8,128)} %copy.28, bf16[504,512]{1,0:T(8,128)(2,1)} %collective-permute-done.11, bf16[640,4096]{1,0:T(8,128)(2,1)} %copy-done.1, s32[]{:T(128)S(6)} %select_n.222), kind=kOutput, calls=%fused_computation.3 | convolution fusion | flops 331591680 | bytes 7704580 | tf_op jit(solution)/shard_map/dot_general | solution.py:306
  134.9 20.3 %collective-permute-done.16.last_ref = bf16[504,512]{1,0:T(8,128)(2,1)S(1)} collective-permute-done((bf16[504,512]{1,0:T(8,128)(2,1)S(1)}, bf16[504,512]{1,0:T(8,128)(2,1)S(1)}, u32[]{:S(2)}, u32[]{:S(2)}) %collective-permute-start.16) | collective-permute-done | bytes 516128 | tf_op jit(solution)/shard_map/ppermute | solution.py:243
  155.2 2.3 %shard_map.110 = (f32[16,16,384]{2,1,0:T(8,128)S(1)}, f32[16,16,384]{2,1,0:T(8,128)S(1)}) custom-call(s32[9]{0:T(128)S(1)} %stack.39.refs_0_.info, f32[640,504]{1,0:T(8,128)S(1)} %fusion.2.sums_ref, bf16[640,4096]{1,0:T(8,128)(2,1)S(1)} %bitcast.47, bf16[504,512]{1,0:T(8,128)(2,1)S(1)} %collective-permute-done.15.first_ref, ...), custom_call_target="tpu_custom_call" | custom-call | tf_op jit(solution)/shard_map/pallas_call | solution.py:309
  159.6 15.1 %all_to_all.25.x_ref = f32[16,16,384]{2,1,0:T(8,128)S(1)} all-to-all(f32[16,16,384]{2,1,0:T(8,128)S(1)} %shard_map.111), channel_id=1, replica_groups={{0,2,4,6,8,10,12,14,16,18,20,22,24,26,28,30},{1,3,5,7,9,11,13,15,17,19,..., dimensions={0} | all-to-all | bytes 786432 | tf_op jit(solution)/shard_map/all_to_all | solution.py:26
  174.8 12.0 %all_to_all.26.refs_0_ = f32[8,16,384]{2,1,0:T(8,128)S(1)} all-to-all(f32[8,16,384]{2,1,0:T(8,128)S(1)} %shard_map.112), channel_id=1, replica_groups=mesh['grp'=8,'tp'=32] {'grp'}, dimensions={0} | all-to-all | bytes 393216 | tf_op jit(solution)/shard_map/all_to_all | solution.py:26
  187.2 13.5 %all_to_all.27 = bf16[32,16,128]{2,1,0:T(8,128)(2,1)S(1)} all-to-all(bf16[32,16,128]{2,1,0:T(8,128)(2,1)S(1)} %shard_map.113), channel_id=1, replica_groups=mesh['grp'=8,'tp'=32] {'tp'}, dimensions={0} | all-to-all | bytes 262144 | tf_op jit(solution)/shard_map/all_to_all | solution.py:26
  203.5 1.5 collective-permute-done.18
  205.5 13.6 %all_to_all.28 = bf16[16,2,8192]{2,1,0:T(2,128)(2,1)S(1)} all-to-all(bf16[16,2,8192]{2,1,0:T(2,128)(2,1)S(1)} %reshape.95), channel_id=1, replica_groups={{0,2,4,6,8,10,12,14,16,18,20,22,24,26,28,30},{1,3,5,7,9,11,13,15,17,19,..., dimensions={0} | all-to-all | bytes 1048576 | tf_op jit(solution)/shard_map/all_to_all | solution.py:26
  (83 shorter events, 19.6 us)
Async XLA Ops:
  0.0 36.1 %copy-start = (bf16[4008,64]{0,1:T(8,128)(2,1)S(1)}, bf16[4008,64]{0,1:T(8,128)(2,1)}, u32[]{:S(2)}) copy-start(bf16[4008,64]{0,1:T(8,128)(2,1)} %param.18) | copy-start | bytes 1539076
  2.9 17.2 %all-to-all-start = ((bf16[8,80,128]{2,1,0:T(8,128)(2,1)}), bf16[8,80,128]{2,1,0:T(8,128)(2,1)S(1)}, u32[]{:S(2)}, u32[]{:S(2)}) async-start(bf16[8,80,128]{2,1,0:T(8,128)(2,1)} %broadcast_in_dim.26), calls=%async_computation | async-start | bytes 327680 | tf_op jit(solution)/shard_map/all_to_all | solution.py:26
  20.1 15.7 %copy-start.7 = (bf16[64,448]{1,0:T(8,128)(2,1)S(1)}, bf16[64,448]{1,0:T(8,128)(2,1)}, u32[]{:S(2)}) copy-start(bf16[64,448]{1,0:T(8,128)(2,1)} %param.14) | copy-start | bytes 172036
  20.2 15.7 %copy-start.8 = (bf16[448,64]{0,1:T(8,128)(2,1)S(1)}, bf16[448,64]{0,1:T(8,128)(2,1)}, u32[]{:S(2)}) copy-start(bf16[448,64]{0,1:T(8,128)(2,1)} %param.19) | copy-start | bytes 172036
  20.2 8.0 %collective-permute-start = (bf16[512,128]{1,0:T(8,128)(2,1)S(1)}, bf16[512,128]{1,0:T(8,128)(2,1)S(1)}, u32[]{:S(2)}, u32[]{:S(2)}) collective-permute-start(bf16[512,128]{1,0:T(8,128)(2,1)S(1)} %bitcast.54), channel_id=1, source_target_pairs={{0,2},{1,3},{2,4},{3,5},{4,6},{5,7},{6,0},{7,1},{8,10},{9,11},{10,... | collective-permute-start | bytes 393224 | tf_op jit(solution)/shard_map/ppermute | solution.py:255
  23.9 48.0 %collective-permute-start.10 = (bf16[504,512]{1,0:T(8,128)(2,1)}, bf16[504,512]{1,0:T(8,128)(2,1)}, u32[]{:S(2)}, u32[]{:S(2)}) collective-permute-start(bf16[504,512]{1,0:T(8,128)(2,1)} %get-tuple-element.23), channel_id=1, source_target_pairs={{0,32},{32,64},{64,96},{96,128},{128,160},{160,192},{192,224},{224... | collective-permute-start | bytes 1548296 | tf_op jit(solution)/shard_map/ppermute | solution.py:243
  24.4 6.2 %collective-permute-start.1 = (bf16[512,128]{1,0:T(8,128)(2,1)S(1)}, bf16[512,128]{1,0:T(8,128)(2,1)S(1)}, u32[]{:S(2)}, u32[]{:S(2)}) collective-permute-start(bf16[512,128]{1,0:T(8,128)(2,1)S(1)} %bitcast.55), channel_id=1, source_target_pairs={{0,4},{1,5},{2,6},{3,7},{4,0},{5,1},{6,2},{7,3},{8,12},{9,13},{10,... | collective-permute-start | bytes 393224 | tf_op jit(solution)/shard_map/ppermute | solution.py:255
  26.9 3.8 %collective-permute-start.2 = (bf16[512,128]{1,0:T(8,128)(2,1)S(1)}, bf16[512,128]{1,0:T(8,128)(2,1)S(1)}, u32[]{:S(2)}, u32[]{:S(2)}) collective-permute-start(bf16[512,128]{1,0:T(8,128)(2,1)S(1)} %bitcast.56), channel_id=1, source_target_pairs={{0,6},{1,7},{2,0},{3,1},{4,2},{5,3},{6,4},{7,5},{8,14},{9,15},{10,... | collective-permute-start | bytes 393224 | tf_op jit(solution)/shard_map/ppermute | solution.py:255
  30.7 14.2 %collective-permute-start.3 = (bf16[4,512,128]{2,1,0:T(8,128)(2,1)S(1)}, bf16[4,512,128]{2,1,0:T(8,128)(2,1)S(1)}, u32[]{:S(2)}, u32[]{:S(2)}) collective-permute-start(bf16[4,512,128]{2,1,0:T(8,128)(2,1)S(1)} %bitcast_dynamic-update-slice_fusion.refs_5_), channel_id=1, source_target_pairs={{0,8},{1,9},{2,10},{3,11},{4,12},{5,13},{6,14},{7,15},{8,16},{9,17... | collective-permute-start | bytes 1572872 | tf_op jit(solution)/shard_map/ppermute | solution.py:255
  32.1 21.7 %collective-permute-start.4 = (bf16[4,512,128]{2,1,0:T(8,128)(2,1)S(1)}, bf16[4,512,128]{2,1,0:T(8,128)(2,1)S(1)}, u32[]{:S(2)}, u32[]{:S(2)}) collective-permute-start(bf16[4,512,128]{2,1,0:T(8,128)(2,1)S(1)} %bitcast_dynamic-update-slice_fusion.refs_5_), channel_id=1, source_target_pairs={{0,16},{1,17},{2,18},{3,19},{4,20},{5,21},{6,22},{7,23},{8,24},{9,... | collective-permute-start | bytes 1572872 | tf_op jit(solution)/shard_map/ppermute | solution.py:255
  34.7 24.1 %collective-permute-start.5 = (bf16[4,512,128]{2,1,0:T(8,128)(2,1)S(1)}, bf16[4,512,128]{2,1,0:T(8,128)(2,1)}, u32[]{:S(2)}, u32[]{:S(2)}) collective-permute-start(bf16[4,512,128]{2,1,0:T(8,128)(2,1)S(1)} %bitcast_dynamic-update-slice_fusion.refs_5_), channel_id=1, source_target_pairs={{0,24},{1,25},{2,26},{3,27},{4,28},{5,29},{6,30},{7,31},{8,0},{9,1... | collective-permute-start | bytes 1572872 | tf_op jit(solution)/shard_map/ppermute | solution.py:255
  36.2 30.4 %copy-start.2 = (bf16[4096,64]{0,1:T(8,128)(2,1)S(1)}, bf16[4096,64]{0,1:T(8,128)(2,1)}, u32[]{:S(2)}) copy-start(bf16[4096,64]{0,1:T(8,128)(2,1)} %param.20) | copy-start | bytes 1572868
  36.3 30.4 %copy-start.3 = (bf16[4096,64]{0,1:T(8,128)(2,1)S(1)}, bf16[4096,64]{0,1:T(8,128)(2,1)}, u32[]{:S(2)}) copy-start(bf16[4096,64]{0,1:T(8,128)(2,1)} %param.17) | copy-start | bytes 1572868
  36.3 30.3 %copy-start.4 = (f32[4096]{0:T(1024)S(1)}, f32[4096]{0:T(1024)}, u32[]{:S(2)}) copy-start(f32[4096]{0:T(1024)} %param.12) | copy-start | bytes 49156
  39.9 19.8 %collective-permute-start.6 = (bf16[4,512,128]{2,1,0:T(8,128)(2,1)S(1)}, bf16[4,512,128]{2,1,0:T(8,128)(2,1)}, u32[]{:S(2)}, u32[]{:S(2)}) collective-permute-start(bf16[4,512,128]{2,1,0:T(8,128)(2,1)S(1)} %bitcast_dynamic-update-slice_fusion.refs_5_), channel_id=1, source_target_pairs={{0,1},{1,0},{2,3},{3,2},{4,5},{5,4},{6,7},{7,6},{8,9},{9,8},{10,11... | collective-permute-start | bytes 1572872 | tf_op jit(solution)/shard_map/ppermute | solution.py:255
  44.9 16.2 %collective-permute-start.7 = (bf16[4,512,128]{2,1,0:T(8,128)(2,1)S(1)}, bf16[4,512,128]{2,1,0:T(8,128)(2,1)}, u32[]{:S(2)}, u32[]{:S(2)}) collective-permute-start(bf16[4,512,128]{2,1,0:T(8,128)(2,1)S(1)} %collective-permute-done.3.refs_6_), channel_id=1, source_target_pairs={{0,1},{1,0},{2,3},{3,2},{4,5},{5,4},{6,7},{7,6},{8,9},{9,8},{10,11... | collective-permute-start | bytes 1572872 | tf_op jit(solution)/shard_map/ppermute | solution.py:255
  53.8 11.5 %collective-permute-start.8 = (bf16[4,512,128]{2,1,0:T(8,128)(2,1)S(1)}, bf16[4,512,128]{2,1,0:T(8,128)(2,1)}, u32[]{:S(2)}, u32[]{:S(2)}) collective-permute-start(bf16[4,512,128]{2,1,0:T(8,128)(2,1)S(1)} %collective-permute-done.4.refs_7_), channel_id=1, source_target_pairs={{0,1},{1,0},{2,3},{3,2},{4,5},{5,4},{6,7},{7,6},{8,9},{9,8},{10,11... | collective-permute-start | bytes 1572872 | tf_op jit(solution)/shard_map/ppermute | solution.py:255
  58.9 6.7 %collective-permute-start.9 = (bf16[4,512,128]{2,1,0:T(8,128)(2,1)}, bf16[4,512,128]{2,1,0:T(8,128)(2,1)}, u32[]{:S(2)}, u32[]{:S(2)}) collective-permute-start(bf16[4,512,128]{2,1,0:T(8,128)(2,1)} %collective-permute-done.5.refs_8_), channel_id=1, source_target_pairs={{0,1},{1,0},{2,3},{3,2},{4,5},{5,4},{6,7},{7,6},{8,9},{9,8},{10,11... | collective-permute-start | bytes 1572872 | tf_op jit(solution)/shard_map/ppermute | solution.py:255
  59.7 23.2 %collective-permute-start.12 = (bf16[504,512]{1,0:T(8,128)(2,1)}, bf16[504,512]{1,0:T(8,128)(2,1)S(1)}, u32[]{:S(2)}, u32[]{:S(2)}) collective-permute-start(bf16[504,512]{1,0:T(8,128)(2,1)} %get-tuple-element.21), channel_id=1, source_target_pairs={{0,128},{32,160},{64,192},{96,224},{128,0},{160,32},{192,64},{224,... | collective-permute-start | bytes 1548296 | tf_op jit(solution)/shard_map/ppermute | solution.py:243
  61.1 60.5 %collective-permute-start.13 = (bf16[504,512]{1,0:T(8,128)(2,1)}, bf16[504,512]{1,0:T(8,128)(2,1)S(1)}, u32[]{:S(2)}, u32[]{:S(2)}) collective-permute-start(bf16[504,512]{1,0:T(8,128)(2,1)} %get-tuple-element.20), channel_id=1, source_target_pairs={{0,96},{32,128},{64,160},{96,192},{128,224},{160,0},{192,32},{224,... | collective-permute-start | bytes 1548296 | tf_op jit(solution)/shard_map/ppermute | solution.py:243
  65.3 57.9 %collective-permute-start.14 = (bf16[504,512]{1,0:T(8,128)(2,1)}, bf16[504,512]{1,0:T(8,128)(2,1)S(1)}, u32[]{:S(2)}, u32[]{:S(2)}) collective-permute-start(bf16[504,512]{1,0:T(8,128)(2,1)} %get-tuple-element.19), channel_id=1, source_target_pairs={{0,160},{32,192},{64,224},{96,0},{128,32},{160,64},{192,96},{224,1... | collective-permute-start | bytes 1548296 | tf_op jit(solution)/shard_map/ppermute | solution.py:243
  65.6 65.9 %collective-permute-start.11 = (bf16[504,512]{1,0:T(8,128)(2,1)}, bf16[504,512]{1,0:T(8,128)(2,1)}, u32[]{:S(2)}, u32[]{:S(2)}) collective-permute-start(bf16[504,512]{1,0:T(8,128)(2,1)} %get-tuple-element.22), channel_id=1, source_target_pairs={{0,224},{32,0},{64,32},{96,64},{128,96},{160,128},{192,160},{224,1... | collective-permute-start | bytes 1548296 | tf_op jit(solution)/shard_map/ppermute | solution.py:243
  71.9 51.3 %copy-start.1 = (bf16[640,4096]{1,0:T(8,128)(2,1)}, bf16[640,4096]{1,0:T(8,128)(2,1)S(1)}, u32[]{:S(2)}) copy-start(bf16[640,4096]{1,0:T(8,128)(2,1)S(1)} %get-tuple-element.12.lhs_ref) | copy-start | bytes 15728644
  71.9 63.0 %collective-permute-start.15 = (bf16[504,512]{1,0:T(8,128)(2,1)}, bf16[504,512]{1,0:T(8,128)(2,1)S(1)}, u32[]{:S(2)}, u32[]{:S(2)}) collective-permute-start(bf16[504,512]{1,0:T(8,128)(2,1)} %get-tuple-element.18), channel_id=1, source_target_pairs={{0,64},{32,96},{64,128},{96,160},{128,192},{160,224},{192,0},{224,... | collective-permute-start | bytes 1548296 | tf_op jit(solution)/shard_map/ppermute | solution.py:243
  77.0 5.8 %copy-start.6 = (bf16[504,512]{1,0:T(8,128)(2,1)S(1)}, bf16[504,512]{1,0:T(8,128)(2,1)}, u32[]{:S(2)}) copy-start(bf16[504,512]{1,0:T(8,128)(2,1)} %get-tuple-element.17) | copy-start | bytes 1548292
  82.8 72.3 %collective-permute-start.16 = (bf16[504,512]{1,0:T(8,128)(2,1)S(1)}, bf16[504,512]{1,0:T(8,128)(2,1)S(1)}, u32[]{:S(2)}, u32[]{:S(2)}) collective-permute-start(bf16[504,512]{1,0:T(8,128)(2,1)S(1)} %copy-done.6), channel_id=1, source_target_pairs={{0,192},{32,224},{64,0},{96,32},{128,64},{160,96},{192,128},{224,1... | collective-permute-start | bytes 1548296 | tf_op jit(solution)/shard_map/ppermute | solution.py:243
  124.9 30.3 %slice-start = ((s8[5242880]{0:T(1024)(128)(4,1)}), s8[1048576]{0:T(1024)(128)(4,1)S(1)}, s32[]{:S(2)}) async-start(s8[5242880]{0:T(1024)(128)(4,1)} %bitcast.46), calls=%async_computation.5 | async-start | bytes 2097152
  127.8 27.4 %slice-start.1 = ((s8[5242880]{0:T(1024)(128)(4,1)}), s8[4194304]{0:T(1024)(128)(4,1)S(1)}, s32[]{:S(2)}) async-start(s8[5242880]{0:T(1024)(128)(4,1)} %bitcast.46), calls=%async_computation.6 | async-start | bytes 8388608
  155.2 46.4 %copy-start.5 = (bf16[8192,256]{1,0:T(8,128)(2,1)S(1)}, bf16[8192,256]{1,0:T(8,128)(2,1)}, u32[]{:S(2)}) copy-start(bf16[8192,256]{1,0:T(8,128)(2,1)} %param.21) | copy-start | bytes 12582916
  157.4 1.9 collective-permute-start.17
  203.0 2.0 collective-permute-start.18

commit v4 on v3

--- a/solution.py
+++ b/solution.py
@@ -190,11 +190,12 @@
     sides = jnp.concatenate(sides, axis=0)
     features = out_ref.shape[1]
     column = lax.broadcasted_iota(jnp.int32, (2 * rank, features), 0)
-    wanted = rank + info[8] + lax.broadcasted_iota(jnp.int32, (2 * rank, features), 1) // rank
-    chosen = (column == wanted).astype(f32).astype(bf16)
+    spot = lax.broadcasted_iota(jnp.int32, (2 * rank, features), 1)
+    chosen = (column == rank + info[8] + spot // rank).astype(f32).astype(bf16)
+    spread = (column == lax.rem(spot, rank)).astype(f32).astype(bf16)
     left = jnp.dot(sides, chosen, preferred_element_type=f32)
-    right = sides[:, :rank].astype(f32)
-    product = left * jnp.concatenate([right] * (features // rank), axis=1)
+    right = jnp.dot(sides, spread, preferred_element_type=f32)
+    product = left * right
     out_ref[...] = jnp.sum(product.reshape(-1, span, features), axis=1).astype(bf16)
 
 

time: 221 us -> 221 us (level)
  no operation moved by 1% of the time
where the time goes in v4:
time: 221 us; the launch traced here: 220 us
  waiting for transfers between devices  72.4 us (33%)
  starting transfers between devices  55.3 us (25%)
  blocking collectives  54.2 us (25%)
  matrix products  14.3 us (6%)
  local copies, waits for them, and re-layouts  11.9 us (5%)
  Pallas kernels  9.08 us (4%)
  other arithmetic  2.76 us (1%)
    ppermute x7, waiting for transfers between devices, head_moves(): lax.ppermute(cut, 'grp', [(i, (i + s) % groups) for i in range(groups)])  54.9 us
    all_to_all x4, blocking collectives, traded(): lax.all_to_all(value, axis, split_axis=0, concat_axis=0, tiled=True, axis...  54.2 us
    ppermute x12, starting transfers between devices, moved(): return lax.ppermute(value, 'tp', [(i, move(i)) for i in range(lanes)])  26.1 us
    ppermute x7, starting transfers between devices, head_moves(): lax.ppermute(cut, 'grp', [(i, (i + s) % groups) for i in range(groups)])  20.1 us
    dot_general x6, matrix products, per_device(): term = lax.dot_general(depth, came[s], by_last, preferred_element_type=f32)  12.8 us
    ppermute x12, waiting for transfers between devices, moved(): return lax.ppermute(value, 'tp', [(i, move(i)) for i in range(lanes)])  9.3 us
    all_to_all x1, starting transfers between devices, traded(): lax.all_to_all(value, axis, split_axis=0, concat_axis=0, tiled=True, axis...  9 us
    all_to_all x1, waiting for transfers between devices, traded(): lax.all_to_all(value, axis, split_axis=0, concat_axis=0, tiled=True, axis...  8.23 us
  transfers between devices with their start and end apart: 20, of which 10 were waited for; matrix products, arithmetic and copies ran while one was open for 10% of the time, Pallas kernels for 2%

profile of v4, /device:TPU:1, one launch (start us, length us, event | category | flops | bytes accessed | tf_op | source)
XLA Modules:
  0.0 220.2 jit_solution(537407167938322381)
XLA Ops:
  2.9 9.0 %all-to-all-start = ((bf16[8,80,128]{2,1,0:T(8,128)(2,1)}), bf16[8,80,128]{2,1,0:T(8,128)(2,1)S(1)}, u32[]{:S(2)}, u32[]{:S(2)}) async-start(bf16[8,80,128]{2,1,0:T(8,128)(2,1)} %broadcast_in_dim.26), calls=%async_computation | async-start | bytes 327680 | tf_op jit(solution)/shard_map/all_to_all | solution.py:26
  11.9 8.2 %all-to-all-done = bf16[8,80,128]{2,1,0:T(8,128)(2,1)S(1)} async-done(((bf16[8,80,128]{2,1,0:T(8,128)(2,1)}), bf16[8,80,128]{2,1,0:T(8,128)(2,1)S(1)}, u32[]{:S(2)}, u32[]{:S(2)}) %all-to-all-start) | async-done | bytes 163872 | tf_op jit(solution)/shard_map/all_to_all | solution.py:26
  21.5 2.4 %dynamic-slice_bitcast_fusion = (bf16[504,512]{1,0:T(8,128)(2,1)}, bf16[504,512]{1,0:T(8,128)(2,1)}) fusion(bf16[512,4008]{0,1:T(8,128)(2,1)} %param.13, s32[]{:T(128)S(6)} %select_n.224, s32[]{:T(128)S(6)} %select_n.220), kind=kLoop, calls=%fused_computation.19 | loop fusion | bytes 2064392 | tf_op jit(solution)/shard_map/dynamic_slice | solution.py:243
  24.4 2.5 %collective-permute-start.1 = (bf16[512,128]{1,0:T(8,128)(2,1)S(1)}, bf16[512,128]{1,0:T(8,128)(2,1)S(1)}, u32[]{:S(2)}, u32[]{:S(2)}) collective-permute-start(bf16[512,128]{1,0:T(8,128)(2,1)S(1)} %bitcast.55), channel_id=1, source_target_pairs={{0,4},{1,5},{2,6},{3,7},{4,0},{5,1},{6,2},{7,3},{8,12},{9,13},{10,... | collective-permute-start | bytes 393224 | tf_op jit(solution)/shard_map/ppermute | solution.py:256
  28.2 2.4 %collective-permute-done.1 = bf16[512,128]{1,0:T(8,128)(2,1)S(1)} collective-permute-done((bf16[512,128]{1,0:T(8,128)(2,1)S(1)}, bf16[512,128]{1,0:T(8,128)(2,1)S(1)}, u32[]{:S(2)}, u32[]{:S(2)}) %collective-permute-start.1) | collective-permute-done | bytes 131104 | tf_op jit(solution)/shard_map/ppermute | solution.py:256
  32.1 2.6 %collective-permute-start.4 = (bf16[4,512,128]{2,1,0:T(8,128)(2,1)S(1)}, bf16[4,512,128]{2,1,0:T(8,128)(2,1)S(1)}, u32[]{:S(2)}, u32[]{:S(2)}) collective-permute-start(bf16[4,512,128]{2,1,0:T(8,128)(2,1)S(1)} %bitcast_dynamic-update-slice_fusion.refs_5_), channel_id=1, source_target_pairs={{0,16},{1,17},{2,18},{3,19},{4,20},{5,21},{6,22},{7,23},{8,24},{9,... | collective-permute-start | bytes 1572872 | tf_op jit(solution)/shard_map/ppermute | solution.py:256
  36.3 3.6 %constant_dynamic-slice_fusion = (bf16[504,512]{1,0:T(8,128)(2,1)}, bf16[504,512]{1,0:T(8,128)(2,1)}, bf16[504,512]{1,0:T(8,128)(2,1)}, bf16[504,512]{1,0:T(8,128)(2,1)}, bf16[504,512]{1,0:T(8,128)(2,1)}) fusion(bf16[4008,512]{1,0:T(8,128)(2,1)} %bitcast.52, s32[]{:T(128)S(6)} %select_n.240, s32[]{:T(128)S(6)} %select_n.238, s32[]{:T(128)S(6)} %select_n.236, ...), kind=kLoop, calls=%fused_computation.35 | loop fusion | bytes 5160980 | tf_op jit(solution)/shard_map/dynamic_slice | solution.py:243
  39.9 5.0 %collective-permute-start.6 = (bf16[4,512,128]{2,1,0:T(8,128)(2,1)S(1)}, bf16[4,512,128]{2,1,0:T(8,128)(2,1)}, u32[]{:S(2)}, u32[]{:S(2)}) collective-permute-start(bf16[4,512,128]{2,1,0:T(8,128)(2,1)S(1)} %bitcast_dynamic-update-slice_fusion.refs_5_), channel_id=1, source_target_pairs={{0,1},{1,0},{2,3},{3,2},{4,5},{5,4},{6,7},{7,6},{8,9},{9,8},{10,11... | collective-permute-start | bytes 1572872 | tf_op jit(solution)/shard_map/ppermute | solution.py:256
  44.9 5.0 %collective-permute-start.7 = (bf16[4,512,128]{2,1,0:T(8,128)(2,1)S(1)}, bf16[4,512,128]{2,1,0:T(8,128)(2,1)}, u32[]{:S(2)}, u32[]{:S(2)}) collective-permute-start(bf16[4,512,128]{2,1,0:T(8,128)(2,1)S(1)} %collective-permute-done.3.refs_6_), channel_id=1, source_target_pairs={{0,1},{1,0},{2,3},{3,2},{4,5},{5,4},{6,7},{7,6},{8,9},{9,8},{10,11... | collective-permute-start | bytes 1572872 | tf_op jit(solution)/shard_map/ppermute | solution.py:256
  49.9 3.9 %collective-permute-done.4.refs_7_ = bf16[4,512,128]{2,1,0:T(8,128)(2,1)S(1)} collective-permute-done((bf16[4,512,128]{2,1,0:T(8,128)(2,1)S(1)}, bf16[4,512,128]{2,1,0:T(8,128)(2,1)S(1)}, u32[]{:S(2)}, u32[]{:S(2)}) %collective-permute-start.4) | collective-permute-done | bytes 524320 | tf_op jit(solution)/shard_map/ppermute | solution.py:256
  53.8 5.1 %collective-permute-start.8 = (bf16[4,512,128]{2,1,0:T(8,128)(2,1)S(1)}, bf16[4,512,128]{2,1,0:T(8,128)(2,1)}, u32[]{:S(2)}, u32[]{:S(2)}) collective-permute-start(bf16[4,512,128]{2,1,0:T(8,128)(2,1)S(1)} %collective-permute-done.4.refs_7_), channel_id=1, source_target_pairs={{0,1},{1,0},{2,3},{3,2},{4,5},{5,4},{6,7},{7,6},{8,9},{9,8},{10,11... | collective-permute-start | bytes 1572872 | tf_op jit(solution)/shard_map/ppermute | solution.py:256
  61.1 4.2 %collective-permute-start.13 = (bf16[504,512]{1,0:T(8,128)(2,1)}, bf16[504,512]{1,0:T(8,128)(2,1)S(1)}, u32[]{:S(2)}, u32[]{:S(2)}) collective-permute-start(bf16[504,512]{1,0:T(8,128)(2,1)} %get-tuple-element.20), channel_id=1, source_target_pairs={{0,96},{32,128},{64,160},{96,192},{128,224},{160,0},{192,32},{224,... | collective-permute-start | bytes 1548296 | tf_op jit(solution)/shard_map/ppermute | solution.py:244
  66.6 5.3 %shard_map.109 = (bf16[640,4096]{1,0:T(8,128)(2,1)S(1)}, f32[16,256]{1,0:T(8,128)S(1)}) custom-call(s32[9]{0:T(128)S(1)} %stack.39.refs_0_.info, s32[16,1]{1,0:T(8,128)S(1)} %convert_element_type.17.refs_1_, f32[1,4096]{1,0:T(1,128)S(1)} %bitcast.51, bf16[64,4096]{1,0:T(8,128)(2,1)S(1)} %bitcast.49, bf16[64,4096]{1,0:T(8,128)(2,1)S(1)} %bitcast.50, ...), custom_call_target="tpu_custom_call" | custom-call | tf_op jit(solution)/shard_map/pallas_call | solution.py:281
  71.9 3.5 %collective-permute-start.15 = (bf16[504,512]{1,0:T(8,128)(2,1)}, bf16[504,512]{1,0:T(8,128)(2,1)S(1)}, u32[]{:S(2)}, u32[]{:S(2)}) collective-permute-start(bf16[504,512]{1,0:T(8,128)(2,1)} %get-tuple-element.18), channel_id=1, source_target_pairs={{0,64},{32,96},{64,128},{96,160},{128,192},{160,224},{192,0},{224,... | collective-permute-start | bytes 1548296 | tf_op jit(solution)/shard_map/ppermute | solution.py:244
  75.4 1.6 fusion.11
  77.0 2.8 %convolution_add_fusion.1 = f32[640,504]{0,1:T(8,128)} fusion(f32[640,504]{0,1:T(8,128)S(1)} %fusion.11, bf16[640,4096]{1,0:T(8,128)(2,1)S(1)} %get-tuple-element.12.lhs_ref, s32[]{:T(128)S(6)} %select_n.215, bf16[4008,512]{1,0:T(8,128)(2,1)} %bitcast.53, s32[]{:T(128)S(6)} %select_n.216), kind=kOutput, calls=%fused_computation.4 | convolution fusion | flops 330624000 | bytes 3751944 | tf_op jit(solution)/shard_map/dot_general | solution.py:307
  79.8 3.1 %collective-permute-done.12 = bf16[504,512]{1,0:T(8,128)(2,1)S(1)} collective-permute-done((bf16[504,512]{1,0:T(8,128)(2,1)}, bf16[504,512]{1,0:T(8,128)(2,1)S(1)}, u32[]{:S(2)}, u32[]{:S(2)}) %collective-permute-start.12) | collective-permute-done | bytes 516128 | tf_op jit(solution)/shard_map/ppermute | solution.py:244
  82.8 9.2 %collective-permute-start.16 = (bf16[504,512]{1,0:T(8,128)(2,1)S(1)}, bf16[504,512]{1,0:T(8,128)(2,1)S(1)}, u32[]{:S(2)}, u32[]{:S(2)}) collective-permute-start(bf16[504,512]{1,0:T(8,128)(2,1)S(1)} %copy-done.6), channel_id=1, source_target_pairs={{0,192},{32,224},{64,0},{96,32},{128,64},{160,96},{192,128},{224,1... | collective-permute-start | bytes 1548296 | tf_op jit(solution)/shard_map/ppermute | solution.py:244
  92.0 1.6 fusion.8
  93.6 27.9 %collective-permute-done.13 = bf16[504,512]{1,0:T(8,128)(2,1)S(1)} collective-permute-done((bf16[504,512]{1,0:T(8,128)(2,1)}, bf16[504,512]{1,0:T(8,128)(2,1)S(1)}, u32[]{:S(2)}, u32[]{:S(2)}) %collective-permute-start.13) | collective-permute-done | bytes 516128 | tf_op jit(solution)/shard_map/ppermute | solution.py:244
  121.6 1.6 fusion.6
  123.2 1.7 fusion.4
  124.9 2.9 %copy.28 = f32[640,504]{1,0:T(8,128)} copy(f32[640,504]{0,1:T(8,128)} %convolution_add_fusion.1) | data formatting | bytes 2580480 | tf_op jit(solution)/shard_map/add | solution.py:308
  127.8 3.7 %collective-permute-done.11 = bf16[504,512]{1,0:T(8,128)(2,1)} collective-permute-done((bf16[504,512]{1,0:T(8,128)(2,1)}, bf16[504,512]{1,0:T(8,128)(2,1)}, u32[]{:S(2)}, u32[]{:S(2)}) %collective-permute-start.11) | collective-permute-done | bytes 516128 | tf_op jit(solution)/shard_map/ppermute | solution.py:244
  131.4 3.5 %fusion.2.sums_ref = f32[640,504]{1,0:T(8,128)S(1)} fusion(f32[640,504]{1,0:T(8,128)} %fusion.4, f32[640,504]{1,0:T(8,128)} %fusion.6, f32[640,504]{1,0:T(8,128)} %fusion.8, f32[640,504]{1,0:T(8,128)} %copy.28, bf16[504,512]{1,0:T(8,128)(2,1)} %collective-permute-done.11, bf16[640,4096]{1,0:T(8,128)(2,1)} %copy-done.1, s32[]{:T(128)S(6)} %select_n.222), kind=kOutput, calls=%fused_computation.3 | convolution fusion | flops 331591680 | bytes 7704580 | tf_op jit(solution)/shard_map/dot_general | solution.py:307
  134.9 20.3 %collective-permute-done.16.last_ref = bf16[504,512]{1,0:T(8,128)(2,1)S(1)} collective-permute-done((bf16[504,512]{1,0:T(8,128)(2,1)S(1)}, bf16[504,512]{1,0:T(8,128)(2,1)S(1)}, u32[]{:S(2)}, u32[]{:S(2)}) %collective-permute-start.16) | collective-permute-done | bytes 516128 | tf_op jit(solution)/shard_map/ppermute | solution.py:244
  155.2 2.3 %shard_map.110 = (f32[16,16,384]{2,1,0:T(8,128)S(1)}, f32[16,16,384]{2,1,0:T(8,128)S(1)}) custom-call(s32[9]{0:T(128)S(1)} %stack.39.refs_0_.info, f32[640,504]{1,0:T(8,128)S(1)} %fusion.2.sums_ref, bf16[640,4096]{1,0:T(8,128)(2,1)S(1)} %bitcast.47, bf16[504,512]{1,0:T(8,128)(2,1)S(1)} %collective-permute-done.15.first_ref, ...), custom_call_target="tpu_custom_call" | custom-call | tf_op jit(solution)/shard_map/pallas_call | solution.py:310
  159.6 15.1 %all_to_all.25.x_ref = f32[16,16,384]{2,1,0:T(8,128)S(1)} all-to-all(f32[16,16,384]{2,1,0:T(8,128)S(1)} %shard_map.111), channel_id=1, replica_groups={{0,2,4,6,8,10,12,14,16,18,20,22,24,26,28,30},{1,3,5,7,9,11,13,15,17,19,..., dimensions={0} | all-to-all | bytes 786432 | tf_op jit(solution)/shard_map/all_to_all | solution.py:26
  174.8 12.0 %all_to_all.26.refs_0_ = f32[8,16,384]{2,1,0:T(8,128)S(1)} all-to-all(f32[8,16,384]{2,1,0:T(8,128)S(1)} %shard_map.112), channel_id=1, replica_groups=mesh['grp'=8,'tp'=32] {'grp'}, dimensions={0} | all-to-all | bytes 393216 | tf_op jit(solution)/shard_map/all_to_all | solution.py:26
  187.2 13.5 %all_to_all.27 = bf16[32,16,128]{2,1,0:T(8,128)(2,1)S(1)} all-to-all(bf16[32,16,128]{2,1,0:T(8,128)(2,1)S(1)} %shard_map.113), channel_id=1, replica_groups=mesh['grp'=8,'tp'=32] {'tp'}, dimensions={0} | all-to-all | bytes 262144 | tf_op jit(solution)/shard_map/all_to_all | solution.py:26
  203.5 1.5 collective-permute-done.18
  205.5 13.6 %all_to_all.28 = bf16[16,2,8192]{2,1,0:T(2,128)(2,1)S(1)} all-to-all(bf16[16,2,8192]{2,1,0:T(2,128)(2,1)S(1)} %reshape.95), channel_id=1, replica_groups={{0,2,4,6,8,10,12,14,16,18,20,22,24,26,28,30},{1,3,5,7,9,11,13,15,17,19,..., dimensions={0} | all-to-all | bytes 1048576 | tf_op jit(solution)/shard_map/all_to_all | solution.py:26
  (83 shorter events, 19.5 us)
Async XLA Ops:
  0.0 36.1 %copy-start = (bf16[4008,64]{0,1:T(8,128)(2,1)S(1)}, bf16[4008,64]{0,1:T(8,128)(2,1)}, u32[]{:S(2)}) copy-start(bf16[4008,64]{0,1:T(8,128)(2,1)} %param.18) | copy-start | bytes 1539076
  2.9 17.2 %all-to-all-start = ((bf16[8,80,128]{2,1,0:T(8,128)(2,1)}), bf16[8,80,128]{2,1,0:T(8,128)(2,1)S(1)}, u32[]{:S(2)}, u32[]{:S(2)}) async-start(bf16[8,80,128]{2,1,0:T(8,128)(2,1)} %broadcast_in_dim.26), calls=%async_computation | async-start | bytes 327680 | tf_op jit(solution)/shard_map/all_to_all | solution.py:26
  20.1 15.7 %copy-start.7 = (bf16[64,448]{1,0:T(8,128)(2,1)S(1)}, bf16[64,448]{1,0:T(8,128)(2,1)}, u32[]{:S(2)}) copy-start(bf16[64,448]{1,0:T(8,128)(2,1)} %param.14) | copy-start | bytes 172036
  20.2 15.7 %copy-start.8 = (bf16[448,64]{0,1:T(8,128)(2,1)S(1)}, bf16[448,64]{0,1:T(8,128)(2,1)}, u32[]{:S(2)}) copy-start(bf16[448,64]{0,1:T(8,128)(2,1)} %param.19) | copy-start | bytes 172036
  20.2 8.0 %collective-permute-start = (bf16[512,128]{1,0:T(8,128)(2,1)S(1)}, bf16[512,128]{1,0:T(8,128)(2,1)S(1)}, u32[]{:S(2)}, u32[]{:S(2)}) collective-permute-start(bf16[512,128]{1,0:T(8,128)(2,1)S(1)} %bitcast.54), channel_id=1, source_target_pairs={{0,2},{1,3},{2,4},{3,5},{4,6},{5,7},{6,0},{7,1},{8,10},{9,11},{10,... | collective-permute-start | bytes 393224 | tf_op jit(solution)/shard_map/ppermute | solution.py:256
  23.9 48.0 %collective-permute-start.10 = (bf16[504,512]{1,0:T(8,128)(2,1)}, bf16[504,512]{1,0:T(8,128)(2,1)}, u32[]{:S(2)}, u32[]{:S(2)}) collective-permute-start(bf16[504,512]{1,0:T(8,128)(2,1)} %get-tuple-element.23), channel_id=1, source_target_pairs={{0,32},{32,64},{64,96},{96,128},{128,160},{160,192},{192,224},{224... | collective-permute-start | bytes 1548296 | tf_op jit(solution)/shard_map/ppermute | solution.py:244
  24.4 6.2 %collective-permute-start.1 = (bf16[512,128]{1,0:T(8,128)(2,1)S(1)}, bf16[512,128]{1,0:T(8,128)(2,1)S(1)}, u32[]{:S(2)}, u32[]{:S(2)}) collective-permute-start(bf16[512,128]{1,0:T(8,128)(2,1)S(1)} %bitcast.55), channel_id=1, source_target_pairs={{0,4},{1,5},{2,6},{3,7},{4,0},{5,1},{6,2},{7,3},{8,12},{9,13},{10,... | collective-permute-start | bytes 393224 | tf_op jit(solution)/shard_map/ppermute | solution.py:256
  26.9 3.8 %collective-permute-start.2 = (bf16[512,128]{1,0:T(8,128)(2,1)S(1)}, bf16[512,128]{1,0:T(8,128)(2,1)S(1)}, u32[]{:S(2)}, u32[]{:S(2)}) collective-permute-start(bf16[512,128]{1,0:T(8,128)(2,1)S(1)} %bitcast.56), channel_id=1, source_target_pairs={{0,6},{1,7},{2,0},{3,1},{4,2},{5,3},{6,4},{7,5},{8,14},{9,15},{10,... | collective-permute-start | bytes 393224 | tf_op jit(solution)/shard_map/ppermute | solution.py:256
  30.7 14.2 %collective-permute-start.3 = (bf16[4,512,128]{2,1,0:T(8,128)(2,1)S(1)}, bf16[4,512,128]{2,1,0:T(8,128)(2,1)S(1)}, u32[]{:S(2)}, u32[]{:S(2)}) collective-permute-start(bf16[4,512,128]{2,1,0:T(8,128)(2,1)S(1)} %bitcast_dynamic-update-slice_fusion.refs_5_), channel_id=1, source_target_pairs={{0,8},{1,9},{2,10},{3,11},{4,12},{5,13},{6,14},{7,15},{8,16},{9,17... | collective-permute-start | bytes 1572872 | tf_op jit(solution)/shard_map/ppermute | solution.py:256
  32.1 21.7 %collective-permute-start.4 = (bf16[4,512,128]{2,1,0:T(8,128)(2,1)S(1)}, bf16[4,512,128]{2,1,0:T(8,128)(2,1)S(1)}, u32[]{:S(2)}, u32[]{:S(2)}) collective-permute-start(bf16[4,512,128]{2,1,0:T(8,128)(2,1)S(1)} %bitcast_dynamic-update-slice_fusion.refs_5_), channel_id=1, source_target_pairs={{0,16},{1,17},{2,18},{3,19},{4,20},{5,21},{6,22},{7,23},{8,24},{9,... | collective-permute-start | bytes 1572872 | tf_op jit(solution)/shard_map/ppermute | solution.py:256
  34.7 24.1 %collective-permute-start.5 = (bf16[4,512,128]{2,1,0:T(8,128)(2,1)S(1)}, bf16[4,512,128]{2,1,0:T(8,128)(2,1)}, u32[]{:S(2)}, u32[]{:S(2)}) collective-permute-start(bf16[4,512,128]{2,1,0:T(8,128)(2,1)S(1)} %bitcast_dynamic-update-slice_fusion.refs_5_), channel_id=1, source_target_pairs={{0,24},{1,25},{2,26},{3,27},{4,28},{5,29},{6,30},{7,31},{8,0},{9,1... | collective-permute-start | bytes 1572872 | tf_op jit(solution)/shard_map/ppermute | solution.py:256
  36.2 30.4 %copy-start.2 = (bf16[4096,64]{0,1:T(8,128)(2,1)S(1)}, bf16[4096,64]{0,1:T(8,128)(2,1)}, u32[]{:S(2)}) copy-start(bf16[4096,64]{0,1:T(8,128)(2,1)} %param.20) | copy-start | bytes 1572868
  36.3 30.4 %copy-start.3 = (bf16[4096,64]{0,1:T(8,128)(2,1)S(1)}, bf16[4096,64]{0,1:T(8,128)(2,1)}, u32[]{:S(2)}) copy-start(bf16[4096,64]{0,1:T(8,128)(2,1)} %param.17) | copy-start | bytes 1572868
  36.3 30.3 %copy-start.4 = (f32[4096]{0:T(1024)S(1)}, f32[4096]{0:T(1024)}, u32[]{:S(2)}) copy-start(f32[4096]{0:T(1024)} %param.12) | copy-start | bytes 49156
  39.9 19.8 %collective-permute-start.6 = (bf16[4,512,128]{2,1,0:T(8,128)(2,1)S(1)}, bf16[4,512,128]{2,1,0:T(8,128)(2,1)}, u32[]{:S(2)}, u32[]{:S(2)}) collective-permute-start(bf16[4,512,128]{2,1,0:T(8,128)(2,1)S(1)} %bitcast_dynamic-update-slice_fusion.refs_5_), channel_id=1, source_target_pairs={{0,1},{1,0},{2,3},{3,2},{4,5},{5,4},{6,7},{7,6},{8,9},{9,8},{10,11... | collective-permute-start | bytes 1572872 | tf_op jit(solution)/shard_map/ppermute | solution.py:256
  44.9 16.2 %collective-permute-start.7 = (bf16[4,512,128]{2,1,0:T(8,128)(2,1)S(1)}, bf16[4,512,128]{2,1,0:T(8,128)(2,1)}, u32[]{:S(2)}, u32[]{:S(2)}) collective-permute-start(bf16[4,512,128]{2,1,0:T(8,128)(2,1)S(1)} %collective-permute-done.3.refs_6_), channel_id=1, source_target_pairs={{0,1},{1,0},{2,3},{3,2},{4,5},{5,4},{6,7},{7,6},{8,9},{9,8},{10,11... | collective-permute-start | bytes 1572872 | tf_op jit(solution)/shard_map/ppermute | solution.py:256
  53.8 11.5 %collective-permute-start.8 = (bf16[4,512,128]{2,1,0:T(8,128)(2,1)S(1)}, bf16[4,512,128]{2,1,0:T(8,128)(2,1)}, u32[]{:S(2)}, u32[]{:S(2)}) collective-permute-start(bf16[4,512,128]{2,1,0:T(8,128)(2,1)S(1)} %collective-permute-done.4.refs_7_), channel_id=1, source_target_pairs={{0,1},{1,0},{2,3},{3,2},{4,5},{5,4},{6,7},{7,6},{8,9},{9,8},{10,11... | collective-permute-start | bytes 1572872 | tf_op jit(solution)/shard_map/ppermute | solution.py:256
  58.9 6.7 %collective-permute-start.9 = (bf16[4,512,128]{2,1,0:T(8,128)(2,1)}, bf16[4,512,128]{2,1,0:T(8,128)(2,1)}, u32[]{:S(2)}, u32[]{:S(2)}) collective-permute-start(bf16[4,512,128]{2,1,0:T(8,128)(2,1)} %collective-permute-done.5.refs_8_), channel_id=1, source_target_pairs={{0,1},{1,0},{2,3},{3,2},{4,5},{5,4},{6,7},{7,6},{8,9},{9,8},{10,11... | collective-permute-start | bytes 1572872 | tf_op jit(solution)/shard_map/ppermute | solution.py:256
  59.7 23.2 %collective-permute-start.12 = (bf16[504,512]{1,0:T(8,128)(2,1)}, bf16[504,512]{1,0:T(8,128)(2,1)S(1)}, u32[]{:S(2)}, u32[]{:S(2)}) collective-permute-start(bf16[504,512]{1,0:T(8,128)(2,1)} %get-tuple-element.21), channel_id=1, source_target_pairs={{0,128},{32,160},{64,192},{96,224},{128,0},{160,32},{192,64},{224,... | collective-permute-start | bytes 1548296 | tf_op jit(solution)/shard_map/ppermute | solution.py:244
  61.1 60.5 %collective-permute-start.13 = (bf16[504,512]{1,0:T(8,128)(2,1)}, bf16[504,512]{1,0:T(8,128)(2,1)S(1)}, u32[]{:S(2)}, u32[]{:S(2)}) collective-permute-start(bf16[504,512]{1,0:T(8,128)(2,1)} %get-tuple-element.20), channel_id=1, source_target_pairs={{0,96},{32,128},{64,160},{96,192},{128,224},{160,0},{192,32},{224,... | collective-permute-start | bytes 1548296 | tf_op jit(solution)/shard_map/ppermute | solution.py:244
  65.3 57.9 %collective-permute-start.14 = (bf16[504,512]{1,0:T(8,128)(2,1)}, bf16[504,512]{1,0:T(8,128)(2,1)S(1)}, u32[]{:S(2)}, u32[]{:S(2)}) collective-permute-start(bf16[504,512]{1,0:T(8,128)(2,1)} %get-tuple-element.19), channel_id=1, source_target_pairs={{0,160},{32,192},{64,224},{96,0},{128,32},{160,64},{192,96},{224,1... | collective-permute-start | bytes 1548296 | tf_op jit(solution)/shard_map/ppermute | solution.py:244
  65.6 65.9 %collective-permute-start.11 = (bf16[504,512]{1,0:T(8,128)(2,1)}, bf16[504,512]{1,0:T(8,128)(2,1)}, u32[]{:S(2)}, u32[]{:S(2)}) collective-permute-start(bf16[504,512]{1,0:T(8,128)(2,1)} %get-tuple-element.22), channel_id=1, source_target_pairs={{0,224},{32,0},{64,32},{96,64},{128,96},{160,128},{192,160},{224,1... | collective-permute-start | bytes 1548296 | tf_op jit(solution)/shard_map/ppermute | solution.py:244
  71.9 51.3 %copy-start.1 = (bf16[640,4096]{1,0:T(8,128)(2,1)}, bf16[640,4096]{1,0:T(8,128)(2,1)S(1)}, u32[]{:S(2)}) copy-start(bf16[640,4096]{1,0:T(8,128)(2,1)S(1)} %get-tuple-element.12.lhs_ref) | copy-start | bytes 15728644
  71.9 63.0 %collective-permute-start.15 = (bf16[504,512]{1,0:T(8,128)(2,1)}, bf16[504,512]{1,0:T(8,128)(2,1)S(1)}, u32[]{:S(2)}, u32[]{:S(2)}) collective-permute-start(bf16[504,512]{1,0:T(8,128)(2,1)} %get-tuple-element.18), channel_id=1, source_target_pairs={{0,64},{32,96},{64,128},{96,160},{128,192},{160,224},{192,0},{224,... | collective-permute-start | bytes 1548296 | tf_op jit(solution)/shard_map/ppermute | solution.py:244
  77.0 5.8 %copy-start.6 = (bf16[504,512]{1,0:T(8,128)(2,1)S(1)}, bf16[504,512]{1,0:T(8,128)(2,1)}, u32[]{:S(2)}) copy-start(bf16[504,512]{1,0:T(8,128)(2,1)} %get-tuple-element.17) | copy-start | bytes 1548292
  82.8 72.3 %collective-permute-start.16 = (bf16[504,512]{1,0:T(8,128)(2,1)S(1)}, bf16[504,512]{1,0:T(8,128)(2,1)S(1)}, u32[]{:S(2)}, u32[]{:S(2)}) collective-permute-start(bf16[504,512]{1,0:T(8,128)(2,1)S(1)} %copy-done.6), channel_id=1, source_target_pairs={{0,192},{32,224},{64,0},{96,32},{128,64},{160,96},{192,128},{224,1... | collective-permute-start | bytes 1548296 | tf_op jit(solution)/shard_map/ppermute | solution.py:244
  124.9 30.3 %slice-start = ((s8[5242880]{0:T(1024)(128)(4,1)}), s8[1048576]{0:T(1024)(128)(4,1)S(1)}, s32[]{:S(2)}) async-start(s8[5242880]{0:T(1024)(128)(4,1)} %bitcast.46), calls=%async_computation.5 | async-start | bytes 2097152
  127.8 27.4 %slice-start.1 = ((s8[5242880]{0:T(1024)(128)(4,1)}), s8[4194304]{0:T(1024)(128)(4,1)S(1)}, s32[]{:S(2)}) async-start(s8[5242880]{0:T(1024)(128)(4,1)} %bitcast.46), calls=%async_computation.6 | async-start | bytes 8388608
  155.2 46.4 %copy-start.5 = (bf16[8192,256]{1,0:T(8,128)(2,1)S(1)}, bf16[8192,256]{1,0:T(8,128)(2,1)}, u32[]{:S(2)}) copy-start(bf16[8192,256]{1,0:T(8,128)(2,1)} %param.21) | copy-start | bytes 12582916
  157.4 1.9 collective-permute-start.17
  203.0 2.0 collective-permute-start.18
